TPU v7x, 32 devices: a whole 2x2x4 slice. The times are simulated.
32 devices in a mesh: head: 4 (over y, x), blk: 8 (over z, core).
Axes of the slice: x: 2, y: 2, z: 4, core: 2. Of those that a mesh axis runs over, the one named last changes fastest.
Arguments:
- hidden: bfloat16 [4, 1024, 2048], P('head', 'blk'), may hold values from -6 to 6
- segment_ids: int32 [4, 1024], replicated, may hold values from 0 to 3, as said below
- block_ids: int32 [4, 1024], replicated, may hold values from 0 to 2, as said below
- positions: int32 [4, 1024], replicated, may hold values from 0 to 767, as said below
- attn_gain: bfloat16 [2048], P(('head', 'blk')), may hold values from 0.099609375 to 1.8984375
- w_query: bfloat16 [2048, 2048], P(('head', 'blk')), may hold values from -0.125 to 0.125
- key_weight_matrix: bfloat16 [2048, 1024], P(('head', 'blk')), may hold values from -0.125 to 0.125
- value_weight_matrix: bfloat16 [2048, 1024], P(('head', 'blk')), may hold values from -0.125 to 0.125
- q_gain: bfloat16 [128], P(('head', 'blk')), may hold values from 0.099609375 to 1.8984375
- k_gain: bfloat16 [128], P(('head', 'blk')), may hold values from 0.099609375 to 1.8984375
- w_head_gate: bfloat16 [2048, 16], P(('head', 'blk')), may hold values from -0.125 to 0.125
- w_out: bfloat16 [2048, 2048], P(('head', 'blk')), may hold values from -2 to 2
- mlp_gain: bfloat16 [2048], P(('head', 'blk')), may hold values from 0.099609375 to 1.8984375
- w_gate: bfloat16 [6144, 2048], P(('head', 'blk')), may hold values from -0.125 to 0.125
- w_up: bfloat16 [6144, 2048], P(('head', 'blk')), may hold values from -0.125 to 0.125
- w_down: bfloat16 [6144, 2048], P(('head', 'blk')), may hold values from -0.078125 to 0.078125
- cotangent: bfloat16 [4, 1024, 2048], P('head', 'blk'), may hold values from -6 to 6
Outputs:
- layer_output: bfloat16 [4, 1024, 2048], P('head', 'blk')
- input_grad: float32 [4, 1024, 2048], P('head', 'blk')
- attn_gain_grad: float32 [2048], P(('head', 'blk'))
- w_query_grad: float32 [2048, 2048], P(('head', 'blk'))
- w_key_grad: float32 [2048, 1024], P(('head', 'blk'))
- w_value_grad: float32 [2048, 1024], P(('head', 'blk'))
- q_gain_grad: float32 [128], P(('head', 'blk'))
- k_gain_grad: float32 [128], P(('head', 'blk'))
- w_head_gate_grad: float32 [2048, 16], P(('head', 'blk'))
- w_out_grad: float32 [2048, 2048], P(('head', 'blk'))
- mlp_gain_grad: float32 [2048], P(('head', 'blk'))
- w_gate_grad: float32 [6144, 2048], P(('head', 'blk'))
- w_up_grad: float32 [6144, 2048], P(('head', 'blk'))
- w_down_grad: float32 [6144, 2048], P(('head', 'blk'))
Inputs may be any that keep to these rules, and one draw needn't show every extreme that they name: `segment_ids`: within a pack the ids never fall and each of the 4 documents is one nonempty run of positions. `positions`: A token's rotary position counts from 0 at its document's first position. block_ids equal positions // 256.
All inputs are finite; a program needn't handle non-finite values.
Results may differ from a plain program's by a relative error of at most 0.025.
Values may be sent and summed in bfloat16 or wider, within the bound.
A program may use at most 512 MiB of HBM per device.

v0:
```python
import math

import jax
import jax.numpy as jnp
from jax import lax
from jax.sharding import PartitionSpec as P

MODEL_WIDTH = 2048
HEADS = 16
KV_HEADS = 8
HEAD_DIM = 128
HQ = 2048
KEY_FEATURES = 1024


EPSILON = 1e-06
ROPE_BASE = 1000000.0
MASKED = -1e30


def rms_parts(values, gain_vec):
    factor = lax.rsqrt(jnp.mean(values * values, axis=-1, keepdims=True) + EPSILON)
    unit_part = values * factor
    return (unit_part * gain_vec, unit_part, factor)


def rms_back(grad_out, unit_part, factor, gain_vec):
    scaled_grad = grad_out * gain_vec
    back_vals = factor * (
        scaled_grad - unit_part * jnp.mean(scaled_grad * unit_part, axis=-1, keepdims=True)
    )
    return (back_vals, grad_out * unit_part)


def angle_tables(position_row):
    frequencies = jnp.exp(
        jnp.arange(HEAD_DIM // 2, dtype=jnp.float32) * (-2.0 * math.log(ROPE_BASE) / HEAD_DIM)
    )
    angles = position_row.astype(jnp.float32)[:, None] * frequencies[None, :]
    return (jnp.cos(angles)[:, None, :], jnp.sin(angles)[:, None, :])


def rotary(values, cosine, sine_table):
    half_dim = values.shape[-1] // 2
    first_half = values[..., :half_dim]
    second_half = values[..., half_dim:]
    return jnp.concatenate(
        [
            first_half * cosine - second_half * sine_table,
            second_half * cosine + first_half * sine_table,
        ],
        axis=-1,
    )


def rotary_back(grad_vals, cosine, sine_table):
    half_dim = grad_vals.shape[-1] // 2
    first_half = grad_vals[..., :half_dim]
    second_half = grad_vals[..., half_dim:]
    return jnp.concatenate(
        [
            first_half * cosine + second_half * sine_table,
            second_half * cosine - first_half * sine_table,
        ],
        axis=-1,
    )


def unit_forward(rows_in, gate_rows, up_rows, down_rows):
    gate_act = jnp.einsum("td,fd->tf", rows_in, gate_rows, preferred_element_type=jnp.float32)
    up_act = jnp.einsum("td,fd->tf", rows_in, up_rows, preferred_element_type=jnp.float32)
    silu_act = jax.nn.silu(gate_act)
    unit_values = (silu_act * up_act).astype(jnp.bfloat16)
    return (
        gate_act,
        up_act,
        silu_act,
        unit_values,
        jnp.dot(unit_values, down_rows, preferred_element_type=jnp.float32),
    )


def unit_backward(grad_rows, gate_act, up_act, silu_act, gate_rows, up_rows, down_rows):
    grad_units = jnp.einsum("td,fd->tf", grad_rows, down_rows, preferred_element_type=jnp.float32)
    sigmoid_gate = jax.nn.sigmoid(gate_act)
    grad_gate = (
        grad_units * up_act * sigmoid_gate * (1.0 + gate_act * (1.0 - sigmoid_gate))
    ).astype(jnp.bfloat16)
    grad_up = (grad_units * silu_act).astype(jnp.bfloat16)
    back_rows = jnp.dot(grad_gate, gate_rows, preferred_element_type=jnp.float32) + jnp.dot(
        grad_up, up_rows, preferred_element_type=jnp.float32
    )
    return (grad_gate, grad_up, back_rows)


def unit_terms(rows_in, grad_rows, grad_gate, grad_up, unit_values):
    return jnp.concatenate(
        [
            jnp.einsum("tf,td->fd", grad_gate, rows_in, preferred_element_type=jnp.float32),
            jnp.einsum("tf,td->fd", grad_up, rows_in, preferred_element_type=jnp.float32),
            jnp.einsum("tf,td->fd", unit_values, grad_rows, preferred_element_type=jnp.float32),
        ],
        axis=1,
    )


def unit_total(partial_sum):
    return lax.psum_scatter(
        partial_sum.astype(jnp.bfloat16), "head", scatter_dimension=0, tiled=True
    ).astype(jnp.float32)


def group_gather(rows_here):
    return lax.all_gather(rows_here[None], "head", axis=0, tiled=True)


def group_total(partial_rows):
    return lax.psum_scatter(
        partial_rows.astype(jnp.bfloat16), "head", scatter_dimension=0, tiled=True
    ).astype(jnp.float32)


def shards(
    hidden,
    segment_ids,
    block_ids,
    positions,
    attn_gain,
    w_query,
    key_weight_matrix,
    value_weight_matrix,
    q_gain,
    k_gain,
    w_head_gate,
    w_out,
    mlp_gain,
    w_gate,
    w_up,
    w_down,
    cotangent,
):
    tokens_here = hidden.shape[1]
    head_count = lax.axis_size("head")
    n_blk = lax.axis_size("blk")
    n_all = lax.axis_size(("head", "blk"))
    head_index = lax.axis_index("head")
    row_offset = lax.axis_index("blk") * tokens_here
    groups = HEADS // KV_HEADS
    inverse_square_root = 1.0 / math.sqrt(HEAD_DIM)
    q_cols = HQ // head_count
    key_value_columns = KEY_FEATURES // head_count
    gate_cols = HEADS // head_count
    heads_here = HEADS // head_count
    kv_here = KV_HEADS // head_count
    group_len = head_count * tokens_here
    (
        gain_attn,
        gain_mlp,
        gain_q,
        gain_k,
        full_query,
        full_key,
        full_value,
        full_head_gate,
        full_out,
    ) = (
        lax.all_gather(attn_gain, ("head", "blk"), axis=0, tiled=True),
        lax.all_gather(mlp_gain, ("head", "blk"), axis=0, tiled=True),
        lax.all_gather(q_gain, ("head", "blk"), axis=0, tiled=True),
        lax.all_gather(k_gain, ("head", "blk"), axis=0, tiled=True),
        lax.all_gather(w_query, ("head", "blk"), axis=0, tiled=True),
        lax.all_gather(key_weight_matrix, ("head", "blk"), axis=0, tiled=True),
        lax.all_gather(value_weight_matrix, ("head", "blk"), axis=0, tiled=True),
        lax.all_gather(w_head_gate, ("head", "blk"), axis=0, tiled=True),
        lax.all_gather(w_out, ("head", "blk"), axis=0, tiled=True),
    )
    gain_attn = gain_attn.astype(jnp.float32)
    gain_mlp = gain_mlp.astype(jnp.float32)
    gain_q = gain_q.astype(jnp.float32)
    gain_k = gain_k.astype(jnp.float32)
    query_cols = lax.dynamic_slice_in_dim(full_query, head_index * q_cols, q_cols, 1)
    key_cols = lax.dynamic_slice_in_dim(
        full_key, head_index * key_value_columns, key_value_columns, 1
    )
    value_cols = lax.dynamic_slice_in_dim(
        full_value, head_index * key_value_columns, key_value_columns, 1
    )
    head_gate_cols = lax.dynamic_slice_in_dim(full_head_gate, head_index * gate_cols, gate_cols, 1)
    out_rows = lax.dynamic_slice_in_dim(full_out, head_index * q_cols, q_cols, 0)
    values_x = hidden[0].astype(jnp.float32)
    normed_x, unit_x, factor_x = rms_parts(values_x, gain_attn)
    xn_low = normed_x.astype(jnp.bfloat16)
    xn_group = group_gather(xn_low).reshape(group_len, MODEL_WIDTH)
    q_lin = jnp.dot(xn_group, query_cols, preferred_element_type=jnp.float32)
    k_lin = jnp.dot(xn_group, key_cols, preferred_element_type=jnp.float32)
    v_low = jnp.dot(xn_group, value_cols, preferred_element_type=jnp.float32).astype(jnp.bfloat16)
    gate_lin = jnp.dot(xn_group, head_gate_cols, preferred_element_type=jnp.float32)
    group_positions = lax.dynamic_slice_in_dim(positions, row_offset, tokens_here, 1).reshape(
        group_len
    )
    cosine, sine_table = angle_tables(group_positions)
    q_normed, q_unit, q_factor = rms_parts(q_lin.reshape(group_len, heads_here, HEAD_DIM), gain_q)
    k_normed, k_unit, k_factor = rms_parts(k_lin.reshape(group_len, kv_here, HEAD_DIM), gain_k)
    q_low = rotary(q_normed, cosine, sine_table).astype(jnp.bfloat16)
    k_low = rotary(k_normed, cosine, sine_table).astype(jnp.bfloat16)
    q_group = q_low.reshape(head_count, tokens_here, kv_here, groups, HEAD_DIM)
    k_split = k_low.reshape(head_count, tokens_here, kv_here, HEAD_DIM)
    v_split = v_low.reshape(head_count, tokens_here, kv_here, HEAD_DIM)
    seg_query = lax.dynamic_slice_in_dim(segment_ids, row_offset, tokens_here, 1)
    blk_query = lax.dynamic_slice_in_dim(block_ids, row_offset, tokens_here, 1)

    def visible_from():
        allowed_pairs = (seg_query[:, :, None] == segment_ids[:, None, :]) & (
            block_ids[:, None, :] <= blk_query[:, :, None]
        )
        return allowed_pairs[:, None, None]

    def key_scores(key_piece):
        return (
            jnp.einsum("ptgrd,psgd->pgrts", q_group, key_piece, preferred_element_type=jnp.float32)
            * inverse_square_root
        )

    def over_keys(step_fn, initial):
        return step_fn(
            initial,
            (
                lax.all_gather(k_split, "blk", axis=1, tiled=True),
                lax.all_gather(v_split, "blk", axis=1, tiled=True),
            ),
            jnp.int32(0),
        )

    def forward_step(carried, key_values, first_key):
        key_piece, value_piece = key_values
        visible = visible_from()

        def forward_update(kept_state):
            run_top, run_total, run_acc = kept_state
            masked = jnp.where(visible, key_scores(key_piece), MASKED)
            new_top = jnp.maximum(run_top, jnp.max(masked, axis=-1))
            weights_now = jnp.where(visible, jnp.exp(masked - new_top[..., None]), 0.0)
            rescale = jnp.exp(run_top - new_top)
            run_total = jnp.sum(weights_now, axis=-1)
            added_part = jnp.einsum(
                "pgrts,psgd->ptgrd",
                weights_now.astype(jnp.bfloat16),
                value_piece,
                preferred_element_type=jnp.float32,
            )
            run_acc = run_acc * jnp.moveaxis(rescale, 3, 1)[..., None] + added_part
            return (new_top, run_total, run_acc)

        return lax.cond(jnp.any(visible), forward_update, lambda kept_state: kept_state, carried)

    top_init = jnp.full((head_count, kv_here, groups, tokens_here), MASKED, jnp.float32)
    acc_init = jnp.zeros((head_count, tokens_here, kv_here, groups, HEAD_DIM), jnp.float32)
    run_top, run_total, run_acc = over_keys(
        forward_step, (top_init, jnp.zeros_like(top_init), acc_init)
    )
    out_f32 = run_acc / jnp.moveaxis(run_total, 3, 1)[..., None]
    log_total = run_top + jnp.log(run_total)
    out_low_f = (
        out_f32.astype(jnp.bfloat16).astype(jnp.float32).reshape(group_len, heads_here, HEAD_DIM)
    )
    gate_sig = jax.nn.sigmoid(gate_lin)
    gated_low = (out_low_f * gate_sig[:, :, None]).reshape(group_len, q_cols).astype(jnp.bfloat16)
    attn_part = jnp.dot(gated_low, out_rows, preferred_element_type=jnp.float32)
    middle = values_x + group_total(attn_part.reshape(head_count, tokens_here, MODEL_WIDTH))[0]
    normed_mid, unit_mid, factor_mid = rms_parts(middle, gain_mlp)
    mid_low = normed_mid.astype(jnp.bfloat16)
    grad_low = cotangent[0]
    gate_rows, up_rows, down_rows = (
        lax.all_gather(w_gate, "blk", axis=0, tiled=True),
        lax.all_gather(w_up, "blk", axis=0, tiled=True),
        lax.all_gather(w_down, "blk", axis=0, tiled=True),
    )
    rows_in, grad_rows = (
        lax.all_gather(mid_low[None], "head", axis=0, tiled=True),
        lax.all_gather(cotangent, "head", axis=0, tiled=True),
    )
    rows_in = rows_in.reshape(head_count * tokens_here, MODEL_WIDTH)
    grad_rows = grad_rows.reshape(head_count * tokens_here, MODEL_WIDTH)
    gate_act, up_act, silu_act, unit_values, mlp_part = unit_forward(
        rows_in, gate_rows, up_rows, down_rows
    )
    mlp_out = unit_total(mlp_part.reshape(head_count, tokens_here, MODEL_WIDTH))[0]
    grad_gate, grad_up, back_part = unit_backward(
        grad_rows, gate_act, up_act, silu_act, gate_rows, up_rows, down_rows
    )
    grad_mid_norm = unit_total(back_part.reshape(head_count, tokens_here, MODEL_WIDTH))[0]
    mlp_terms = lax.psum_scatter(
        unit_terms(rows_in, grad_rows, grad_gate, grad_up, unit_values).astype(jnp.bfloat16),
        "blk",
        scatter_dimension=0,
        tiled=True,
    ).astype(jnp.float32)
    layer_output = (middle + mlp_out).astype(jnp.bfloat16)[None]
    back_mid, mlp_gain_term = rms_back(grad_mid_norm, unit_mid, factor_mid, gain_mlp)
    grad_middle = grad_low.astype(jnp.float32) + back_mid
    grad_attn_low = grad_middle.astype(jnp.bfloat16)
    dy_group = group_gather(grad_attn_low).reshape(group_len, MODEL_WIDTH)
    out_weight_term = jnp.einsum(
        "tk,td->kd", gated_low, dy_group, preferred_element_type=jnp.float32
    )
    grad_gated = jnp.einsum(
        "td,kd->tk", dy_group, out_rows, preferred_element_type=jnp.float32
    ).reshape(group_len, heads_here, HEAD_DIM)
    grad_out_low = (grad_gated * gate_sig[:, :, None]).astype(jnp.bfloat16)
    grad_gate_low = (jnp.sum(grad_gated * out_low_f, axis=-1) * gate_sig * (1.0 - gate_sig)).astype(
        jnp.bfloat16
    )
    grad_group = grad_out_low.reshape(head_count, tokens_here, kv_here, groups, HEAD_DIM)
    delta_rows = jnp.moveaxis(jnp.sum(grad_group.astype(jnp.float32) * out_f32, axis=-1), 1, 3)

    def backward_step(carried, key_values, first_key):
        key_piece, value_piece = key_values
        visible = visible_from()

        def backward_update(kept_grads):
            masked = jnp.where(visible, key_scores(key_piece), MASKED)
            attention_probabilities = jnp.where(
                visible, jnp.exp(masked - log_total[..., None]), 0.0
            )
            grad_probs = jnp.einsum(
                "ptgrd,psgd->pgrts", grad_group, value_piece, preferred_element_type=jnp.float32
            )
            grad_scores = (attention_probabilities * (grad_probs - delta_rows[..., None])).astype(
                jnp.bfloat16
            )
            grad_query = (
                jnp.einsum(
                    "pgrts,psgd->ptgrd", grad_scores, key_piece, preferred_element_type=jnp.float32
                )
                * inverse_square_root
            )
            key_part = (
                jnp.einsum(
                    "pgrts,ptgrd->psgd", grad_scores, q_group, preferred_element_type=jnp.float32
                )
                * inverse_square_root
            )
            value_part = jnp.einsum(
                "pgrts,ptgrd->psgd",
                attention_probabilities.astype(jnp.bfloat16),
                grad_group,
                preferred_element_type=jnp.float32,
            )
            return (grad_query, key_part, value_part)

        return lax.cond(jnp.any(visible), backward_update, lambda kept_state: kept_state, carried)

    pack_len = tokens_here * n_blk
    zeros_keys = jnp.zeros((head_count, pack_len, kv_here, HEAD_DIM), jnp.float32)
    grad_query, grad_keys, grad_values = over_keys(
        backward_step, (jnp.zeros_like(acc_init), zeros_keys, zeros_keys)
    )
    key_sums, value_sums = (
        lax.psum_scatter(
            grad_keys.astype(jnp.bfloat16), "blk", scatter_dimension=1, tiled=True
        ).astype(jnp.float32),
        lax.psum_scatter(
            grad_values.astype(jnp.bfloat16), "blk", scatter_dimension=1, tiled=True
        ).astype(jnp.float32),
    )
    q_back = (
        grad_query.reshape(group_len, heads_here, HEAD_DIM).astype(jnp.bfloat16).astype(jnp.float32)
    )
    k_back = key_sums.reshape(group_len, kv_here, HEAD_DIM).astype(jnp.bfloat16).astype(jnp.float32)
    grad_qn = rotary_back(q_back, cosine, sine_table)
    back_q, q_gain_part = rms_back(grad_qn, q_unit, q_factor, gain_q)
    grad_q_low = back_q.reshape(group_len, q_cols).astype(jnp.bfloat16)
    grad_kn = rotary_back(k_back, cosine, sine_table)
    back_k, k_gain_part = rms_back(grad_kn, k_unit, k_factor, gain_k)
    grad_k_low = back_k.reshape(group_len, key_value_columns).astype(jnp.bfloat16)
    grad_v_low = value_sums.reshape(group_len, key_value_columns).astype(jnp.bfloat16)
    xn_part = (
        jnp.einsum("tk,dk->td", grad_q_low, query_cols, preferred_element_type=jnp.float32)
        + jnp.einsum("tk,dk->td", grad_k_low, key_cols, preferred_element_type=jnp.float32)
        + jnp.einsum("tk,dk->td", grad_v_low, value_cols, preferred_element_type=jnp.float32)
        + jnp.einsum("tk,dk->td", grad_gate_low, head_gate_cols, preferred_element_type=jnp.float32)
    )
    grad_xn = group_total(xn_part.reshape(head_count, tokens_here, MODEL_WIDTH))[0]
    back_x, attn_gain_part = rms_back(grad_xn, unit_x, factor_x, gain_attn)
    input_grad = (grad_middle + back_x)[None]

    def reorder_rows(term):
        columns = term.shape[1]
        return jnp.swapaxes(
            term.reshape(head_count, n_blk, MODEL_WIDTH // n_all, columns), 0, 1
        ).reshape(MODEL_WIDTH, columns)

    query_term = reorder_rows(
        jnp.einsum("td,tk->dk", xn_group, grad_q_low, preferred_element_type=jnp.float32)
    )
    key_term = reorder_rows(
        jnp.einsum("td,tk->dk", xn_group, grad_k_low, preferred_element_type=jnp.float32)
    )
    value_term = reorder_rows(
        jnp.einsum("td,tk->dk", xn_group, grad_v_low, preferred_element_type=jnp.float32)
    )
    head_gate_term = reorder_rows(
        jnp.einsum("td,tk->dk", xn_group, grad_gate_low, preferred_element_type=jnp.float32)
    )
    query_sum, key_sum, value_sum, head_gate_sum, out_grad = (
        lax.psum_scatter(
            query_term.astype(jnp.bfloat16), "blk", scatter_dimension=0, tiled=True
        ).astype(jnp.float32),
        lax.psum_scatter(
            key_term.astype(jnp.bfloat16), "blk", scatter_dimension=0, tiled=True
        ).astype(jnp.float32),
        lax.psum_scatter(
            value_term.astype(jnp.bfloat16), "blk", scatter_dimension=0, tiled=True
        ).astype(jnp.float32),
        lax.psum_scatter(
            head_gate_term.astype(jnp.bfloat16), "blk", scatter_dimension=0, tiled=True
        ).astype(jnp.float32),
        lax.psum_scatter(
            out_weight_term.astype(jnp.bfloat16), "blk", scatter_dimension=0, tiled=True
        ).astype(jnp.float32),
    )
    query_grad, key_grad, value_grad, head_gate_grad = (
        lax.all_to_all(
            query_sum.astype(jnp.bfloat16), "head", split_axis=0, concat_axis=1, tiled=True
        ).astype(query_sum.dtype),
        lax.all_to_all(
            key_sum.astype(jnp.bfloat16), "head", split_axis=0, concat_axis=1, tiled=True
        ).astype(key_sum.dtype),
        lax.all_to_all(
            value_sum.astype(jnp.bfloat16), "head", split_axis=0, concat_axis=1, tiled=True
        ).astype(value_sum.dtype),
        lax.all_to_all(
            head_gate_sum.astype(jnp.bfloat16), "head", split_axis=0, concat_axis=1, tiled=True
        ).astype(head_gate_sum.dtype),
    )
    gain_grads = (
        lax.psum_scatter(
            jnp.sum(attn_gain_part, axis=0), ("head", "blk"), scatter_dimension=0, tiled=True
        ),
        lax.psum_scatter(
            jnp.sum(q_gain_part, axis=(0, 1)), ("head", "blk"), scatter_dimension=0, tiled=True
        ),
        lax.psum_scatter(
            jnp.sum(k_gain_part, axis=(0, 1)), ("head", "blk"), scatter_dimension=0, tiled=True
        ),
        lax.psum_scatter(
            jnp.sum(mlp_gain_term, axis=0), ("head", "blk"), scatter_dimension=0, tiled=True
        ),
    )
    return (
        layer_output,
        input_grad,
        gain_grads[0],
        query_grad,
        key_grad,
        value_grad,
        gain_grads[1],
        gain_grads[2],
        head_gate_grad,
        out_grad,
        gain_grads[3],
        mlp_terms[:, :MODEL_WIDTH],
        mlp_terms[:, MODEL_WIDTH : 2 * MODEL_WIDTH],
        mlp_terms[:, 2 * MODEL_WIDTH :],
    )


def solution(mesh):
    placed = (
        P("head", "blk", None),
        P(),
        P(),
        P(),
        P(("head", "blk")),
        P(("head", "blk"), None),
        P(("head", "blk"), None),
        P(("head", "blk"), None),
        P(("head", "blk")),
        P(("head", "blk")),
        P(("head", "blk"), None),
        P(("head", "blk"), None),
        P(("head", "blk")),
        P(("head", "blk"), None),
        P(("head", "blk"), None),
        P(("head", "blk"), None),
        P("head", "blk", None),
    )
    return jax.shard_map(
        shards,
        mesh=mesh,
        in_specs=placed,
        out_specs=(
            P("head", "blk", None),
            P("head", "blk", None),
            P(("head", "blk")),
            P(("head", "blk"), None),
            P(("head", "blk"), None),
            P(("head", "blk"), None),
            P(("head", "blk")),
            P(("head", "blk")),
            P(("head", "blk"), None),
            P(("head", "blk"), None),
            P(("head", "blk")),
            P(("head", "blk"), None),
            P(("head", "blk"), None),
            P(("head", "blk"), None),
        ),
        check_vma=False,
    )
```

profile of v0, /device:TPU:16, one launch (start us, length us, event | category | flops | bytes accessed | tf_op | source)
XLA Modules:
  0.0 1346.6 jit_solution(10967843454929329735)
XLA Ops:
  11.4 40.7 %all-reduce.13 = (bf16[2048]{0:T(1024)(128)(2,1)S(1)}, bf16[128]{0:T(256)(128)(2,1)S(1)}, bf16[128]{0:T(256)(128)(2,1)S(1)}, bf16[2048]{0:T(1024)(128)(2,1)S(1)}) all-reduce(bf16[2048]{0:T(1024)(128)(2,1)S(1)} %dynamic-update-slice, bf16[128]{0:T(256)(128)(2,1)S(1)} %dynamic-update-slice.1, ...), channel_id=1, replica_groups=mesh['head'=4,'blk'=8] {'head','blk'}, use_global_device_ids=true, to_apply=%add | all-reduce | flops 4352 | bytes 17408
  58.5 15.0 %all-gather.17.cloned.1.call-done = bf16[2048,1024]{1,0:T(8,128)(2,1)} async-done(((bf16[64,1024]{1,0:T(8,128)(2,1)}), bf16[2048,1024]{1,0:T(8,128)(2,1)}) %all-gather.17.cloned.1.call-update) | async-done | bytes 4194320 | tf_op jit(solution)/shard_map/all_gather | solution.py:172
  75.4 35.2 %all-gather.15.cloned.1.call-done = bf16[4,128,2048]{2,1,0:T(8,128)(2,1)} async-done(((bf16[1,128,2048]{2,1,0:T(8,128)(2,1)}), bf16[4,128,2048]{2,1,0:T(8,128)(2,1)}) %all-gather.15.cloned.1.call-update) | async-done | bytes 2097168 | tf_op jit(solution)/shard_map/all_gather | solution.py:114
  115.3 59.6 %all-gather.23.cloned.1.call-done = bf16[2048,1024]{1,0:T(8,128)(2,1)} async-done(((bf16[64,1024]{1,0:T(8,128)(2,1)}), bf16[2048,1024]{1,0:T(8,128)(2,1)}) %all-gather.23.cloned.1.call-update) | async-done | bytes 4194320 | tf_op jit(solution)/shard_map/all_gather | solution.py:173
  181.3 36.3 %all-gather = bf16[32,64,16]{1,2,0:T(8,128)(2,1)S(1)} all-gather(bf16[1,64,16]{1,2,0:T(8,128)(2,1)S(1)} %bitcast.345), channel_id=1, replica_groups=mesh['head'=4,'blk'=8] {'head','blk'}, dimensions={0}, use_global_device_ids=true | all-gather | bytes 67584 | tf_op jit(solution)/shard_map/all_gather | solution.py:174
  225.3 29.1 %all-gather.21.cloned.1.call-done = bf16[2048,2048]{1,0:T(8,128)(2,1)} async-done(((bf16[64,2048]{1,0:T(8,128)(2,1)}), bf16[2048,2048]{1,0:T(8,128)(2,1)}) %all-gather.21.cloned.1.call-update) | async-done | bytes 8388624 | tf_op jit(solution)/shard_map/all_gather | solution.py:171
  267.7 16.5 %all-gather.19.cloned.1.call-done = bf16[4,1024,2,128]{3,1,2,0:T(8,128)(2,1)} async-done(((bf16[4,128,2,128]{3,1,2,0:T(8,128)(2,1)}), bf16[4,1024,2,128]{3,1,2,0:T(8,128)(2,1)}) %all-gather.19.cloned.1.call-update) | async-done | bytes 2097168 | tf_op jit(solution)/shard_map/all_gather | solution.py:228
  284.2 30.7 %all-gather.25.cloned.1.call-done = bf16[4,1024,2,128]{3,1,2,0:T(8,128)(2,1)} async-done(((bf16[4,128,2,128]{3,1,2,0:T(8,128)(2,1)}), bf16[4,1024,2,128]{3,1,2,0:T(8,128)(2,1)}) %all-gather.25.cloned.1.call-update) | async-done | bytes 2097168 | tf_op jit(solution)/shard_map/all_gather | solution.py:229
  314.9 12.4 conditional.2
  329.2 65.6 %all-gather.27.cloned.1.call-done = bf16[2048,2048]{1,0:T(8,128)(2,1)} async-done(((bf16[64,2048]{1,0:T(8,128)(2,1)}), bf16[2048,2048]{1,0:T(8,128)(2,1)}) %all-gather.27.cloned.1.call-update) | async-done | bytes 8388624 | tf_op jit(solution)/shard_map/all_gather | solution.py:175
  401.4 33.7 %reduce-scatter.39.cloned.1.call-done = bf16[1,128,2048]{2,1,0:T(8,128)(2,1)} async-done(((bf16[4,128,2048]{2,1,0:T(8,128)(2,1)}), bf16[1,128,2048]{2,1,0:T(8,128)(2,1)}) %reduce-scatter.39.cloned.1.call-update) | async-done | bytes 524304
  440.5 59.7 %all-gather.31.cloned.1.call-done = bf16[1536,2048]{1,0:T(8,128)(2,1)} async-done(((bf16[192,2048]{1,0:T(8,128)(2,1)}), bf16[1536,2048]{1,0:T(8,128)(2,1)}) %all-gather.31.cloned.1.call-update) | async-done | bytes 6291472 | tf_op jit(solution)/shard_map/all_gather | solution.py:274
  500.2 37.7 %all-gather.29.cloned.1.call-done = bf16[4,128,2048]{2,1,0:T(8,128)(2,1)} async-done(((bf16[1,128,2048]{2,1,0:T(8,128)(2,1)}), bf16[4,128,2048]{2,1,0:T(8,128)(2,1)}) %all-gather.29.cloned.1.call-update) | async-done | bytes 2097168 | tf_op jit(solution)/shard_map/all_gather | solution.py:279
  538.0 8.5 fusion.118
  546.4 56.7 %all-gather.33.cloned.1.call-done = bf16[1536,2048]{1,0:T(8,128)(2,1)} async-done(((bf16[192,2048]{1,0:T(8,128)(2,1)}), bf16[1536,2048]{1,0:T(8,128)(2,1)}) %all-gather.33.cloned.1.call-update) | async-done | bytes 6291472 | tf_op jit(solution)/shard_map/all_gather | solution.py:275
  603.2 8.6 fusion.119
  611.7 28.6 %all-gather.37.cloned.1.call-done = bf16[4,128,2048]{2,1,0:T(8,128)(2,1)} async-done(((bf16[1,128,2048]{2,1,0:T(8,128)(2,1)}), bf16[4,128,2048]{2,1,0:T(8,128)(2,1)}) %all-gather.37.cloned.1.call-update) | async-done | bytes 2097168 | tf_op jit(solution)/shard_map/all_gather | solution.py:280
  640.3 65.2 %all-gather.35.cloned.1.call-done = bf16[1536,2048]{1,0:T(8,128)(2,1)} async-done(((bf16[192,2048]{1,0:T(8,128)(2,1)}), bf16[1536,2048]{1,0:T(8,128)(2,1)}) %all-gather.35.cloned.1.call-update) | async-done | bytes 6291472 | tf_op jit(solution)/shard_map/all_gather | solution.py:276
  705.5 10.8 multiply_convert_fusion
  716.4 7.2 fusion.120
  728.5 35.3 %reduce-scatter.43.cloned.1.call-done = bf16[1,128,2048]{2,1,0:T(8,128)(2,1)} async-done(((bf16[4,128,2048]{2,1,0:T(8,128)(2,1)}), bf16[1,128,2048]{2,1,0:T(8,128)(2,1)}) %reduce-scatter.43.cloned.1.call-update) | async-done | bytes 524304
  769.0 34.1 %all-gather.39.cloned.1.call-done = bf16[4,128,2048]{2,1,0:T(8,128)(2,1)} async-done(((bf16[1,128,2048]{2,1,0:T(8,128)(2,1)}), bf16[4,128,2048]{2,1,0:T(8,128)(2,1)}) %all-gather.39.cloned.1.call-update) | async-done | bytes 2097168 | tf_op jit(solution)/shard_map/all_gather | solution.py:114
  811.5 17.0 %conditional.3 = (bf16[4,1024,2,128]{3,1,2,0:T(8,128)(2,1)}, bf16[4,1024,2,128]{3,1,2,0:T(8,128)(2,1)}, f32[512,4,64]{0,2,1:T(8,128)}, f32[512,4,64]{0,2,1:T(8,128)}) conditional(s32[]{:T(128)} %convert_element_type.278, () %tuple.28, (pred[4,1,1,128,1024]{3,4,0,2,1:T(8,128)(4,1)}, bf16[4,1024,2,128]{3,1,2,0:T(8,128)(2,1)S(1)}, ...), branch_computations={%region_14.15_spmd.clone, %region_15.16_spmd.clone} | conditional | flops 2712406016 | bytes 71352432 | solution.py:351
  867.1 27.8 %reduce-scatter.25.cloned.1.call-done = bf16[4,128,2,128]{3,1,2,0:T(8,128)(2,1)} async-done(((bf16[4,1024,2,128]{3,1,2,0:T(8,128)(2,1)}), bf16[4,128,2,128]{3,1,2,0:T(8,128)(2,1)}) %reduce-scatter.25.cloned.1.call-update) | async-done | bytes 262160 | tf_op jit(solution)/shard_map/reduce_scatter | solution.py:362
  909.3 7.5 convolution_convert_fusion.4
  930.0 16.3 %pad_maximum_fusion = bf16[1536,6144]{1,0:T(8,128)(2,1)} fusion(bf16[1536,2048]{1,0:T(8,128)(2,1)S(1)} %convolution_convert_fusion, bf16[1536,2048]{1,0:T(8,128)(2,1)S(1)} %convolution_convert_fusion.1, bf16[1536,2048]{1,0:T(8,128)(2,1)S(1)} %convolution_convert_fusion.2), kind=kLoop, calls=%fused_computation.48 | loop fusion | flops 56623104 | bytes 37748736 | tf_op jit(solution)/shard_map/concatenate | solution.py:97
  967.0 32.3 %reduce-scatter.33.cloned.1.call-done = bf16[64,2048]{1,0:T(8,128)(2,1)} async-done(((bf16[512,2048]{1,0:T(8,128)(2,1)}), bf16[64,2048]{1,0:T(8,128)(2,1)}) %reduce-scatter.33.cloned.1.call-update) | async-done | bytes 262160 | tf_op jit(solution)/shard_map/reduce_scatter | solution.py:418
  1001.1 32.6 %reduce-scatter.29.cloned.1.call-done = bf16[256,256]{1,0:T(8,128)(2,1)} async-done(((bf16[2048,256]{1,0:T(8,128)(2,1)}), bf16[256,256]{1,0:T(8,128)(2,1)}) %reduce-scatter.29.cloned.1.call-update) | async-done | bytes 131088 | tf_op jit(solution)/shard_map/reduce_scatter | solution.py:409
  1038.0 28.8 %reduce-scatter.31.cloned.1.call-done = bf16[256,256]{1,0:T(8,128)(2,1)} async-done(((bf16[2048,256]{1,0:T(8,128)(2,1)}), bf16[256,256]{1,0:T(8,128)(2,1)}) %reduce-scatter.31.cloned.1.call-update) | async-done | bytes 131088 | tf_op jit(solution)/shard_map/reduce_scatter | solution.py:412
  1076.1 33.5 %reduce-scatter.45.cloned.1.call-done = bf16[1,128,2048]{2,1,0:T(8,128)(2,1)} async-done(((bf16[4,128,2048]{2,1,0:T(8,128)(2,1)}), bf16[1,128,2048]{2,1,0:T(8,128)(2,1)}) %reduce-scatter.45.cloned.1.call-update) | async-done | bytes 524304
  1111.1 39.8 %all-reduce.12 = (f32[2048]{0:T(1024)S(1)}, f32[128]{0:T(128)S(1)}, f32[128]{0:T(128)S(1)}, f32[2048]{0:T(1024)S(1)}) all-reduce(f32[2048]{0:T(1024)S(1)} %get-tuple-element.126, f32[128]{0:T(128)S(1)} %get-tuple-element.120, f32[128]{0:T(128)S(1)} %get-tuple-element.124, ...), channel_id=8, replica_groups=mesh['head'=4,'blk'=8] {'head','blk'}, use_global_device_ids=true, to_apply=%region_24.25.clone | all-reduce | flops 4352 | bytes 34816
  1156.5 179.4 %reduce-scatter.35.cloned.1.call-done = bf16[192,6144]{1,0:T(8,128)(2,1)} async-done(((bf16[1536,6144]{1,0:T(8,128)(2,1)}), bf16[192,6144]{1,0:T(8,128)(2,1)}) %reduce-scatter.35.cloned.1.call-update) | async-done | bytes 2359312 | tf_op jit(solution)/shard_map/reduce_scatter | solution.py:292
  (274 shorter events, 217.6 us)
Async XLA Ops:
  7.2 66.3 %all-gather.17.cloned.1.call-start = ((), (), s32[]{:S(2)}) async-start(), calls=%async_computation.17 | async-start | bytes 4325376 | tf_op jit(solution)/shard_map/all_gather | solution.py:172
  7.9 102.6 %all-gather.15.cloned.1.call-start = ((), (), s32[]{:S(2)}) async-start(), calls=%async_computation.16 | async-start | bytes 2621440 | tf_op jit(solution)/shard_map/all_gather | solution.py:114
  55.9 119.1 %all-gather.23.cloned.1.call-start = ((), (), s32[]{:S(2)}) async-start(), calls=%async_computation.20 | async-start | bytes 4325376 | tf_op jit(solution)/shard_map/all_gather | solution.py:173
  56.6 197.9 %all-gather.21.cloned.1.call-start = ((), (), s32[]{:S(2)}) async-start(), calls=%async_computation.19 | async-start | bytes 8650752 | tf_op jit(solution)/shard_map/all_gather | solution.py:171
  57.2 227.0 %all-gather.19.cloned.1.call-start = ((), (), s32[]{:S(2)}) async-start(), calls=%async_computation.18 | async-start | bytes 2359296 | tf_op jit(solution)/shard_map/all_gather | solution.py:228
  115.3 199.6 %all-gather.25.cloned.1.call-start = ((), (), s32[]{:S(2)}) async-start(), calls=%async_computation.21 | async-start | bytes 2359296 | tf_op jit(solution)/shard_map/all_gather | solution.py:229
  177.7 217.1 %all-gather.27.cloned.1.call-start = ((), (), s32[]{:S(2)}) async-start(), calls=%async_computation.22 | async-start | bytes 8650752 | tf_op jit(solution)/shard_map/all_gather | solution.py:175
  178.4 256.6 %reduce-scatter.39.cloned.1.call-start = ((), (), s32[]{:S(2)}) async-start(), calls=%async_computation.37 | async-start | bytes 2621440
  400.6 99.6 %all-gather.31.cloned.1.call-start = ((), (), s32[]{:S(2)}) async-start(), calls=%async_computation.24 | async-start | bytes 7077888 | tf_op jit(solution)/shard_map/all_gather | solution.py:274
  401.3 136.7 %all-gather.29.cloned.1.call-start = ((), (), s32[]{:S(2)}) async-start(), calls=%async_computation.23 | async-start | bytes 2621440 | tf_op jit(solution)/shard_map/all_gather | solution.py:279
  438.4 164.8 %all-gather.33.cloned.1.call-start = ((), (), s32[]{:S(2)}) async-start(), calls=%async_computation.25 | async-start | bytes 7077888 | tf_op jit(solution)/shard_map/all_gather | solution.py:275
  439.1 201.2 %all-gather.37.cloned.1.call-start = ((), (), s32[]{:S(2)}) async-start(), calls=%async_computation.27 | async-start | bytes 2621440 | tf_op jit(solution)/shard_map/all_gather | solution.py:280
  439.7 265.8 %all-gather.35.cloned.1.call-start = ((), (), s32[]{:S(2)}) async-start(), calls=%async_computation.26 | async-start | bytes 7077888 | tf_op jit(solution)/shard_map/all_gather | solution.py:276
  440.5 323.3 %reduce-scatter.43.cloned.1.call-start = ((), (), s32[]{:S(2)}) async-start(), calls=%async_computation.39 | async-start | bytes 2621440
  728.4 74.7 %all-gather.39.cloned.1.call-start = ((), (), s32[]{:S(2)}) async-start(), calls=%async_computation.28 | async-start | bytes 2621440 | tf_op jit(solution)/shard_map/all_gather | solution.py:114
  767.7 90.1 %reduce-scatter.23.cloned.1.call-start = ((), (), s32[]{:S(2)}) async-start(), calls=%async_computation.29 | async-start | bytes 2359296 | tf_op jit(solution)/shard_map/reduce_scatter | solution.py:359
  828.5 66.3 %reduce-scatter.25.cloned.1.call-start = ((), (), s32[]{:S(2)}) async-start(), calls=%async_computation.30 | async-start | bytes 2359296 | tf_op jit(solution)/shard_map/reduce_scatter | solution.py:362
  829.1 117.3 %reduce-scatter.37.cloned.1.call-start = ((), (), s32[]{:S(2)}) async-start(), calls=%async_computation.36 | async-start | bytes 589824
  838.3 124.6 %reduce-scatter.27.cloned.1.call-start = ((), (), s32[]{:S(2)}) async-start(), calls=%async_computation.31 | async-start | bytes 2359296 | tf_op jit(solution)/shard_map/reduce_scatter | solution.py:406
  842.3 157.0 %reduce-scatter.33.cloned.1.call-start = ((), (), s32[]{:S(2)}) async-start(), calls=%async_computation.34 | async-start | bytes 2359296 | tf_op jit(solution)/shard_map/reduce_scatter | solution.py:418
  850.9 182.8 %reduce-scatter.29.cloned.1.call-start = ((), (), s32[]{:S(2)}) async-start(), calls=%async_computation.32 | async-start | bytes 1179648 | tf_op jit(solution)/shard_map/reduce_scatter | solution.py:409
  867.0 199.7 %reduce-scatter.31.cloned.1.call-start = ((), (), s32[]{:S(2)}) async-start(), calls=%async_computation.33 | async-start | bytes 1179648 | tf_op jit(solution)/shard_map/reduce_scatter | solution.py:412
  899.7 210.0 %reduce-scatter.45.cloned.1.call-start = ((), (), s32[]{:S(2)}) async-start(), calls=%async_computation.40 | async-start | bytes 2621440
  909.0 244.3 %reduce-scatter.41.cloned.1.call-start = ((), (), s32[]{:S(2)}) async-start(), calls=%async_computation.38 | async-start | bytes 2621440
  916.8 419.1 %reduce-scatter.35.cloned.1.call-start = ((), (), s32[]{:S(2)}) async-start(), calls=%async_computation.35 | async-start | bytes 21233664 | tf_op jit(solution)/shard_map/reduce_scatter | solution.py:292
  948.0 7.8 all-to-all-start.3
  962.9 38.1 %all-to-all-start = ((bf16[4,64,512]{2,1,0:T(8,128)(2,1)}), bf16[4,64,512]{2,1,0:T(8,128)(2,1)S(1)}, u32[]{:S(2)}, u32[]{:S(2)}) async-start(bf16[4,64,512]{2,1,0:T(8,128)(2,1)} %bitcast.335), calls=%async_computation.3 | async-start | bytes 524288 | tf_op jit(solution)/shard_map/all_to_all | solution.py:423
  966.3 186.9 %copy-start.11 = (bf16[1,128,2048]{2,1,0:T(8,128)(2,1)S(1)}, bf16[1,128,2048]{2,1,0:T(8,128)(2,1)}, u32[]{:S(2)}) copy-start(bf16[1,128,2048]{2,1,0:T(8,128)(2,1)} %param.37) | copy-start | bytes 1572868
  966.4 186.9 %copy-start.13 = (bf16[1,128,2048]{2,1,0:T(8,128)(2,1)S(1)}, bf16[1,128,2048]{2,1,0:T(8,128)(2,1)}, u32[]{:S(2)}) copy-start(bf16[1,128,2048]{2,1,0:T(8,128)(2,1)} %reduce-scatter.43.cloned.1.call-done) | copy-start | bytes 1572868
  966.4 186.9 %copy-start.29 = (f32[128]{0:T(128)S(1)}, f32[128]{0:T(128)}, u32[]{:S(2)}) copy-start(f32[128]{0:T(128)} %copy-done.28) | copy-start | bytes 1540
  1033.7 33.0 %all-to-all-start.1 = ((bf16[4,64,256]{2,1,0:T(8,128)(2,1)}), bf16[4,64,256]{2,1,0:T(8,128)(2,1)S(1)}, u32[]{:S(2)}, u32[]{:S(2)}) async-start(bf16[4,64,256]{2,1,0:T(8,128)(2,1)} %bitcast.339), calls=%async_computation.5 | async-start | bytes 262144 | tf_op jit(solution)/shard_map/all_to_all | solution.py:426
  1066.7 8.7 all-to-all-start.2
  (36 other events, 1106.2 us)
Sparse Core Ops, SparseCore 0:
  11.0 62.3 all-gather.16
  75.9 34.6 all-gather.14
  113.6 61.2 all-gather.22
  177.8 76.6 all-gather.20
  256.5 27.6 all-gather.18
  286.3 28.5 all-gather.24
  317.9 76.8 all-gather.26
  400.7 34.2 reduce-scatter.38
  436.8 63.3 all-gather.30
  502.6 35.2 all-gather.28
  539.7 63.4 all-gather.32
  605.0 35.2 all-gather.36
  642.1 63.4 all-gather.34
  728.5 35.1 reduce-scatter.42
  767.8 35.2 all-gather.38
  828.6 29.0 reduce-scatter.22
  859.9 34.8 reduce-scatter.24
  897.0 29.6 reduce-scatter.36
  929.1 33.7 reduce-scatter.26
  965.2 34.0 reduce-scatter.32
  1002.3 31.4 reduce-scatter.28
  1036.1 30.5 reduce-scatter.30
  1070.0 39.6 reduce-scatter.44
  1112.5 35.4 reduce-scatter.40
  1150.4 185.4 reduce-scatter.34
where the time goes:
time: 1360 us; the launch traced here: 1350 us
  waiting for transfers between devices  966 us (71%)
  blocking collectives  117 us (9%)
  matrix products  115 us (8%)
  local copies, waits for them, and re-layouts  62.1 us (5%)
  other arithmetic  55.7 us (4%)
  between operations  15.8 us (1%)
  starting transfers between devices  14.5 us (1%)
    reduce_scatter x1, waiting for transfers between devices, shards(): lax.psum_scatter(unit_terms(rows_in, grad_rows, grad_gate, grad_up, unit_...  179 us
    unnamed x30, waiting for transfers between devices  108 us
    unnamed x2, blocking collectives  80.5 us
    all_gather x2, waiting for transfers between devices, group_gather(): return lax.all_gather(rows_here[None], 'head', axis=0, tiled=True)  69.3 us
    all_gather x1, waiting for transfers between devices, shards(): lax.all_gather(w_out, ('head', 'blk'), axis=0, tiled=True)  65.6 us
    all_gather x1, waiting for transfers between devices, shards(): lax.all_gather(w_down, 'blk', axis=0, tiled=True)  65.2 us
    all_gather x1, waiting for transfers between devices, shards(): lax.all_gather(w_gate, 'blk', axis=0, tiled=True)  59.7 us
    all_gather x1, waiting for transfers between devices, shards(): lax.all_gather(value_weight_matrix, ('head', 'blk'), axis=0, tiled=True)  59.6 us
  transfers between devices with their start and end apart: 29, of which 25 were waited for; matrix products, arithmetic and copies ran while one was open for 13% of the time, Pallas kernels for 0%

commit v1 on v0

v1 whole, which is shorter than its diff:
```python
import math

import jax
import jax.numpy as jnp
from jax import lax
from jax.experimental import pallas as pl
from jax.experimental.pallas import tpu as pltpu
from jax.sharding import PartitionSpec as P

MODEL_WIDTH = 2048
HEADS = 16
KV_HEADS = 8
HEAD_DIM = 128
GATE_PAD = 128
EPSILON = 1e-06
ROPE_BASE = 1000000.0
MASKED = -1e30
F32 = jnp.float32
BF16 = jnp.bfloat16
MESH = pl.DeviceIdType.MESH


def mm(a, b):
    return jnp.dot(a, b, preferred_element_type=F32)


def mm_nt(a, b):
    return lax.dot_general(a, b, (((1,), (1,)), ((), ())), preferred_element_type=F32)


def mm_tn(a, b):
    return lax.dot_general(a, b, (((0,), (0,)), ((), ())), preferred_element_type=F32)


def unit_of(values):
    factor = lax.rsqrt(jnp.mean(values * values, axis=-1, keepdims=True) + EPSILON)
    return values * factor, factor


def unit_back(scaled, unit, factor):
    return factor * (scaled - unit * jnp.mean(scaled * unit, axis=-1, keepdims=True))


def signal_to(semaphore, target):
    pl.semaphore_signal(semaphore, inc=1, device_id=target, device_id_type=MESH)


class Line:
    def __init__(self, n_blk):
        self.me = lax.axis_index("blk")
        self.chips = n_blk // 2
        self.i = self.me // 2
        self.c = self.me % 2
        self.right = {"blk": self.me + 2}
        self.left = {"blk": self.me - 2}
        self.sibling = {"blk": self.me + 1 - 2 * self.c}
        self.has_right = self.i < self.chips - 1
        self.has_left = self.i > 0

    def greet(self, barrier):
        signal_to(barrier, self.sibling)

        @pl.when(self.has_right)
        def _():
            signal_to(barrier, self.right)

        @pl.when(self.has_left)
        def _():
            signal_to(barrier, self.left)

        return 1 + self.has_right.astype(jnp.int32) + self.has_left.astype(jnp.int32)


class Gather:
    def __init__(self, line, src, out, sems):
        self.line, self.src, self.out, self.sems = line, src, out, sems
        self.pieces = sems.shape[2]
        self.rows = src.shape[0] // self.pieces

    def part(self, p):
        return pl.ds(p * self.rows, self.rows)

    def move(self, kind, src, j, p, target):
        return pltpu.make_async_remote_copy(
            src_ref=src.at[self.part(p)],
            dst_ref=self.out.at[j, self.line.c, self.part(p)],
            send_sem=self.sems.at[kind, j, p],
            recv_sem=self.sems.at[3 + kind, j, p],
            device_id=target,
            device_id_type=MESH,
        )

    def arrived(self, kind, j, p, core):
        there = self.out.at[j, core, self.part(p)]
        pltpu.make_async_remote_copy(
            src_ref=there,
            dst_ref=there,
            send_sem=self.sems.at[kind, j, p],
            recv_sem=self.sems.at[3 + kind, j, p],
            device_id=self.line.sibling,
            device_id_type=MESH,
        ).wait_recv()

    def send(self, src, j, p, right, left):
        line = self.line
        if right is not None:

            @pl.when(right)
            def _():
                self.move(0, src, j, p, line.right).start()

        if left is not None:

            @pl.when(left)
            def _():
                self.move(1, src, j, p, line.left).start()

        self.move(2, src, j, p, line.sibling).start()

    def own_copy(self):
        return pltpu.make_async_copy(
            self.src, self.out.at[self.line.i, self.line.c], self.sems.at[6, 0, 0]
        )

    def start(self):
        line = self.line
        for p in range(self.pieces):
            self.send(self.src, line.i, p, line.has_right, line.has_left)
        self.own_copy().start()

    def step(self, s):
        line = self.line
        from_left, from_right = line.i - s, line.i + s
        for p in range(self.pieces):

            @pl.when(from_left >= 0)
            def _(p=p):
                self.arrived(0, from_left, p, line.c)
                self.send(self.out.at[from_left, line.c], from_left, p, line.has_right, None)

            @pl.when(from_right < line.chips)
            def _(p=p):
                self.arrived(1, from_right, p, line.c)
                self.send(self.out.at[from_right, line.c], from_right, p, None, line.has_left)

    def finish(self):
        line = self.line
        for j in range(line.chips):
            mine = self.out.at[j, line.c]
            for p in range(self.pieces):
                self.arrived(2, j, p, 1 - line.c)
                self.move(2, mine, j, p, line.sibling).wait_send()

                @pl.when((line.i >= j) & line.has_right)
                def _(j=j, p=p, mine=mine):
                    self.move(0, mine, j, p, line.right).wait_send()

                @pl.when((line.i <= j) & line.has_left)
                def _(j=j, p=p, mine=mine):
                    self.move(1, mine, j, p, line.left).wait_send()

        self.own_copy().wait()

    def run(self):
        self.start()
        for s in range(1, self.line.chips):
            self.step(s)
        self.finish()


def by_rows(rows, step, body):
    def one(k, carry):
        body(pl.ds(pl.multiple_of(k * step, step), step))
        return carry

    lax.fori_loop(0, rows // step, one, 0)


class Scatter:
    def __init__(self, line, part, bufs, sems):
        self.line, self.part, self.sems = line, part, sems
        self.own, self.sib, self.inn, self.out = bufs

    def copy(self, kind, src, dst, j, target):
        return pltpu.make_async_remote_copy(
            src_ref=src,
            dst_ref=dst,
            send_sem=self.sems.at[kind, j],
            recv_sem=self.sems.at[3 + kind, j],
            device_id=target,
            device_id_type=MESH,
        )

    def to_sibling(self, j):
        line = self.line
        return self.copy(2, self.part.at[j, 1 - line.c], self.sib.at[j], j, line.sibling)

    def to_own(self, j):
        return pltpu.make_async_copy(
            self.part.at[j, self.line.c], self.own.at[j], self.sems.at[6, j]
        )

    def along(self, way, j):
        line = self.line
        target = line.left if way else line.right
        return self.copy(way, self.out.at[j], self.inn.at[way, j], j, target)

    def start(self):
        chips = self.line.chips
        order = []
        for k in range((chips + 1) // 2):
            order += [chips - 1 - k, k]
        for j in order[:chips]:
            self.to_sibling(j).start()
            self.to_own(j).start()

    def ready(self, j):
        self.to_sibling(j).wait_recv()
        self.to_own(j).wait()

    def pass_on(self, way, j, first):
        self.ready(j)
        rows = self.own.shape[1]

        @pl.when(first)
        def _():
            def body(r):
                total = self.own[j, r, :].astype(F32) + self.sib[j, r, :].astype(F32)
                self.out[j, r, :] = total.astype(BF16)

            by_rows(rows, 16, body)

        @pl.when(jnp.logical_not(first))
        def _():
            self.along(way, j).wait_recv()

            def body(r):
                total = self.own[j, r, :].astype(F32) + self.sib[j, r, :].astype(F32)
                self.out[j, r, :] = (total + self.inn[way, j, r, :].astype(F32)).astype(BF16)

            by_rows(rows, 16, body)

        self.along(way, j).start()

    def step(self, tau):
        line = self.line

        @pl.when((line.i <= tau) & line.has_right)
        def _():
            self.pass_on(0, line.chips - 1 - tau + line.i, line.i == 0)

        @pl.when((line.chips - 1 - line.i <= tau) & line.has_left)
        def _():
            self.pass_on(1, tau - (line.chips - 1 - line.i), line.i == line.chips - 1)

    def total(self, consume):
        line, i = self.line, self.line.i
        self.ready(i)

        @pl.when(line.has_left)
        def _():
            self.along(0, i).wait_recv()

        @pl.when(line.has_right)
        def _():
            self.along(1, i).wait_recv()

        rows = self.own.shape[1]

        def add(r, with_left, with_right):
            total = self.own[i, r, :].astype(F32) + self.sib[i, r, :].astype(F32)
            if with_left:
                total += self.inn[0, i, r, :].astype(F32)
            if with_right:
                total += self.inn[1, i, r, :].astype(F32)
            consume(r, total)

        @pl.when(line.has_left & line.has_right)
        def _():
            by_rows(rows, 16, lambda r: add(r, True, True))

        @pl.when(line.has_left & jnp.logical_not(line.has_right))
        def _():
            by_rows(rows, 16, lambda r: add(r, True, False))

        @pl.when(line.has_right & jnp.logical_not(line.has_left))
        def _():
            by_rows(rows, 16, lambda r: add(r, False, True))

    def finish(self):
        line = self.line
        for j in range(line.chips):
            self.to_sibling(j).wait_send()

            @pl.when(j > line.i)
            def _(j=j):
                self.along(0, j).wait_send()

            @pl.when(j < line.i)
            def _(j=j):
                self.along(1, j).wait_send()

    def run(self, consume):
        self.start()
        for tau in range(self.line.chips - 1):
            self.step(tau)
        self.total(consume)
        self.finish()


PIECES = 2


def gather_sems(chips):
    return pltpu.SemaphoreType.DMA((7, chips, PIECES))


def scatter_bufs(chips, rows, width):
    return [
        pltpu.VMEM((chips, rows, width), BF16),
        pltpu.VMEM((chips, rows, width), BF16),
        pltpu.VMEM((2, chips, rows, width), BF16),
        pltpu.VMEM((chips, rows, width), BF16),
        pltpu.SemaphoreType.DMA((7, chips)),
    ]


ANYWHERE = pl.BlockSpec(memory_space=pl.ANY)
IN_VMEM = pl.BlockSpec(memory_space=pltpu.VMEM)


def params(collective_id):
    return pltpu.CompilerParams(
        collective_id=collective_id, has_side_effects=True, vmem_limit_bytes=56 * 2**20
    )


def comm_cost(byte_count):
    return pl.CostEstimate(flops=0, transcendentals=0, bytes_accessed=40 * byte_count)


class Exchange:
    def __init__(self, axis, size):
        self.axis, self.size = axis, size
        self.me = lax.axis_index(axis)

    def peer(self, k):
        return lax.rem(self.me + k, self.size)

    def greet(self, barrier):
        for k in range(1, self.size):
            signal_to(barrier, {self.axis: self.peer(k)})

    def copy(self, k, src, dst, sems):
        return pltpu.make_async_remote_copy(
            src_ref=src,
            dst_ref=dst,
            send_sem=sems.at[0, k],
            recv_sem=sems.at[1, k],
            device_id={self.axis: self.peer(k)},
            device_id_type=MESH,
        )

    def sems(self):
        return pltpu.SemaphoreType.DMA((2, self.size))


def pair_sems(size):
    return pltpu.SemaphoreType.DMA((2, size))


def greet_all(exchanges, line=None, moves=None):
    barrier = pltpu.get_barrier_semaphore()
    count = 0
    for exchange in exchanges:
        exchange.greet(barrier)
        count += exchange.size - 1
    if line is not None:
        count += line.greet(barrier)
    if moves is not None:
        whether, source = moves

        @pl.when(whether)
        def _():
            signal_to(barrier, source)

        count += whether.astype(jnp.int32)
    pl.semaphore_wait(barrier, count)


def flip_copy(src, dst, bit, sems, *index):
    return pltpu.make_async_remote_copy(
        src_ref=src,
        dst_ref=dst,
        send_sem=sems.at[(0, *index)],
        recv_sem=sems.at[(1, *index)],
        device_id={"head": lax.axis_index("head") ^ (1 << bit)},
        device_id_type=MESH,
    )


def ff_entries(rows, n_head):
    bits = tuple(range(n_head.bit_length() - 1))
    back, half = bits[::-1], rows // 2
    return (
        (0, pl.ds(0, rows), bits),
        (1, pl.ds(0, rows), back),
        (2, pl.ds(0, half), bits),
        (2, pl.ds(half, half), back),
    )


def place_of_out_rows(n_head, n_blk):
    h, b = lax.axis_index("head"), lax.axis_index("blk")
    d = h * n_blk + b
    source = b * n_head + h
    return (d % n_head, d // n_head), (source // n_blk, source % n_blk)


PACK_ROWS = 24


def weight_pieces(b, q_cols, copies):
    kv = b // copies * HEAD_DIM
    return (
        (0, pl.ds(pl.multiple_of(b * q_cols, HEAD_DIM), q_cols), pl.ds(0, q_cols)),
        (1, pl.ds(pl.multiple_of(kv, HEAD_DIM), HEAD_DIM), pl.ds(q_cols, HEAD_DIM)),
        (2, pl.ds(pl.multiple_of(kv, HEAD_DIM), HEAD_DIM), pl.ds(q_cols + HEAD_DIM, HEAD_DIM)),
    )


def first_gather(rows, weights, pack, w_out, ids, q_cols, copies, n_head, n_blk, collective_id):
    count, width = rows.shape
    chips, length = n_blk // 2, n_blk * count
    rows_here = weights[0].shape[0]
    columns = q_cols + 2 * HEAD_DIM
    together = 128 // rows_here
    chunk = 256

    def kernel(src, *refs):
        w_src, (pack_src, out_src), (pos, seg, blk) = refs[:3], refs[3:5], refs[5:8]
        out, w_all, moved_out, vec, gates, cos_ref, sin_ref, low_ref, code_ref, key_ref = refs[8:18]
        g_all, sems, block_sems, w_sems, pack_sems, g_sems, moved, local = refs[18:]
        line = Line(n_blk)
        across, along = Exchange("head", n_head), Exchange("blk", n_blk)
        h, b = across.me, along.me
        (th, tb), (sh, sb) = place_of_out_rows(n_head, n_blk)
        stays = (th == h) & (tb == b)
        moves = jnp.logical_not(stays)
        greet_all((across, along), moves=(moves, {"head": sh, "blk": sb}))

        def block_copies(k):
            for w, there, here in weight_pieces(along.peer(k), q_cols, copies):
                yield along.copy(
                    k, w_src[w].at[:, there], w_all.at[h, b, :, here], block_sems.at[w]
                )

        def pack_copy(k):
            return along.copy(k, pack_src, g_all.at[h, b], pack_sems)

        def w_copy(k):
            return across.copy(k, w_all.at[h], w_all.at[h], w_sems)

        def g_copy(k):
            return across.copy(k, g_all.at[h], g_all.at[h], g_sems)

        move_out = pltpu.make_async_remote_copy(
            src_ref=out_src,
            dst_ref=moved_out,
            send_sem=moved.at[0],
            recv_sem=moved.at[1],
            device_id={"head": th, "blk": tb},
            device_id_type=MESH,
        )
        keep_out = pltpu.make_async_copy(out_src, moved_out, moved.at[2])
        locals_ = [
            pltpu.make_async_copy(w_src[w].at[:, there], w_all.at[h, b, :, here], local.at[w])
            for w, there, here in weight_pieces(b, q_cols, copies)
        ] + [pltpu.make_async_copy(pack_src, g_all.at[h, b], local.at[3])]
        for k in range(1, n_blk):
            for copy in block_copies(k):
                copy.start()
        gather = Gather(line, src, out, sems)
        gather.start()
        for k in range(1, n_blk):
            pack_copy(k).start()
        for one in locals_:
            one.start()

        @pl.when(stays)
        def _():
            keep_out.start()

        @pl.when(moves)
        def _():
            move_out.start()

        half = HEAD_DIM // 2
        index = lax.broadcasted_iota(jnp.int32, (half, chunk), 0).astype(F32)
        frequency = jnp.exp(index * (-2.0 * math.log(ROPE_BASE) / HEAD_DIM))
        key_ref[...] = (seg[...] * length + blk[...]).astype(F32)

        def tables(n, carry):
            r = block_of(n, chunk)
            angles = frequency * pos[:, r].astype(F32)
            cosine, sine = jnp.cos(angles), jnp.sin(angles)
            cos_ref[r, :] = jnp.concatenate([cosine, cosine], axis=0).T
            sin_ref[r, :] = jnp.concatenate([-sine, sine], axis=0).T
            low_ref[r, :] = jnp.broadcast_to((seg[:, r] * length).astype(F32), (128, chunk)).T
            code_ref[r, :] = jnp.broadcast_to(key_ref[:, r], (128, chunk)).T
            return carry

        lax.fori_loop(0, length // chunk, tables, 0)
        for one in locals_:
            one.wait()
        for k in range(1, n_blk):
            pack_copy(k).wait_recv()
        for k in range(1, n_head):
            g_copy(k).start()
        gather.step(1)
        for k in range(1, n_blk):
            for copy in block_copies(k):
                copy.wait_recv()
        for k in range(1, n_head):
            w_copy(k).start()
        for s in range(2, chips):
            gather.step(s)
        for k in range(1, n_head):
            g_copy(k).wait()
        everyone = [g_all.at[d // n_blk, d % n_blk] for d in range(n_head * n_blk)]
        vec[...] = jnp.zeros_like(vec)
        for t in range(width // 128):
            tile = sum(one[...] for one in everyone[t * together : (t + 1) * together])
            vec[0:2, t * 128 : (t + 1) * 128] = tile[0:2]
            gates[:, t * 128 : (t + 1) * 128] = tile[8:].astype(BF16)
        vec[2:4, 0:128] = sum(one[2:4, :] for one in everyone)
        gather.finish()
        for k in range(1, n_head):
            w_copy(k).wait()
        for k in range(1, n_blk):
            pack_copy(k).wait_send()
            for copy in block_copies(k):
                copy.wait_send()

        @pl.when(stays)
        def _():
            keep_out.wait()

        @pl.when(moves)
        def _():
            move_out.wait()

    dma = pltpu.SemaphoreType.DMA
    out, w_attn, *rest = pl.pallas_call(
        kernel,
        out_shape=(
            jax.ShapeDtypeStruct((chips, 2, count, width), rows.dtype),
            jax.ShapeDtypeStruct((n_head, n_blk, rows_here, columns), BF16),
            jax.ShapeDtypeStruct(w_out.shape, w_out.dtype),
            jax.ShapeDtypeStruct((8, width), F32),
            jax.ShapeDtypeStruct((HEADS, width), BF16),
            *[jax.ShapeDtypeStruct((length, 128), F32)] * 4,
            jax.ShapeDtypeStruct((1, length), F32),
        ),
        in_specs=[IN_VMEM] + [ANYWHERE] * 5 + [IN_VMEM] * 3,
        out_specs=[ANYWHERE] * 3 + [IN_VMEM] * 7,
        scratch_shapes=[
            pltpu.VMEM((n_head, n_blk, PACK_ROWS, 128), F32),
            gather_sems(chips),
            dma((3, 2, n_blk)),
            pair_sems(n_head),
            pair_sems(n_blk),
            pair_sems(n_head),
            dma((3,)),
            dma((4,)),
        ],
        compiler_params=params(collective_id),
        cost_estimate=comm_cost(n_blk * count * width),
        name="first_gather",
    )(rows, *weights, pack, w_out, *ids)
    return (
        out.reshape(length, width),
        w_attn.reshape(n_head * n_blk * rows_here, columns),
        *rest,
    )


class Spread:
    def __init__(self, full, entries, n_head, sems):
        self.full, self.entries, self.n_head, self.sems = full, entries, n_head, sems

    def copies(self, e, level):
        weight, part, order = self.entries[e]
        full = self.full[weight]
        bit = order[level]
        keys = [0]
        for low in order[:level]:
            keys += [key ^ (1 << low) for key in keys]
        for key in keys:
            there = key ^ (1 << bit)
            yield flip_copy(
                full.at[key, part], full.at[there, part], bit, self.sems, e, there
            )

    def level(self, level):
        for e in range(len(self.entries)):
            if level > 1:
                for copy in self.copies(e, level - 1):
                    copy.wait_recv()
            for copy in self.copies(e, level):
                copy.start()

    def start(self):
        self.level(1)

    def finish(self):
        levels = self.n_head.bit_length() - 1
        for level in range(2, levels):
            self.level(level)
        for e in range(len(self.entries)):
            for level in range(1, levels):
                for copy in self.copies(e, level):
                    copy.wait_send()
                    if level == levels - 1:
                        copy.wait_recv()

    @staticmethod
    def sem_shape(n_head):
        return pltpu.SemaphoreType.DMA((2, 4, n_head))


class Collect:
    def __init__(self, have, kept, inbox, total, entries, n_head, sems):
        self.have, self.kept, self.inbox, self.total = have, kept, inbox, total
        self.entries, self.n_head, self.sems = entries, n_head, sems

    def keys(self, order, level):
        keys = [0]
        for low in order[: len(order) - 1 - level]:
            keys += [key ^ (1 << low) for key in keys]
        return keys

    def slot(self, order, key):
        return self.keys(order, 0).index(key)

    def copies(self, e, level):
        weight, part, order = self.entries[e]
        bit = order[len(order) - 1 - level]
        for key in self.keys(order, level):
            slot = self.slot(order, key)
            if level == 0:
                src = self.have[weight].at[key ^ (1 << bit), part]
            else:
                src = self.kept[weight].at[self.slot(order, key ^ (1 << bit)), part]
            yield flip_copy(src, self.inbox[weight].at[level, slot, part], bit, self.sems, e, level, slot)

    def locals_(self):
        for e, (weight, part, order) in enumerate(self.entries):
            for key in self.keys(order, 0):
                slot = self.slot(order, key)
                yield pltpu.make_async_copy(
                    self.have[weight].at[key, part],
                    self.kept[weight].at[slot, part],
                    self.sems.at[2, e, 0, slot],
                )

    def start(self):
        for copy in self.locals_():
            copy.start()
        for e in range(len(self.entries)):
            for copy in self.copies(e, 0):
                copy.start()

    def finish(self):
        for copy in self.locals_():
            copy.wait()
        levels = self.n_head.bit_length() - 2
        for level in range(levels):
            last = level == levels - 1
            for e, (weight, part, order) in enumerate(self.entries):
                for copy in self.copies(e, level):
                    copy.wait_recv()
                for at, key in enumerate(self.keys(order, level)):
                    slot = self.slot(order, key)
                    kept, inbox = self.kept[weight], self.inbox[weight]
                    into = self.total[weight] if last else kept
                    where = at if last else slot

                    def body(r, part=part, slot=slot, kept=kept, inbox=inbox, into=into, where=where):
                        r = pl.ds(pl.multiple_of(r.start + part.start, 16), r.size)
                        value = kept[slot, r, :].astype(F32) + inbox[level, slot, r, :].astype(F32)
                        into[where, r, :] = value.astype(BF16)

                    by_rows(part.size, 16, body)
            for e in range(len(self.entries)):
                if not last:
                    for copy in self.copies(e, level + 1):
                        copy.start()
        for level in range(levels):
            for e in range(len(self.entries)):
                for copy in self.copies(e, level):
                    copy.wait_send()

    @staticmethod
    def sem_shape(n_head):
        levels = n_head.bit_length() - 2
        return pltpu.SemaphoreType.DMA((3, 4, levels, n_head // 2))


def last_scatter(
    partial_rows, w_grad, out_grad, pack, sums, hidden, gain, q_cols, copies, n_head, n_blk, collective_id
):
    total_rows, width = partial_rows.shape
    chips, count = n_blk // 2, total_rows // n_blk
    _, _, rows_here, columns = w_grad.shape
    n_sums = len(sums)
    entries = ff_entries(sums[0].shape[1], n_head) if sums else ()

    def kernel(part, w_src, o_src, g_src, *refs):
        ff_src, (x_ref, gain_ref), refs = refs[:n_sums], refs[n_sums : n_sums + 2], refs[n_sums + 2 :]
        out, wq_out, wk_out, wv_out, o_out, g_out = refs[:6]
        ff_out, refs = refs[6 : 6 + n_sums], refs[6 + n_sums :]
        bufs, sems = refs[:4], refs[4]
        w_in, w_sum, o_in, o_sum, g_in, g_sum, g_last = refs[5:12]
        w_sems, block_sems, o_sems, g_sems, pack_sems, moved, ff_sems, local = refs[12:]
        line = Line(n_blk)
        across, along = Exchange("head", n_head), Exchange("blk", n_blk)
        h, b = across.me, along.me
        (sh, sb), (th, tb) = place_of_out_rows(n_head, n_blk)
        stays = (th == h) & (tb == b)
        moves = jnp.logical_not(stays)
        greet_all((across, along), moves=(moves, {"head": sh, "blk": sb}))

        def w_copy(k):
            return across.copy(k, w_src.at[across.peer(k)], w_in.at[k], w_sems)

        def o_copy(k):
            return across.copy(k, o_src.at[across.peer(k)], o_in.at[k], o_sems)

        lanes = n_blk * rows_here

        def g_part(head):
            return g_src.at[:, pl.ds(pl.multiple_of(head * lanes, 128), lanes)]

        def g_copy(k):
            return across.copy(k, g_part(across.peer(k)), g_in.at[k], g_sems)

        def landings():
            kv = pl.ds(pl.multiple_of(b // copies * HEAD_DIM, HEAD_DIM), HEAD_DIM)
            return (
                wq_out.at[:, pl.ds(pl.multiple_of(b * q_cols, HEAD_DIM), q_cols)],
                wk_out.at[b % copies, :, kv],
                wv_out.at[b % copies, :, kv],
            )

        spans = (
            pl.ds(0, q_cols),
            pl.ds(q_cols, HEAD_DIM),
            pl.ds(q_cols + HEAD_DIM, HEAD_DIM),
        )

        def block_copies(k):
            for w, there in enumerate(landings()):
                yield along.copy(
                    k, w_sum.at[along.peer(k), :, spans[w]], there, block_sems.at[w]
                )

        def pack_copy(k):
            tile = along.peer(k) * rows_here // 128 * 128
            part = g_sum.at[:, pl.ds(pl.multiple_of(tile, 128), 128)]
            return along.copy(k, part, g_last.at[b], pack_sems)

        move_out = pltpu.make_async_remote_copy(
            src_ref=o_sum,
            dst_ref=o_out,
            send_sem=moved.at[0],
            recv_sem=moved.at[1],
            device_id={"head": th, "blk": tb},
            device_id_type=MESH,
        )
        keep_out = pltpu.make_async_copy(o_sum, o_out, moved.at[2])

        def hop(e):
            weight, part, order = entries[e]
            return flip_copy(
                ff_src[weight].at[1, part], ff_out[weight].at[part], order[0], ff_sems, e
            )

        own_w = pltpu.make_async_copy(w_src.at[h], w_in.at[0], local.at[0])
        own_g = pltpu.make_async_copy(g_part(h), g_in.at[0], local.at[1])
        own_blocks = [
            pltpu.make_async_copy(w_sum.at[b, :, spans[w]], there, local.at[4 + w])
            for w, there in enumerate(landings())
        ]
        own_o = pltpu.make_async_copy(o_src.at[h], o_in.at[0], local.at[3])
        scatter = Scatter(line, part, bufs, sems)
        scatter.start()
        own_w.start()
        own_g.start()
        own_o.start()
        for k in range(1, n_head):
            g_copy(k).start()
            w_copy(k).start()
        for k in range(1, n_head):
            o_copy(k).start()
        for e in range(len(entries)):
            hop(e).start()
        scatter.step(0)
        own_g.wait()
        for k in range(1, n_head):
            g_copy(k).wait_recv()
        g_sum[...] = sum(g_in[k] for k in range(n_head))
        own_tile = b * rows_here // 128 * 128
        g_last[b] = g_sum[:, pl.ds(pl.multiple_of(own_tile, 128), 128)]
        for k in range(1, n_blk):
            pack_copy(k).start()
        for tau in range(1, chips - 2):
            scatter.step(tau)
        own_w.wait()
        for k in range(1, n_head):
            w_copy(k).wait_recv()

        def add(j, carry):
            total = w_in[0, j].astype(F32)
            for k in range(1, n_head):
                total += w_in[k, j].astype(F32)
            w_sum[j] = total.astype(BF16)
            return carry

        lax.fori_loop(0, n_blk, add, 0)
        for one in own_blocks:
            one.start()
        for k in range(1, n_blk):
            for copy in block_copies(k):
                copy.start()

        scatter.step(chips - 2)
        own_o.wait()
        for k in range(1, n_head):
            o_copy(k).wait_recv()

        def add_out(r):
            total = o_in[0, r, :].astype(F32)
            for k in range(1, n_head):
                total += o_in[k, r, :].astype(F32)
            o_sum[r, :] = total.astype(BF16)

        by_rows(rows_here, 16, add_out)

        @pl.when(stays)
        def _():
            keep_out.start()

        @pl.when(jnp.logical_not(stays))
        def _():
            move_out.start()

        def consume(r, dxn):
            unit, factor = unit_of(x_ref[r, :].astype(F32))
            out[r, :] = unit_back(dxn * gain_ref[0:1, :], unit, factor)

        scatter.total(consume)
        for k in range(1, n_blk):
            pack_copy(k).wait_recv()
        g_out[...] = sum(g_last[k] for k in range(n_blk))
        scatter.finish()
        for one in own_blocks:
            one.wait()
        for k in range(1, n_head):
            g_copy(k).wait_send()
            o_copy(k).wait_send()
            w_copy(k).wait_send()
        for k in range(1, n_blk):
            pack_copy(k).wait_send()
            for copy in block_copies(k):
                copy.wait()
        for e in range(len(entries)):
            hop(e).wait()

        @pl.when(stays)
        def _():
            keep_out.wait()

        @pl.when(jnp.logical_not(stays))
        def _():
            move_out.wait()

    return pl.pallas_call(
        kernel,
        out_shape=(
            jax.ShapeDtypeStruct((count, width), F32),
            jax.ShapeDtypeStruct((rows_here, n_blk * q_cols), BF16),
            *[jax.ShapeDtypeStruct((copies, rows_here, n_blk // copies * HEAD_DIM), BF16)] * 2,
            jax.ShapeDtypeStruct((rows_here, width), BF16),
            jax.ShapeDtypeStruct((pack.shape[0], 128), F32),
            *(jax.ShapeDtypeStruct(one.shape[1:], BF16) for one in sums),
        ),
        in_specs=[ANYWHERE] * (4 + n_sums) + [IN_VMEM] * 2,
        out_specs=[IN_VMEM] + [ANYWHERE] * 4 + [IN_VMEM] + [ANYWHERE] * n_sums,
        scratch_shapes=[
            *scatter_bufs(chips, count, width),
            pltpu.VMEM((n_head, n_blk, rows_here, columns), BF16),
            pltpu.VMEM((n_blk, rows_here, columns), BF16),
            pltpu.VMEM((n_head, rows_here, width), BF16),
            pltpu.VMEM((rows_here, width), BF16),
            pltpu.VMEM((n_head, pack.shape[0], n_blk * rows_here), F32),
            pltpu.VMEM((pack.shape[0], n_blk * rows_here), F32),
            pltpu.VMEM((n_blk, pack.shape[0], 128), F32),
            pair_sems(n_head),
            pltpu.SemaphoreType.DMA((3, 2, n_blk)),
            pair_sems(n_head),
            pair_sems(n_head),
            pair_sems(n_blk),
            pltpu.SemaphoreType.DMA((3,)),
            pair_sems(max(1, len(entries))),
            pltpu.SemaphoreType.DMA((7,)),
        ],
        compiler_params=params(collective_id),
        cost_estimate=comm_cost(total_rows * width),
        name="last_scatter",
    )(
        partial_rows.astype(BF16).reshape(chips, 2, count, width),
        w_grad,
        out_grad.reshape(n_head, rows_here, width),
        pack,
        *sums,
        hidden,
        gain,
    )


ROWS = 256
CHUNKS = 2


def block_of(k, size=ROWS):
    return pl.ds(pl.multiple_of(k * size, size), size)


class View:
    def __init__(self, ref, rows):
        self.ref, self.rows = ref, rows
        self.at = self

    def __getitem__(self, index):
        if len(index) == 3:
            j, core, inner = index
            return self.ref.at[j, core, pl.ds(self.rows.start + inner.start, inner.size)]
        j, core = index
        return self.ref.at[j, core, self.rows]


def scatter_gather(
    partial_rows, prepare, between, inputs, outputs, beside, n_head, n_blk, collective_id
):
    total_rows, width = partial_rows.shape
    chips, count = n_blk // 2, total_rows // n_blk
    size = count // CHUNKS
    operands, results, result_specs, more_scratch, aliases, make = beside
    n_in, n_out, n_op, n_res = len(inputs), len(outputs), len(operands), len(results)

    def kernel(part, *refs):
        refs = list(refs)

        def take(n):
            taken = refs[:n]
            del refs[:n]
            return taken

        ins, ops, outs = take(n_in), take(n_op), take(n_out)
        (gathered,) = take(1)
        ress = take(n_res)
        (made,) = take(1)
        chunk_scratch = [take(6) for _ in range(CHUNKS)]
        line = Line(n_blk)
        across = Exchange("head", n_head)
        greet_all((across,), line)
        prepare(outs)
        other = make(ops, ress, refs)
        scatters, gathers = [], []
        for q in range(CHUNKS):
            own, sib, inn, outgoing, sems, g_sems = chunk_scratch[q]
            rows = pl.ds(q * size, size)
            scatters.append(Scatter(line, View(part, rows), (own, sib, inn, outgoing), sems))
            gathers.append(Gather(line, made.at[rows], View(gathered, rows), g_sems))

        def turn(q):
            def consume(r, value):
                r = pl.ds(pl.multiple_of(r.start + q * size, 16), r.size)
                made[r, :] = between(r, value, ins, outs).astype(BF16)

            scatters[q].total(consume)
            gathers[q].start()

        scatters[0].start()
        other.start()
        for q in range(1, CHUNKS):
            scatters[q].start()
        for q in range(CHUNKS):
            for tau in range(chips - 1):
                scatters[q].step(tau)
                if q:
                    gathers[q - 1].step(tau + 1)
            turn(q)
        for s in range(1, chips):
            gathers[-1].step(s)
        for q in range(CHUNKS):
            scatters[q].finish()
            gathers[q].finish()
        other.finish()

    per_chunk = []
    for _ in range(CHUNKS):
        per_chunk += [*scatter_bufs(chips, size, width), gather_sems(chips)]
    given = pl.pallas_call(
        kernel,
        out_shape=(
            *outputs,
            jax.ShapeDtypeStruct((chips, 2, count, width), BF16),
            *results,
        ),
        in_specs=[ANYWHERE] + [IN_VMEM] * n_in + [ANYWHERE] * n_op,
        out_specs=[IN_VMEM] * n_out + [ANYWHERE] + list(result_specs),
        scratch_shapes=[pltpu.VMEM((count, width), BF16), *per_chunk, *more_scratch],
        input_output_aliases={1 + n_in + i: n_out + 1 + o for i, o in aliases.items()},
        compiler_params=params(collective_id),
        cost_estimate=comm_cost(2 * total_rows * width),
        name="scatter_gather",
    )(partial_rows.astype(BF16).reshape(chips, 2, count, width), *inputs, *operands)
    return (
        *given[:n_out],
        given[n_out].reshape(total_rows, width),
        *given[n_out + 1 :],
    )


def spread_beside(full, n_head):
    entries = ff_entries(full[0].shape[1], n_head)

    def make(ops, ress, scratch):
        return Spread(ress, entries, n_head, scratch[0])

    return (
        tuple(full),
        tuple(jax.ShapeDtypeStruct(w.shape, w.dtype) for w in full),
        [ANYWHERE] * 3,
        [Spread.sem_shape(n_head)],
        {0: 0, 1: 1, 2: 2},
        make,
    )


def collect_beside(have, carried, n_head):
    entries = ff_entries(have[0].shape[1], n_head)
    levels = n_head.bit_length() - 2
    shapes = [(n_head // 2, *one.shape[1:]) for one in have]

    def make(ops, ress, scratch):
        kept, inbox = scratch[0:3], scratch[3:6]
        return Collect(ops[:3], kept, inbox, ress[:3], entries, n_head, scratch[6])

    return (
        (*have, carried),
        (
            *(jax.ShapeDtypeStruct((2, *one.shape[1:]), BF16) for one in have),
            jax.ShapeDtypeStruct(carried.shape, carried.dtype),
        ),
        [IN_VMEM] * 3 + [ANYWHERE],
        [
            *(pltpu.VMEM(shape, BF16) for shape in shapes),
            *(pltpu.VMEM((levels, *shape), BF16) for shape in shapes),
            Collect.sem_shape(n_head),
        ],
        {3: 3},
        make,
    )


def turned(values, cosine, sine):
    return values * cosine + pltpu.roll(values, HEAD_DIM // 2, 1) * sine


def local_params(collective_id):
    if collective_id is None:
        return pltpu.CompilerParams(vmem_limit_bytes=60 * 2**20)
    return pltpu.CompilerParams(
        collective_id=collective_id, has_side_effects=True, vmem_limit_bytes=60 * 2**20
    )


def spec_of(shape, dtype):
    return jax.ShapeDtypeStruct(shape, dtype)


def attention_forward(
    x_all, w_attn, vec, gates, tables, out_moved, cot, ff, q_here, n_head, n_blk, collective_id
):
    pack, width = x_all.shape
    chips, count = n_blk // 2, cot.shape[0]
    rows_here, rows_ff = out_moved.shape[0], ff[0].shape[0]
    entries = ff_entries(rows_ff, n_head)
    columns = w_attn.shape[1]
    q_cols = q_here * HEAD_DIM
    blocks = pack // ROWS
    scale = 1.0 / math.sqrt(HEAD_DIM)

    def kernel(x_hbm, moved_hbm, *refs):
        ff_src, (cot_ref, w_ref, vec_ref, gate_ref) = refs[:3], refs[3:7]
        cos_ref, sin_ref, low_ref, code_ref, key_ref = refs[7:12]
        part_hbm, xn_hbm, p_hbm, cot_hbm = refs[12:16]
        ff_out, refs = refs[16:19], refs[19:]
        lin_ref, q_ref, k_ref, v_ref, sig_ref, o_ref, gated_ref, o_rows = refs[:8]
        x_s, xn_s, p_s, in_sem, xn_sem, p_sem, part_sem = refs[8:15]
        cot_sems, out_sems, ff_sems, own_sem = refs[15:]
        line = Line(n_blk)
        across = Exchange("head", n_head)
        h_me, b_me = across.me, line.me
        greet_all((across,), line)
        mine = pl.ds(pl.multiple_of(h_me * rows_here, rows_here), rows_here)

        def out_copy(k):
            return across.copy(k, moved_hbm, o_rows.at[mine], out_sems)

        def hop(e):
            weight, part, order = entries[e]
            return flip_copy(
                ff_src[weight].at[part], ff_out[weight].at[part], order[0], ff_sems, e
            )

        own_out = pltpu.make_async_copy(moved_hbm, o_rows.at[mine], own_sem)
        gather = Gather(line, cot_ref, cot_hbm, cot_sems)
        for k in range(1, n_head):
            out_copy(k).start()
        own_out.start()
        gather.start()
        for e in range(len(entries)):
            hop(e).start()

        def load(n):
            return pltpu.make_async_copy(x_hbm.at[block_of(n)], x_s.at[block_of(n)], in_sem.at[n])

        def xn_store(n):
            return pltpu.make_async_copy(
                xn_s.at[block_of(n)], xn_hbm.at[block_of(n)], xn_sem.at[n]
            )

        def p_store(h, n):
            return pltpu.make_async_copy(
                p_s.at[h, block_of(n)], p_hbm.at[h, block_of(n)], p_sem.at[h, n]
            )

        def part_store(n):
            return pltpu.make_async_copy(
                x_s.at[block_of(n)], part_hbm.at[block_of(n)], part_sem.at[n]
            )

        for n in range(blocks):
            load(n).start()

        def project(n, carry):
            r = block_of(n)
            load(n).wait()
            unit, _ = unit_of(x_s[r, :].astype(F32))
            xn = (unit * vec_ref[0:1, :]).astype(BF16)
            xn_s[r, :] = xn
            xn_store(n).start()
            lin = mm(xn, w_ref[...])
            lin_ref[r, :] = lin
            gate = mm_nt(xn, gate_ref[...])
            one_of = lax.broadcasted_iota(jnp.int32, (ROWS, HEADS), 1)
            lane = lax.broadcasted_iota(jnp.int32, (ROWS, GATE_PAD), 1)
            sigs = jnp.zeros((ROWS, GATE_PAD), F32)
            for h in range(q_here):
                own = jnp.where(one_of == b_me * q_here + h, gate, 0.0)
                own = jax.nn.sigmoid(jnp.sum(own, axis=1, keepdims=True))
                sigs = jnp.where(lane == h, own, sigs)
            sig_ref[r, :] = sigs
            cosine, sine = cos_ref[r, :], sin_ref[r, :]
            for h in range(q_here):
                at = slice(h * HEAD_DIM, (h + 1) * HEAD_DIM)
                unit_q, _ = unit_of(lin[:, at])
                q_ref[r, at] = turned(unit_q * vec_ref[2:3, :HEAD_DIM], cosine, sine).astype(BF16)
            unit_k, _ = unit_of(lin[:, q_cols : q_cols + HEAD_DIM])
            k_ref[r, :] = turned(unit_k * vec_ref[3:4, :HEAD_DIM], cosine, sine).astype(BF16)
            v_ref[r, :] = lin[:, q_cols + HEAD_DIM :].astype(BF16)
            return carry

        lax.fori_loop(0, blocks, project, 0)
        gather.step(1)
        own_out.wait()
        for k in range(1, n_head):
            out_copy(k).wait_recv()

        def attend(n, carry):
            r = block_of(n)
            visible = (key_ref[...] >= low_ref[r, 0:1]) & (key_ref[...] <= code_ref[r, 0:1])
            for h in range(q_here):
                at = slice(h * HEAD_DIM, (h + 1) * HEAD_DIM)
                scores = mm_nt(q_ref[r, at], k_ref[...]) * scale
                scores = jnp.where(visible, scores, MASKED)
                top = jnp.max(scores, axis=-1, keepdims=True)
                weights = jnp.exp(scores - top)
                weights = weights * (1.0 / jnp.sum(weights, axis=-1, keepdims=True))
                prob = weights.astype(BF16)
                p_s[h, r, :] = prob
                p_store(h, n).start()
                out = mm(prob, v_ref[...]).astype(BF16)
                o_ref[r, at] = out
                gated_ref[r, at] = (out.astype(F32) * sig_ref[r, h : h + 1]).astype(BF16)
            x_s[r, :] = mm(gated_ref[r, :], o_rows[...]).astype(BF16)
            part_store(n).start()
            return carry

        lax.fori_loop(0, blocks - 1, attend, 0)
        gather.step(2)
        lax.fori_loop(blocks - 1, blocks, attend, 0)
        for s in range(3, chips):
            gather.step(s)
        gather.finish()
        for k in range(1, n_head):
            out_copy(k).wait_send()
        for e in range(len(entries)):
            hop(e).wait()
        for n in range(blocks):
            xn_store(n).wait()
            part_store(n).wait()
            for h in range(q_here):
                p_store(h, n).wait()

    dma = pltpu.SemaphoreType.DMA
    return pl.pallas_call(
        kernel,
        out_shape=(
            spec_of((pack, width), BF16),
            spec_of((pack, width), BF16),
            spec_of((q_here, pack, pack), BF16),
            spec_of((chips, 2, count, width), BF16),
            *(spec_of(w.shape, BF16) for w in ff),
            spec_of((pack, columns), F32),
            spec_of((pack, q_cols), BF16),
            spec_of((pack, HEAD_DIM), BF16),
            spec_of((pack, HEAD_DIM), BF16),
            spec_of((pack, GATE_PAD), F32),
            spec_of((pack, q_cols), BF16),
            spec_of((pack, q_cols), BF16),
            spec_of((q_cols, width), BF16),
        ),
        in_specs=[ANYWHERE] * 5 + [IN_VMEM] * 9,
        out_specs=[ANYWHERE] * 7 + [IN_VMEM] * 8,
        scratch_shapes=[
            pltpu.VMEM((pack, width), BF16),
            pltpu.VMEM((pack, width), BF16),
            pltpu.VMEM((q_here, pack, pack), BF16),
            dma((blocks,)),
            dma((blocks,)),
            dma((q_here, blocks)),
            dma((blocks,)),
            gather_sems(chips),
            pair_sems(n_head),
            pair_sems(len(entries)),
            dma,
        ],
        compiler_params=local_params(collective_id),
        cost_estimate=comm_cost(pack * width),
        name="attention_forward",
    )(x_all, out_moved, *ff, cot, w_attn, vec, gates, *tables)


def attention_backward(
    dy, xn, p, saved, w_attn, vec, gates, tables, mlp_gain_part, q_here, beside=None
):
    pack, width = dy.shape
    columns = w_attn.shape[1]
    q_cols = q_here * HEAD_DIM
    blocks = pack // ROWS
    scale = 1.0 / math.sqrt(HEAD_DIM)

    have, n_head, collective_id = beside or ((), 0, None)
    n_have = len(have)
    sum_scratch = []
    if have:
        entries = ff_entries(have[0].shape[1], n_head)
        sum_scratch = [pair_sems(len(entries))]

    def kernel(dy_hbm, xn_hbm, p_hbm, *refs):
        have_refs, refs = refs[:n_have], refs[n_have:]
        n_plain = 14 + 4
        plain, more = refs[:n_plain], refs[n_plain:]
        got, more = more[:n_have], more[n_have:]
        plain_scratch, sems = more[:14], more[14:]
        if not have:
            return local(dy_hbm, xn_hbm, p_hbm, *plain, *plain_scratch)
        greet_all((Exchange("head", n_head),))
        copies = [
            flip_copy(have_refs[w].at[1, part], got[w].at[part], order[0], sems[0], e)
            for e, (w, part, order) in enumerate(entries)
        ]
        for copy in copies:
            copy.start()
        local(dy_hbm, xn_hbm, p_hbm, *plain, *plain_scratch)
        for copy in copies:
            copy.wait()

    def local(dy_hbm, xn_hbm, p_hbm, lin_ref, q_ref, k_ref, v_ref, sig_ref, o_ref, *refs):
        gated_ref, o_rows, w_ref, vec_ref, gate_ref, cos_ref, sin_ref, mlp_ref = refs[:8]
        dxn_hbm, dw_ref, pack_ref, dout_ref = refs[8:12]
        dy_s, xn_s, p_s, do_s, delta_s, dgate_s, dlin_s, dk_s, dv_s, dgq_s = refs[12:22]
        dy_sem, xn_sem, p_sem, out_sem = refs[22:]
        first_head = lax.axis_index("blk") * q_here

        def dy_load(n):
            return pltpu.make_async_copy(
                dy_hbm.at[block_of(n)], dy_s.at[block_of(n)], dy_sem.at[n]
            )

        def p_load(h, n):
            return pltpu.make_async_copy(
                p_hbm.at[h, block_of(n)], p_s.at[h, block_of(n)], p_sem.at[h, n]
            )

        def dxn_store(n):
            return pltpu.make_async_copy(
                dy_s.at[block_of(n)], dxn_hbm.at[block_of(n)], out_sem.at[n]
            )

        xn_load = pltpu.make_async_copy(xn_hbm, xn_s, xn_sem)
        for n in range(blocks):
            dy_load(n).start()
        for n in range(blocks):
            for h in range(q_here):
                p_load(h, n).start()
        xn_load.start()

        def through_gate(n, carry):
            r = block_of(n)
            dy_load(n).wait()
            dgated = mm_nt(dy_s[r, :], o_rows[...])
            lane = lax.broadcasted_iota(jnp.int32, (ROWS, GATE_PAD), 1)
            dgates = jnp.zeros((ROWS, GATE_PAD), F32)
            deltas = jnp.zeros((ROWS, GATE_PAD), F32)
            for h in range(q_here):
                at = slice(h * HEAD_DIM, (h + 1) * HEAD_DIM)
                sig = sig_ref[r, h : h + 1]
                out = o_ref[r, at].astype(F32)
                do = (dgated[:, at] * sig).astype(BF16)
                do_s[r, at] = do
                dgate = jnp.sum(dgated[:, at] * out, axis=-1, keepdims=True) * sig * (1.0 - sig)
                delta = jnp.sum(do.astype(F32) * out, axis=-1, keepdims=True)
                dgates = jnp.where(lane == first_head + h, dgate, dgates)
                deltas = jnp.where(lane == h, delta, deltas)
            dgate_s[r, :] = dgates.astype(BF16)
            delta_s[r, :] = deltas
            return carry

        lax.fori_loop(0, blocks, through_gate, 0)

        def out_grad(n, carry):
            c = block_of(n)
            dout_ref[:, c] = mm_tn(gated_ref[...], dy_s[:, c]).astype(BF16)
            return carry

        lax.fori_loop(0, width // ROWS, out_grad, 0)
        dk_s[...] = jnp.zeros_like(dk_s)
        dv_s[...] = jnp.zeros_like(dv_s)
        dgq_s[...] = jnp.zeros_like(dgq_s)

        def into_lin(grad, lin, gain, r):
            grad = turned(grad.astype(BF16).astype(F32), cos_ref[r, :], -sin_ref[r, :])
            unit, factor = unit_of(lin)
            return unit_back(grad * gain, unit, factor).astype(BF16), grad * unit

        def attend(n, carry):
            r = block_of(n)
            for h in range(q_here):
                at = slice(h * HEAD_DIM, (h + 1) * HEAD_DIM)
                p_load(h, n).wait()
                do, prob, q = do_s[r, at], p_s[h, r, :], q_ref[r, at]
                dp = mm_nt(do, v_ref[...])
                ds = (prob.astype(F32) * (dp - delta_s[r, h : h + 1])).astype(BF16)
                dq = mm(ds, k_ref[...]) * scale
                dk_s[...] += mm(q.T, ds)
                dv_s[...] += mm(do.T, prob)
                dlin, part = into_lin(dq, lin_ref[r, at], vec_ref[2:3, :HEAD_DIM], r)
                dlin_s[r, at] = dlin
                dgq_s[...] += jnp.sum(part.reshape(ROWS // 8, 8, HEAD_DIM), axis=0)
            return carry

        lax.fori_loop(0, blocks, attend, 0)
        every = pl.ds(0, pack)
        k_cols = slice(q_cols, q_cols + HEAD_DIM)
        dlin, part = into_lin(
            dk_s[...].T * scale, lin_ref[:, k_cols], vec_ref[3:4, :HEAD_DIM], every
        )
        dlin_s[:, k_cols] = dlin
        dgk = jnp.sum(part, axis=0, keepdims=True)
        dgq = jnp.sum(dgq_s[...], axis=0, keepdims=True)
        pack_ref[HEADS:, :] = jnp.zeros((PACK_ROWS - HEADS, width), F32)
        pack_ref[HEADS : HEADS + 1, :] = jnp.sum(mlp_ref[...], axis=0, keepdims=True)
        for t in range(width // HEAD_DIM):
            lanes = slice(t * HEAD_DIM, (t + 1) * HEAD_DIM)
            pack_ref[HEADS + 1 : HEADS + 2, lanes] = dgq
            pack_ref[HEADS + 2 : HEADS + 3, lanes] = dgk
        dlin_s[:, q_cols + HEAD_DIM :] = dv_s[...].T.astype(BF16)

        def into_x(n, carry):
            r = block_of(n)
            dxn = mm_nt(dlin_s[r, :], w_ref[...]) + mm(dgate_s[r, :HEADS], gate_ref[...])
            dy_s[r, :] = dxn.astype(BF16)
            dxn_store(n).start()
            return carry

        lax.fori_loop(0, blocks, into_x, 0)
        xn_load.wait()
        dgate_t = dgate_s[...].astype(F32).T[:HEADS].astype(BF16)

        def weights(n, carry):
            c = block_of(n)
            xn_cols = xn_s[:, c]
            dw_ref[c, :] = mm_tn(xn_cols, dlin_s[...]).astype(BF16)
            pack_ref[:HEADS, c] = mm(dgate_t, xn_cols)
            return carry

        lax.fori_loop(0, width // ROWS, weights, 0)
        for n in range(blocks):
            dxn_store(n).wait()

    return pl.pallas_call(
        kernel,
        out_shape=(
            spec_of((pack, width), BF16),
            spec_of((width, columns), BF16),
            spec_of((PACK_ROWS, width), F32),
            spec_of((q_cols, width), BF16),
            *(spec_of(one.shape[1:], BF16) for one in have),
        ),
        in_specs=[ANYWHERE] * (3 + n_have) + [IN_VMEM] * 14,
        out_specs=[ANYWHERE] + [IN_VMEM] * 3 + [ANYWHERE] * n_have,
        scratch_shapes=[
            pltpu.VMEM((pack, width), BF16),
            pltpu.VMEM((pack, width), BF16),
            pltpu.VMEM((q_here, pack, pack), BF16),
            pltpu.VMEM((pack, q_cols), BF16),
            pltpu.VMEM((pack, GATE_PAD), F32),
            pltpu.VMEM((pack, GATE_PAD), BF16),
            pltpu.VMEM((pack, columns), BF16),
            pltpu.VMEM((HEAD_DIM, pack), F32),
            pltpu.VMEM((HEAD_DIM, pack), F32),
            pltpu.VMEM((8, HEAD_DIM), F32),
            pltpu.SemaphoreType.DMA((blocks,)),
            pltpu.SemaphoreType.DMA,
            pltpu.SemaphoreType.DMA((q_here, blocks)),
            pltpu.SemaphoreType.DMA((blocks,)),
            *sum_scratch,
        ],
        compiler_params=local_params(collective_id),
        name="attention_backward",
    )(dy, xn, p, *have, *saved, w_attn, vec, gates, *tables, mlp_gain_part)


class Rows:
    def __init__(self, ref, q, size, chips):
        self.ref, self.base, self.size = ref, q * size * chips * 2, size
        self.at = self

    def rows(self, j, core, start=0, count=None):
        first = self.base + (j * 2 + core) * self.size + start
        return pl.ds(pl.multiple_of(first, 16), count or self.size)

    def __getitem__(self, index):
        j, core, *inner = index
        if inner:
            return self.ref.at[self.rows(j, core, inner[0].start, inner[0].size)]
        return self.ref.at[self.rows(j, core)]


class OwnRows:
    def __init__(self, rows, core):
        self.view, self.core = rows, core
        self.shape = (0, rows.size)

    def __getitem__(self, index):
        j, r, _ = index
        return self.view.ref[self.view.rows(j, self.core, r.start, r.size), :]


class LocalScatter(Scatter):
    def __init__(self, line, part, bufs, sems):
        super().__init__(line, part, (OwnRows(part, line.c), *bufs), sems)

    def start(self):
        chips = self.line.chips
        order = []
        for k in range((chips + 1) // 2):
            order += [chips - 1 - k, k]
        for j in order[:chips]:
            self.to_sibling(j).start()

    def ready(self, j):
        self.to_sibling(j).wait_recv()


def feed_forward(attn_part, ff, halfway, cot, inputs, to_mlp, to_attention, n_head, n_blk, collective_id):
    total_rows, width = attn_part.shape
    chips, count = n_blk // 2, total_rows // n_blk
    size, half = count // CHUNKS, total_rows // CHUNKS
    rows_ff = ff[0].shape[0]
    units = n_head * rows_ff
    entries = ff_entries(rows_ff, n_head)
    n_in = len(inputs)

    def kernel(part, cot_hbm, *refs):
        refs = list(refs)

        def take(n):
            taken = refs[:n]
            del refs[:n]
            return taken

        sources = take(3), take(3)
        ins = take(n_in)
        middle, dmid, gain_part, dy_hbm, mlp_hbm, *sum_hbm = take(8)
        made, hn_s, cot_s, dhn_s, u_s, da_s, db_s, stage = take(8)
        inboxes, weights = take(3), take(3)
        chunk_scratch = [take(8) for _ in range(CHUNKS)]
        load_sems, hop_sems, cot_sems, stage_sems, sum_sems, grad_sems = refs
        line = Line(n_blk)
        across = Exchange("head", n_head)
        greet_all((across,), line)
        gain_part[...] = jnp.zeros_like(gain_part)

        def place(key, span):
            return pl.ds(key * rows_ff + span.start, span.size)

        loads, hops = [], []
        for e, (w, span, order) in enumerate(entries):
            first, second = 1 << order[0], 1 << order[1]
            for at, key in enumerate((0, first)):
                src = sources[at][w].at[span]
                loads.append(
                    pltpu.make_async_copy(src, weights[w].at[place(key, span)], load_sems.at[e, at])
                )
                there = weights[w].at[place(key ^ second, span)]
                hops.append(flip_copy(src, there, order[1], hop_sems, e, at))

        def cot_loads(q):
            for j in range(chips):
                for c in range(2):
                    yield pltpu.make_async_copy(
                        cot_hbm.at[j, c, pl.ds(q * size, size)],
                        Rows(cot_s, q, size, chips)[j, c],
                        cot_sems.at[q, 2 * j + c],
                    )

        first, gather1, second, gather2 = [], [], [], []
        for q in range(CHUNKS):
            own, sib, inn, outgoing, sems, g_sems, sems2, g_sems2 = chunk_scratch[q]
            rows = pl.ds(q * size, size)
            first.append(Scatter(line, View(part, rows), (own, sib, inn, outgoing), sems))
            gather1.append(Gather(line, made.at[rows], Rows(hn_s, q, size, chips), g_sems))
            second.append(
                LocalScatter(line, Rows(dhn_s, q, size, chips), (sib, inn, outgoing), sems2)
            )
            gather2.append(Gather(line, made.at[rows], View(dy_hbm, rows), g_sems2))

        def turn(q, scatter, between, outs, gather):
            def consume(r, value):
                r = pl.ds(pl.multiple_of(r.start + q * size, 16), r.size)
                made[r, :] = between(r, value, ins, outs).astype(BF16)

            scatter[q].total(consume)
            gather[q].start()

        def loop(steps, body):
            lax.fori_loop(0, steps, lambda k, carry: body(k) or carry, 0)

        def span_of(q):
            return pl.ds(q * half, half)

        def unit_block(q, f):
            r, fr = span_of(q), block_of(f)
            a = mm_nt(hn_s[r, :], weights[0][fr, :])
            b = mm_nt(hn_s[r, :], weights[1][fr, :])
            du = mm_nt(cot_s[r, :], weights[2][fr, :])
            sig = jax.nn.sigmoid(a)
            silu = a * sig
            u_s[r, fr] = (silu * b).astype(BF16)
            da_s[r, fr] = (du * b * sig * (1.0 + a * (1.0 - sig))).astype(BF16)
            db_s[r, fr] = (du * silu).astype(BF16)

        def back(q):
            r = span_of(q)

            def body(n):
                cols = block_of(n, 512)
                dhn = mm(da_s[r, :], weights[0][:, cols]) + mm(db_s[r, :], weights[1][:, cols])
                dhn_s[r, cols] = dhn.astype(BF16)

            loop(width // 512, body)

        def stage_stores(q):
            for j in range(chips):
                for c in range(2):
                    yield pltpu.make_async_copy(
                        Rows(stage, 0, size, chips)[j, c],
                        mlp_hbm.at[j, c, pl.ds(q * size, size)],
                        stage_sems.at[2 * j + c],
                    )

        def mlp_out(q):
            if q:
                for store in stage_stores(q - 1):
                    store.wait()
            r = span_of(q)

            def body(n):
                cols = block_of(n, 512)
                stage[:, cols] = mm(u_s[r, :], weights[2][:, cols]).astype(BF16)

            loop(width // 512, body)
            for store in stage_stores(q):
                store.start()

        def grad(w):
            left, right = ((da_s, hn_s), (db_s, hn_s), (u_s, cot_s))[w]

            def body(f):
                fr = block_of(f)
                weights[w][fr, :] = mm_tn(left[:, fr], right[...]).astype(BF16)

            loop(units // ROWS, body)

        def sum_copies(w):
            for e, (weight, span, order) in enumerate(entries):
                if weight == w:
                    for at, key in enumerate((0, 1 << order[0])):
                        yield flip_copy(
                            weights[w].at[place(key ^ (1 << order[1]), span)],
                            inboxes[w].at[at, span],
                            order[1],
                            sum_sems,
                            e,
                            at,
                        )

        def sum_stores(w):
            for e, (weight, span, order) in enumerate(entries):
                if weight == w:
                    for at, key in enumerate((0, 1 << order[0])):
                        yield pltpu.make_async_copy(
                            weights[w].at[place(key, span)],
                            sum_hbm[w].at[at, span],
                            grad_sems.at[e, at],
                        )

        def send_grad(w):
            grad(w)
            for copy in sum_copies(w):
                copy.start()

        def add_grad(w):
            for copy in sum_copies(w):
                copy.wait()
            for weight, span, order in entries:
                if weight == w:
                    for at, key in enumerate((0, 1 << order[0])):

                        def body(r, span=span, at=at, key=key):
                            r = pl.ds(pl.multiple_of(r.start + span.start, 16), r.size)
                            mine = pl.ds(pl.multiple_of(r.start + key * rows_ff, 16), r.size)
                            value = weights[w][mine, :].astype(F32)
                            value += inboxes[w][at, r, :].astype(F32)
                            weights[w][mine, :] = value.astype(BF16)

                        by_rows(span.size, 16, body)
            for store in sum_stores(w):
                store.start()

        first[0].start()
        for hop in hops:
            hop.start()
        for q in range(1, CHUNKS):
            first[q].start()
        for load in loads:
            load.start()
        for q in range(CHUNKS):
            for load in cot_loads(q):
                load.start()
        steps = chips - 1
        for tau in range(steps):
            first[0].step(tau)
        turn(0, first, to_mlp, (middle,), gather1)
        for tau in range(steps):
            first[1].step(tau)
            gather1[0].step(tau + 1)
        turn(1, first, to_mlp, (middle,), gather1)
        for q in range(CHUNKS):
            first[q].finish()
        gather1[0].finish()
        gather1[1].step(1)
        for load in loads:
            load.wait()
        for load in cot_loads(0):
            load.wait()
        for hop in hops:
            hop.wait()
        blocks = units // ROWS
        unit_block(0, 0)
        for s in range(2, chips):
            gather1[1].step(s)
            if s == 2:
                unit_block(0, 1)
        for f in range(2, blocks):
            unit_block(0, f)
        back(0)
        second[0].start()
        gather1[1].finish()
        for load in cot_loads(1):
            load.wait()
        second[0].step(0)
        loop(blocks, lambda f: unit_block(1, f))
        second[0].step(1)
        back(1)
        second[1].start()
        send_grad(0)
        for tau in range(2, steps):
            second[0].step(tau)
        second[1].step(0)
        send_grad(1)
        turn(0, second, to_attention, (middle, dmid, gain_part), gather2)
        second[1].step(1)
        mlp_out(0)
        mlp_out(1)
        gather2[0].step(1)
        send_grad(2)
        for tau in range(2, steps):
            second[1].step(tau)
            gather2[0].step(tau)
        turn(1, second, to_attention, (middle, dmid, gain_part), gather2)
        gather2[0].step(chips - 1)
        for s in range(1, chips):
            gather2[1].step(s)
        for w in range(3):
            add_grad(w)
        for q in range(CHUNKS):
            second[q].finish()
            gather2[q].finish()
        for store in stage_stores(CHUNKS - 1):
            store.wait()
        for w in range(3):
            for store in sum_stores(w):
                store.wait()

    per_chunk = []
    for _ in range(CHUNKS):
        own, sib, inn, outgoing, sems = scatter_bufs(chips, size, width)
        per_chunk += [own, sib, inn, outgoing, sems, gather_sems(chips), sems, gather_sems(chips)]
    sums = jax.ShapeDtypeStruct((2, rows_ff, width), BF16)
    shards_ = jax.ShapeDtypeStruct((chips, 2, count, width), BF16)
    dma = pltpu.SemaphoreType.DMA
    middle, dmid, gain_part, dy, mlp_part, *ff_sums = pl.pallas_call(
        kernel,
        out_shape=(
            jax.ShapeDtypeStruct((count, width), F32),
            jax.ShapeDtypeStruct((count, width), F32),
            jax.ShapeDtypeStruct((8, width), F32),
            shards_,
            shards_,
            *[sums] * 3,
        ),
        in_specs=[ANYWHERE] * 8 + [IN_VMEM] * n_in,
        out_specs=[IN_VMEM] * 3 + [ANYWHERE] * 5,
        scratch_shapes=[
            pltpu.VMEM((count, width), BF16),
            *[pltpu.VMEM((total_rows, width), BF16)] * 3,
            *[pltpu.VMEM((total_rows, units), BF16)] * 3,
            pltpu.VMEM((half, width), BF16),
            *[pltpu.VMEM((2, rows_ff, width), BF16)] * 3,
            *[pltpu.VMEM((units, width), BF16)] * 3,
            *per_chunk,
            dma((len(entries), 2)),
            dma((2, len(entries), 2)),
            dma((CHUNKS, n_blk)),
            dma((n_blk,)),
            dma((2, len(entries), 2)),
            dma((len(entries), 2)),
        ],
        compiler_params=pltpu.CompilerParams(
            collective_id=collective_id, has_side_effects=True, vmem_limit_bytes=62 * 2**20
        ),
        cost_estimate=comm_cost(2 * total_rows * width),
        name="feed_forward",
    )(
        attn_part.reshape(chips, 2, count, width),
        cot.reshape(chips, 2, count, width),
        *ff,
        *halfway,
        *inputs,
    )
    return (
        middle,
        dmid,
        gain_part,
        dy.reshape(total_rows, width),
        mlp_part.reshape(total_rows, width),
        ff_sums,
    )


def padded(values, size):
    return jnp.pad(values, [(0, 0)] * (values.ndim - 1) + [(0, size - values.shape[-1])])


def shards(
    hidden,
    segment_ids,
    block_ids,
    positions,
    attn_gain,
    w_query,
    key_weight_matrix,
    value_weight_matrix,
    q_gain,
    k_gain,
    w_head_gate,
    w_out,
    mlp_gain,
    w_gate,
    w_up,
    w_down,
    cotangent,
):
    n_head = lax.axis_size("head")
    n_blk = lax.axis_size("blk")
    n_all = n_head * n_blk
    my_head = lax.axis_index("head")
    my_blk = lax.axis_index("blk")
    tokens = hidden.shape[1]
    pack = tokens * n_blk
    rows_here = w_query.shape[0]
    rows_ff = w_gate.shape[0]
    q_here = HEADS // n_blk
    q_cols = q_here * HEAD_DIM
    kv_copies = max(1, n_blk // KV_HEADS)
    kv_here = max(1, KV_HEADS // n_blk)
    kv_cols = kv_here * HEAD_DIM
    device = my_head * n_blk + my_blk
    together = 128 // rows_here
    lane = jnp.arange(128)
    here = (lane // rows_here == device % together)[None]
    mine = jnp.concatenate(
        [
            attn_gain[None],
            mlp_gain[None],
            jnp.zeros((6, rows_here), BF16),
            w_head_gate.T,
        ]
    )
    small = jnp.where(here, jnp.tile(mine, (1, together)), 0).astype(F32)
    share = q_gain.shape[0]
    head_gains = jnp.stack([jnp.tile(q_gain, n_all), jnp.tile(k_gain, n_all)]).astype(F32)
    head_gains = jnp.where(lane // share == device, head_gains, 0)
    small = small + jnp.pad(head_gains, ((2, PACK_ROWS - 4), (0, 0)))
    ids = [
        lax.dynamic_slice_in_dim(ids_, my_head, 1, 0) for ids_ in (positions, segment_ids, block_ids)
    ]
    x_all, w_attn, out_moved, vec, gates, *tables = first_gather(
        hidden[0],
        (w_query, key_weight_matrix, value_weight_matrix),
        small,
        w_out,
        ids,
        q_cols,
        kv_copies,
        n_head,
        n_blk,
        0,
    )
    ff = (w_gate, w_up, w_down)
    attn_part, xn, prob, cot, *rest = attention_forward(
        x_all, w_attn, vec, gates, tables, out_moved, cotangent[0], ff, q_here, n_head, n_blk, 4
    )
    halfway, saved = rest[:3], rest[3:]

    def to_mlp(r, total, ins, outs):
        x_ref, gain_ref = ins
        mid = x_ref[r, :].astype(F32) + total
        outs[0][r, :] = mid
        unit, _ = unit_of(mid)
        return unit * gain_ref[1:2, :]

    def to_attention(r, dhn, ins, outs):
        mid_ref, cot_ref, gain_ref = ins
        unit, factor = unit_of(mid_ref[r, :])
        product = dhn * unit
        seen = outs[1]
        seen[...] += product[:8] + product[8:]
        back = cot_ref[r, :].astype(F32) + unit_back(dhn * gain_ref[1:2, :], unit, factor)
        outs[0][r, :] = back
        return back

    fused = n_head == 4 and pack <= 1024
    if fused:

        def into_mlp(r, total, ins, outs):
            return to_mlp(r, total, (ins[0], ins[2]), outs)

        def into_attention(r, dhn, ins, outs):
            return to_attention(r, dhn, (outs[0], ins[1], ins[2]), outs[1:])

        middle, dmid, mlp_gain_part, dy, mlp_part, ff_sums = feed_forward(
            attn_part,
            ff,
            halfway,
            cot,
            (hidden[0], cotangent[0], vec),
            into_mlp,
            into_attention,
            n_head,
            n_blk,
            1,
        )
    else:
        cot = cot.reshape(pack, MODEL_WIDTH)
        ff_full = []
        for w, (own, other) in enumerate(zip(ff, halfway)):
            full = jnp.zeros((n_head, *own.shape), BF16).at[0].set(own)
            for weight, part, order in ff_entries(rows_ff, n_head):
                if weight == w:
                    span = slice(part.start, part.start + part.size)
                    full = full.at[1 << order[0], span].set(other[span])
            ff_full.append(full)
        middle, hn, *ff_rows = scatter_gather(
            attn_part,
            lambda outs: None,
            to_mlp,
            (hidden[0], vec),
            (jax.ShapeDtypeStruct(hidden.shape[1:], F32),),
            spread_beside(ff_full, n_head),
            n_head,
            n_blk,
            1,
        )
        gate_rows, up_rows, down_rows = (one.reshape(n_head * rows_ff, MODEL_WIDTH) for one in ff_rows)

        a = mm_nt(hn, gate_rows)
        b = mm_nt(hn, up_rows)
        sig = jax.nn.sigmoid(a)
        silu = a * sig
        u = (silu * b).astype(BF16)
        mlp_part = mm(u, down_rows).astype(BF16)
        du = mm_nt(cot, down_rows)
        da = (du * b * sig * (1.0 + a * (1.0 - sig))).astype(BF16)
        db = (du * silu).astype(BF16)
        ff_parts = [
            mm_tn(left, right).astype(BF16).reshape(n_head, rows_ff, MODEL_WIDTH)
            for left, right in ((da, hn), (db, hn), (u, cot))
        ]

        def clear(outs):
            outs[1][...] = jnp.zeros_like(outs[1])

        dmid, mlp_gain_part, dy, *ff_sums, mlp_part = scatter_gather(
            mm(da, gate_rows) + mm(db, up_rows),
            clear,
            to_attention,
            (middle, cotangent[0], vec),
            (
                jax.ShapeDtypeStruct(hidden.shape[1:], F32),
                jax.ShapeDtypeStruct((8, MODEL_WIDTH), F32),
            ),
            collect_beside(ff_parts, mlp_part, n_head),
            n_head,
            n_blk,
            2,
        )

    layer_output = (
        middle + lax.psum_scatter(mlp_part, "blk", scatter_dimension=0, tiled=True).astype(F32)
    ).astype(BF16)[None]
    dxn_part, attn_grad, small_parts, out_grad, *ff_last = attention_backward(
        dy,
        xn,
        prob,
        saved,
        w_attn,
        vec,
        gates,
        tables[:2],
        mlp_gain_part,
        q_here,
        (ff_sums, n_head, 2) if fused else None,
    )
    back_x, query_grad, key_grad, value_grad, out_grad, small_sums, *ff_rest = last_scatter(
        dxn_part,
        attn_grad.reshape(n_head, n_blk, rows_here, -1),
        out_grad,
        small_parts,
        () if fused else ff_sums,
        hidden[0],
        vec,
        q_cols,
        kv_copies,
        n_head,
        n_blk,
        3,
    )
    ff_last = ff_last or ff_rest
    input_grad = (dmid + back_x)[None]
    ff_grads = [one[0].astype(F32) + two.astype(F32) for one, two in zip(ff_sums, ff_last)]

    query_grad = query_grad.astype(F32)
    key_grad = jnp.sum(key_grad.astype(F32), axis=0)
    value_grad = jnp.sum(value_grad.astype(F32), axis=0)
    small_sums = jnp.sum(
        jnp.where(
            jnp.arange(together)[None, :, None] == device % together,
            small_sums.reshape(PACK_ROWS, together, rows_here),
            0.0,
        ),
        axis=1,
    ), small_sums[HEADS + 1 : HEADS + 3]
    small_sums, head_sums = small_sums
    head_sums = lax.dynamic_slice_in_dim(head_sums, device * share, share, 1)
    head_gate_grad = small_sums[:HEADS].T
    attn_gain_grad = (
        jnp.sum(w_query.astype(F32) * query_grad, axis=1)
        + jnp.sum(key_weight_matrix.astype(F32) * key_grad, axis=1)
        + jnp.sum(value_weight_matrix.astype(F32) * value_grad, axis=1)
        + jnp.sum(w_head_gate.astype(F32) * head_gate_grad, axis=1)
    ) / attn_gain.astype(F32)
    return (
        layer_output,
        input_grad,
        attn_gain_grad,
        query_grad,
        key_grad,
        value_grad,
        head_sums[0],
        head_sums[1],
        head_gate_grad,
        out_grad.astype(F32),
        small_sums[HEADS],
        ff_grads[0],
        ff_grads[1],
        ff_grads[2],
    )


def solution(mesh):
    rows = P(("head", "blk"), None)
    vector = P(("head", "blk"))
    token = P("head", "blk", None)
    return jax.shard_map(
        shards,
        mesh=mesh,
        in_specs=(
            token, P(), P(), P(), vector, rows, rows, rows, vector, vector, rows, rows, vector,
            rows, rows, rows, token,
        ),
        out_specs=(
            token, token, vector, rows, rows, rows, vector, vector, rows, rows, vector,
            rows, rows, rows,
        ),
        check_vma=False,
    )
```

time: 1360 us -> 421 us (0.31)
  waiting for transfers between devices: 966 us -> 0.02 us
  Pallas kernels: 0 us -> 373 us
  blocking collectives: 117 us -> 0 us
  matrix products: 115 us -> 0 us
  local copies, waits for them, and re-layouts: 62.1 us -> 9.3 us
  other arithmetic: 55.7 us -> 16.9 us
  starting transfers between devices: 14.5 us -> 0.04 us
    all_gather x13 -> x0, waiting for transfers between devices: 534 us -> none  [the longest x2 69.3 us: group_gather(): return lax.all_gather(rows_here[None], 'head', axis=0, tiled=True)]
    pallas_call x0 -> x5, Pallas kernels: none -> 373 us  [the longest x1 157 us: feed_forward(): pl.pallas_call(kernel, out_shape=(jax.ShapeDtypeStruct((count, width), F3...]
    reduce_scatter x7 -> x1, waiting for transfers between devices: 315 us -> 0.01 us  [shards(): lax.psum_scatter(mlp_part, 'blk', scatter_dimension=0, tiled=True)]
    dot_general x31 -> x0, matrix products: 115 us -> none  [the longest x1 10.8 us: unit_backward(): jnp.einsum('td,fd->tf', grad_rows, down_rows, preferred_element_type=jnp....]
    unnamed x30 -> x1, waiting for transfers between devices: 108 us -> 0.02 us
    unnamed x2 -> x0, blocking collectives: 80.5 us -> none
    all_gather x1 -> x0, blocking collectives: 36.3 us -> none  [shards(): lax.all_gather(w_head_gate, ('head', 'blk'), axis=0, tiled=True)]
    concatenate x3 -> x1, other arithmetic: 18.3 us -> 0.78 us  [shards(): jnp.concatenate([attn_gain[None], mlp_gain[None], jnp.zeros((6, rows_here...]
  transfers between devices with their start and end apart: 29 -> 1, of which waited for: 25 -> 0; matrix products, arithmetic and copies ran while one was open for 13% -> 4% of each run, Pallas kernels for 0% -> 24%
where the time goes in v1:
time: 421 us; the launch traced here: 414 us
  Pallas kernels  373 us (89%)
  other arithmetic  16.9 us (4%)
  between operations  14.3 us (3%)
  local copies, waits for them, and re-layouts  9.3 us (2%)
    pallas_call x1, Pallas kernels, feed_forward(): pl.pallas_call(kernel, out_shape=(jax.ShapeDtypeStruct((count, width), F3...  157 us
    pallas_call x1, Pallas kernels, first_gather(): pl.pallas_call(kernel, out_shape=(jax.ShapeDtypeStruct((chips, 2, count,...  67.5 us
    pallas_call x1, Pallas kernels, last_scatter(): pl.pallas_call(kernel, out_shape=(jax.ShapeDtypeStruct((count, width), F3...  65.3 us
    pallas_call x1, Pallas kernels, attention_forward(): pl.pallas_call(kernel, out_shape=(spec_of((pack, width), BF16), spec_of((...  49.3 us
    pallas_call x1, Pallas kernels, attention_backward(): pl.pallas_call(kernel, out_shape=(spec_of((pack, width), BF16), spec_of((...  34.5 us
  transfers between devices with their start and end apart: 1, of which 0 were waited for; matrix products, arithmetic and copies ran while one was open for 4% of the time, Pallas kernels for 24%

profile of v1, /device:TPU:16, one launch (start us, length us, event | category | flops | bytes accessed | tf_op | source)
XLA Modules:
  0.0 414.0 jit_solution(9703873262920323657)
XLA Ops:
  7.4 0.8 pad_maximum_fusion
  8.2 0.7 tile.10
  9.0 0.7 tile.11
  9.8 0.6 constant_dynamic-slice_fusion.3.refs_5_
  10.4 1.3 constant_dynamic-slice_fusion.1
  11.7 0.6 pad_add_fusion.refs_3_
  12.4 67.5 %first_gather.1 = (bf16[4,2,128,2048]{3,2,1,0:T(8,128)(2,1)}, bf16[4,8,64,512]{3,2,1,0:T(8,128)(2,1)}, bf16[64,2048]{1,0:T(8,128)(2,1)}, f32[8,2048]{1,0:T(8,128...) custom-call(bf16[128,2048]{1,0:T(8,128)(2,1)} %bitcast.45, ...), custom_call_target="tpu_custom_call" | custom-call | bytes 83886080 | tf_op jit(solution)/shard_map/first_gather/pallas_call | solution.py:554
  79.9 49.3 %attention_forward.1 = (bf16[1024,2048]{1,0:T(8,128)(2,1)}, bf16[1024,2048]{1,0:T(8,128)(2,1)}, bf16[2,1024,1024]{2,1,0:T(8,128)(2,1)}, bf16[4,2,128,2048]{3,2,1...) custom-call(bf16[1024,2048]{1,0:T(8,128)(2,1)} %bitcast.52, ...), custom_call_target="tpu_custom_call" | custom-call | bytes 83886080 | tf_op jit(solution)/shard_map/attention_forward/pallas_call | solution.py:1231
  129.2 156.9 %feed_forward.1 = (f32[128,2048]{1,0:T(8,128)}, f32[128,2048]{1,0:T(8,128)}, f32[8,2048]{1,0:T(8,128)}, bf16[4,2,128,2048]{3,2,1,0:T(8,128)(2,1)}, bf16[4,2,128,...) custom-call(bf16[4,2,128,2048]{3,2,1,0:T(8,128)(2,1)} %bitcast.49, ...), custom_call_target="tpu_custom_call" | custom-call | bytes 167772160 | tf_op jit(solution)/shard_map/feed_forward/pallas_call | solution.py:1760
  286.1 34.5 %attention_backward.1 = (bf16[1024,2048]{1,0:T(8,128)(2,1)}, bf16[2048,512]{1,0:T(8,128)(2,1)}, f32[24,2048]{1,0:T(8,128)}, bf16[256,2048]{1,0:T(8,128)(2,1)}, b...) custom-call(bf16[1024,2048]{1,0:T(8,128)(2,1)} %bitcast.48, ...), custom_call_target="tpu_custom_call" | custom-call | tf_op jit(solution)/shard_map/attention_backward/pallas_call | solution.py:1427
  320.6 65.3 %last_scatter.1 = (f32[128,2048]{1,0:T(8,128)}, bf16[64,2048]{1,0:T(8,128)(2,1)}, bf16[1,64,1024]{2,1,0:T(8,128)(2,1)}, bf16[1,64,1024]{2,1,0:T(8,128)(2,1)}, bf...) custom-call(bf16[4,2,128,2048]{3,2,1,0:T(8,128)(2,1)} %bitcast.51, bf16[4,8,64,512]{3,2,1,0:T(8,128)(2,1)} %bitcast.55, ...), custom_call_target="tpu_custom_call" | custom-call | bytes 83886080 | tf_op jit(solution)/shard_map/last_scatter/pallas_call | solution.py:888
  386.0 0.8 slice.25
  386.8 0.8 reshape.98
  387.6 1.8 convert_element_type.78
  389.5 0.5 slice_bitcast_fusion.2
  390.1 0.6 multiply_reduce_fusion.3
  390.7 1.7 multiply_reduce_fusion.2
  392.4 1.7 multiply_reduce_fusion.1
  394.2 1.9 multiply_reduce_fusion
  396.1 0.5 convert_divide_fusion
  396.6 0.5 slice_bitcast_fusion.1
  397.2 1.4 convert_add_fusion.2
  398.5 0.6 copy-done.3
  399.1 0.2 copy-done.10
  399.3 1.4 convert_add_fusion.1
  400.7 0.6 copy-done.2
  401.3 0.2 copy-done.9
  401.5 1.4 convert_add_fusion
  402.9 0.7 copy-done.6
  403.6 1.1 add_bitcast_fusion
  404.7 0.5 copy-done.7
  405.2 1.9 fusion
  (40 shorter events, 0.7 us)
Async XLA Ops:
  7.2 2.6 copy-start
  7.2 397.5 %reduce-scatter.2.cloned.1.call-start = ((), (), s32[]{:S(2)}) async-start(), calls=%async_computation.1 | async-start | bytes 4718592 | tf_op jit(solution)/shard_map/reduce_scatter | solution.py:1978
  320.6 69.5 %copy-start.14 = (bf16[64,16]{0,1:T(8,128)(2,1)S(1)}, bf16[64,16]{0,1:T(8,128)(2,1)}, u32[]{:S(2)}) copy-start(bf16[64,16]{0,1:T(8,128)(2,1)} %param.27) | copy-start | bytes 6148
  320.6 70.1 %copy-start.12 = (bf16[64,1024]{1,0:T(8,128)(2,1)S(1)}, bf16[64,1024]{1,0:T(8,128)(2,1)}, u32[]{:S(2)}) copy-start(bf16[64,1024]{1,0:T(8,128)(2,1)} %refs_1_.3) | copy-start | bytes 393220
  320.6 71.8 %copy-start.13 = (bf16[64,1024]{1,0:T(8,128)(2,1)S(1)}, bf16[64,1024]{1,0:T(8,128)(2,1)}, u32[]{:S(2)}) copy-start(bf16[64,1024]{1,0:T(8,128)(2,1)} %refs_2_.3) | copy-start | bytes 393220
  385.9 8.3 %copy-start.8 = (bf16[64,2048]{1,0:T(8,128)(2,1)S(1)}, bf16[64,2048]{1,0:T(8,128)(2,1)}, u32[]{:S(2)}) copy-start(bf16[64,2048]{1,0:T(8,128)(2,1)} %refs_0_.3) | copy-start | bytes 786436
  385.9 10.2 %copy-start.15 = (bf16[64]{0:T(256)(128)(2,1)S(1)}, bf16[64]{0:T(256)(128)(2,1)}, u32[]{:S(2)}) copy-start(bf16[64]{0:T(256)(128)(2,1)} %param.21) | copy-start | bytes 388
  385.9 11.2 %copy-start.4 = (bf16[2,192,2048]{2,1,0:T(8,128)(2,1)S(1)}, bf16[2,192,2048]{2,1,0:T(8,128)(2,1)}, u32[]{:S(2)}) copy-start(bf16[2,192,2048]{2,1,0:T(8,128)(2,1)} %get-tuple-element.81.refs_0_) | copy-start | bytes 4718596
  386.0 11.2 %copy-start.11 = (bf16[192,2048]{1,0:T(8,128)(2,1)S(1)}, bf16[192,2048]{1,0:T(8,128)(2,1)}, u32[]{:S(2)}) copy-start(bf16[192,2048]{1,0:T(8,128)(2,1)} %get-tuple-element.103) | copy-start | bytes 2359300
  397.1 2.0 copy-start.3
  397.2 2.2 copy-start.10
  399.3 2.0 copy-start.2
  399.3 2.2 copy-start.9
  401.5 1.4 copy-start.5
  401.5 2.1 copy-start.6
  403.6 1.6 copy-start.7
  403.6 3.5 copy-start.1
Sparse Core Ops, SparseCore 0:
  286.2 44.8 reduce-scatter.1

commit v2 on v1

--- a/solution.py
+++ b/solution.py
@@ -176,34 +176,42 @@
     lax.fori_loop(0, rows // step, one, 0)
 
 
+SUMS = 2
+
+
 class Scatter:
     def __init__(self, line, part, bufs, sems):
         self.line, self.part, self.sems = line, part, sems
         self.own, self.sib, self.inn, self.out = bufs
 
-    def copy(self, kind, src, dst, j, target):
+    def copy(self, kind, src, dst, slot, target):
         return pltpu.make_async_remote_copy(
             src_ref=src,
             dst_ref=dst,
-            send_sem=self.sems.at[kind, j],
-            recv_sem=self.sems.at[3 + kind, j],
+            send_sem=self.sems.at[(kind, *slot)],
+            recv_sem=self.sems.at[(3 + kind, *slot)],
             device_id=target,
             device_id_type=MESH,
         )
 
     def to_sibling(self, j):
         line = self.line
-        return self.copy(2, self.part.at[j, 1 - line.c], self.sib.at[j], j, line.sibling)
+        return self.copy(2, self.part.at[j, 1 - line.c], self.sib.at[j], (j, 0), line.sibling)
 
     def to_own(self, j):
         return pltpu.make_async_copy(
-            self.part.at[j, self.line.c], self.own.at[j], self.sems.at[6, j]
+            self.part.at[j, self.line.c], self.own.at[j], self.sems.at[6, j, 0]
         )
 
-    def along(self, way, j):
+    @property
+    def size(self):
+        return self.own.shape[1] // SUMS
+
+    def along(self, way, j, p):
         line = self.line
         target = line.left if way else line.right
-        return self.copy(way, self.out.at[j], self.inn.at[way, j], j, target)
+        span = pl.ds(p * self.size, self.size)
+        return self.copy(way, self.out.at[j, span], self.inn.at[way, j, span], (j, p), target)
 
     def start(self):
         chips = self.line.chips
@@ -218,29 +226,36 @@
         self.to_sibling(j).wait_recv()
         self.to_own(j).wait()
 
+    def rows_of(self, p, body):
+        def shifted(r):
+            body(pl.ds(pl.multiple_of(r.start + p * self.size, 16), r.size))
+
+        by_rows(self.size, 16, shifted)
+
     def pass_on(self, way, j, first):
         self.ready(j)
-        rows = self.own.shape[1]
-
-        @pl.when(first)
-        def _():
-            def body(r):
-                total = self.own[j, r, :].astype(F32) + self.sib[j, r, :].astype(F32)
-                self.out[j, r, :] = total.astype(BF16)
-
-            by_rows(rows, 16, body)
-
-        @pl.when(jnp.logical_not(first))
-        def _():
-            self.along(way, j).wait_recv()
-
-            def body(r):
-                total = self.own[j, r, :].astype(F32) + self.sib[j, r, :].astype(F32)
-                self.out[j, r, :] = (total + self.inn[way, j, r, :].astype(F32)).astype(BF16)
-
-            by_rows(rows, 16, body)
-
-        self.along(way, j).start()
+        for p in range(SUMS):
+
+            @pl.when(first)
+            def _(p=p):
+                def body(r):
+                    total = self.own[j, r, :].astype(F32) + self.sib[j, r, :].astype(F32)
+                    self.out[j, r, :] = total.astype(BF16)
+
+                self.rows_of(p, body)
+
+            @pl.when(jnp.logical_not(first))
+            def _(p=p):
+                self.along(way, j, p).wait_recv()
+
+                def body(r):
+                    total = self.own[j, r, :].astype(F32) + self.sib[j, r, :].astype(F32)
+                    total += self.inn[way, j, r, :].astype(F32)
+                    self.out[j, r, :] = total.astype(BF16)
+
+                self.rows_of(p, body)
+
+            self.along(way, j, p).start()
 
     def step(self, tau):
         line = self.line
@@ -256,14 +271,15 @@
     def total(self, consume):
         line, i = self.line, self.line.i
         self.ready(i)
-
-        @pl.when(line.has_left)
-        def _():
-            self.along(0, i).wait_recv()
-
-        @pl.when(line.has_right)
-        def _():
-            self.along(1, i).wait_recv()
+        for p in range(SUMS):
+
+            @pl.when(line.has_left)
+            def _(p=p):
+                self.along(0, i, p).wait_recv()
+
+            @pl.when(line.has_right)
+            def _(p=p):
+                self.along(1, i, p).wait_recv()
 
         rows = self.own.shape[1]
 
@@ -291,21 +307,15 @@
         line = self.line
         for j in range(line.chips):
             self.to_sibling(j).wait_send()
-
-            @pl.when(j > line.i)
-            def _(j=j):
-                self.along(0, j).wait_send()
-
-            @pl.when(j < line.i)
-            def _(j=j):
-                self.along(1, j).wait_send()
-
-    def run(self, consume):
-        self.start()
-        for tau in range(self.line.chips - 1):
-            self.step(tau)
-        self.total(consume)
-        self.finish()
+            for p in range(SUMS):
+
+                @pl.when(j > line.i)
+                def _(j=j, p=p):
+                    self.along(0, j, p).wait_send()
+
+                @pl.when(j < line.i)
+                def _(j=j, p=p):
+                    self.along(1, j, p).wait_send()
 
 
 PIECES = 2
@@ -321,7 +331,7 @@
         pltpu.VMEM((chips, rows, width), BF16),
         pltpu.VMEM((2, chips, rows, width), BF16),
         pltpu.VMEM((chips, rows, width), BF16),
-        pltpu.SemaphoreType.DMA((7, chips)),
+        pltpu.SemaphoreType.DMA((7, chips, SUMS)),
     ]
 
 
@@ -429,159 +439,15 @@
     )
 
 
-def first_gather(rows, weights, pack, w_out, ids, q_cols, copies, n_head, n_blk, collective_id):
-    count, width = rows.shape
-    chips, length = n_blk // 2, n_blk * count
-    rows_here = weights[0].shape[0]
-    columns = q_cols + 2 * HEAD_DIM
-    together = 128 // rows_here
-    chunk = 256
-
-    def kernel(src, *refs):
-        w_src, (pack_src, out_src), (pos, seg, blk) = refs[:3], refs[3:5], refs[5:8]
-        out, w_all, moved_out, vec, gates, cos_ref, sin_ref, low_ref, code_ref, key_ref = refs[8:18]
-        g_all, sems, block_sems, w_sems, pack_sems, g_sems, moved, local = refs[18:]
-        line = Line(n_blk)
-        across, along = Exchange("head", n_head), Exchange("blk", n_blk)
-        h, b = across.me, along.me
-        (th, tb), (sh, sb) = place_of_out_rows(n_head, n_blk)
-        stays = (th == h) & (tb == b)
-        moves = jnp.logical_not(stays)
-        greet_all((across, along), moves=(moves, {"head": sh, "blk": sb}))
-
-        def block_copies(k):
-            for w, there, here in weight_pieces(along.peer(k), q_cols, copies):
-                yield along.copy(
-                    k, w_src[w].at[:, there], w_all.at[h, b, :, here], block_sems.at[w]
-                )
-
-        def pack_copy(k):
-            return along.copy(k, pack_src, g_all.at[h, b], pack_sems)
-
-        def w_copy(k):
-            return across.copy(k, w_all.at[h], w_all.at[h], w_sems)
-
-        def g_copy(k):
-            return across.copy(k, g_all.at[h], g_all.at[h], g_sems)
-
-        move_out = pltpu.make_async_remote_copy(
-            src_ref=out_src,
-            dst_ref=moved_out,
-            send_sem=moved.at[0],
-            recv_sem=moved.at[1],
-            device_id={"head": th, "blk": tb},
-            device_id_type=MESH,
-        )
-        keep_out = pltpu.make_async_copy(out_src, moved_out, moved.at[2])
-        locals_ = [
-            pltpu.make_async_copy(w_src[w].at[:, there], w_all.at[h, b, :, here], local.at[w])
-            for w, there, here in weight_pieces(b, q_cols, copies)
-        ] + [pltpu.make_async_copy(pack_src, g_all.at[h, b], local.at[3])]
-        for k in range(1, n_blk):
-            for copy in block_copies(k):
-                copy.start()
-        gather = Gather(line, src, out, sems)
-        gather.start()
-        for k in range(1, n_blk):
-            pack_copy(k).start()
-        for one in locals_:
-            one.start()
-
-        @pl.when(stays)
-        def _():
-            keep_out.start()
-
-        @pl.when(moves)
-        def _():
-            move_out.start()
-
-        half = HEAD_DIM // 2
-        index = lax.broadcasted_iota(jnp.int32, (half, chunk), 0).astype(F32)
-        frequency = jnp.exp(index * (-2.0 * math.log(ROPE_BASE) / HEAD_DIM))
-        key_ref[...] = (seg[...] * length + blk[...]).astype(F32)
-
-        def tables(n, carry):
-            r = block_of(n, chunk)
-            angles = frequency * pos[:, r].astype(F32)
-            cosine, sine = jnp.cos(angles), jnp.sin(angles)
-            cos_ref[r, :] = jnp.concatenate([cosine, cosine], axis=0).T
-            sin_ref[r, :] = jnp.concatenate([-sine, sine], axis=0).T
-            low_ref[r, :] = jnp.broadcast_to((seg[:, r] * length).astype(F32), (128, chunk)).T
-            code_ref[r, :] = jnp.broadcast_to(key_ref[:, r], (128, chunk)).T
-            return carry
-
-        lax.fori_loop(0, length // chunk, tables, 0)
-        for one in locals_:
-            one.wait()
-        for k in range(1, n_blk):
-            pack_copy(k).wait_recv()
-        for k in range(1, n_head):
-            g_copy(k).start()
-        gather.step(1)
-        for k in range(1, n_blk):
-            for copy in block_copies(k):
-                copy.wait_recv()
-        for k in range(1, n_head):
-            w_copy(k).start()
-        for s in range(2, chips):
-            gather.step(s)
-        for k in range(1, n_head):
-            g_copy(k).wait()
-        everyone = [g_all.at[d // n_blk, d % n_blk] for d in range(n_head * n_blk)]
-        vec[...] = jnp.zeros_like(vec)
-        for t in range(width // 128):
-            tile = sum(one[...] for one in everyone[t * together : (t + 1) * together])
-            vec[0:2, t * 128 : (t + 1) * 128] = tile[0:2]
-            gates[:, t * 128 : (t + 1) * 128] = tile[8:].astype(BF16)
-        vec[2:4, 0:128] = sum(one[2:4, :] for one in everyone)
-        gather.finish()
-        for k in range(1, n_head):
-            w_copy(k).wait()
-        for k in range(1, n_blk):
-            pack_copy(k).wait_send()
-            for copy in block_copies(k):
-                copy.wait_send()
-
-        @pl.when(stays)
-        def _():
-            keep_out.wait()
-
-        @pl.when(moves)
-        def _():
-            move_out.wait()
-
-    dma = pltpu.SemaphoreType.DMA
-    out, w_attn, *rest = pl.pallas_call(
-        kernel,
-        out_shape=(
-            jax.ShapeDtypeStruct((chips, 2, count, width), rows.dtype),
-            jax.ShapeDtypeStruct((n_head, n_blk, rows_here, columns), BF16),
-            jax.ShapeDtypeStruct(w_out.shape, w_out.dtype),
-            jax.ShapeDtypeStruct((8, width), F32),
-            jax.ShapeDtypeStruct((HEADS, width), BF16),
-            *[jax.ShapeDtypeStruct((length, 128), F32)] * 4,
-            jax.ShapeDtypeStruct((1, length), F32),
-        ),
-        in_specs=[IN_VMEM] + [ANYWHERE] * 5 + [IN_VMEM] * 3,
-        out_specs=[ANYWHERE] * 3 + [IN_VMEM] * 7,
-        scratch_shapes=[
-            pltpu.VMEM((n_head, n_blk, PACK_ROWS, 128), F32),
-            gather_sems(chips),
-            dma((3, 2, n_blk)),
-            pair_sems(n_head),
-            pair_sems(n_blk),
-            pair_sems(n_head),
-            dma((3,)),
-            dma((4,)),
-        ],
-        compiler_params=params(collective_id),
-        cost_estimate=comm_cost(n_blk * count * width),
-        name="first_gather",
-    )(rows, *weights, pack, w_out, *ids)
+PACK_ROWS = 24
+
+
+def weight_pieces(b, q_cols, copies):
+    kv = b // copies * HEAD_DIM
     return (
-        out.reshape(length, width),
-        w_attn.reshape(n_head * n_blk * rows_here, columns),
-        *rest,
+        (0, pl.ds(pl.multiple_of(b * q_cols, HEAD_DIM), q_cols), pl.ds(0, q_cols)),
+        (1, pl.ds(pl.multiple_of(kv, HEAD_DIM), HEAD_DIM), pl.ds(q_cols, HEAD_DIM)),
+        (2, pl.ds(pl.multiple_of(kv, HEAD_DIM), HEAD_DIM), pl.ds(q_cols + HEAD_DIM, HEAD_DIM)),
     )
 
 
@@ -1076,6 +942,48 @@
     )
 
 
+class Rows:
+    def __init__(self, ref, q, size, chips):
+        self.ref, self.base, self.size = ref, q * size * chips * 2, size
+        self.at = self
+
+    def rows(self, j, core, start=0, count=None):
+        first = self.base + (j * 2 + core) * self.size + start
+        return pl.ds(pl.multiple_of(first, 16), count or self.size)
+
+    def __getitem__(self, index):
+        j, core, *inner = index
+        if inner:
+            return self.ref.at[self.rows(j, core, inner[0].start, inner[0].size)]
+        return self.ref.at[self.rows(j, core)]
+
+
+class OwnRows:
+    def __init__(self, rows, core):
+        self.view, self.core = rows, core
+        self.shape = (0, rows.size)
+
+    def __getitem__(self, index):
+        j, r, _ = index
+        return self.view.ref[self.view.rows(j, self.core, r.start, r.size), :]
+
+
+class LocalScatter(Scatter):
+    def __init__(self, line, part, bufs, sems):
+        super().__init__(line, part, (OwnRows(part, line.c), *bufs), sems)
+
+    def start(self):
+        chips = self.line.chips
+        order = []
+        for k in range((chips + 1) // 2):
+            order += [chips - 1 - k, k]
+        for j in order[:chips]:
+            self.to_sibling(j).start()
+
+    def ready(self, j):
+        self.to_sibling(j).wait_recv()
+
+
 def turned(values, cosine, sine):
     return values * cosine + pltpu.roll(values, HEAD_DIM // 2, 1) * sine
 
@@ -1093,33 +1001,64 @@
 
 
 def attention_forward(
-    x_all, w_attn, vec, gates, tables, out_moved, cot, ff, q_here, n_head, n_blk, collective_id
+    rows, weights, small, w_out, ids, cot, ff, q_cols, copies, n_head, n_blk, collective_id
 ):
-    pack, width = x_all.shape
-    chips, count = n_blk // 2, cot.shape[0]
-    rows_here, rows_ff = out_moved.shape[0], ff[0].shape[0]
+    count, width = rows.shape
+    chips, pack = n_blk // 2, n_blk * count
+    rows_here, rows_ff = w_out.shape[0], ff[0].shape[0]
     entries = ff_entries(rows_ff, n_head)
-    columns = w_attn.shape[1]
-    q_cols = q_here * HEAD_DIM
+    columns, q_here = q_cols + 2 * HEAD_DIM, q_cols // HEAD_DIM
+    together, n_all = 128 // rows_here, n_head * n_blk
     blocks = pack // ROWS
     scale = 1.0 / math.sqrt(HEAD_DIM)
 
-    def kernel(x_hbm, moved_hbm, *refs):
-        ff_src, (cot_ref, w_ref, vec_ref, gate_ref) = refs[:3], refs[3:7]
-        cos_ref, sin_ref, low_ref, code_ref, key_ref = refs[7:12]
-        part_hbm, xn_hbm, p_hbm, cot_hbm = refs[12:16]
-        ff_out, refs = refs[16:19], refs[19:]
-        lin_ref, q_ref, k_ref, v_ref, sig_ref, o_ref, gated_ref, o_rows = refs[:8]
-        x_s, xn_s, p_s, in_sem, xn_sem, p_sem, part_sem = refs[8:15]
-        cot_sems, out_sems, ff_sems, own_sem = refs[15:]
+    def kernel(src, cot_ref, *refs):
+        w_src, (pack_src, out_src), ff_src = refs[:3], refs[3:5], refs[5:8]
+        pos, seg, blk_ids = refs[8:11]
+        part_hbm, xn_hbm, p_hbm, cot_hbm = refs[11:15]
+        ff_out, refs = refs[15:18], refs[18:]
+        w_ref, vec_ref, gate_ref, cos_ref, sin_ref = refs[:5]
+        lin_ref, q_ref, k_ref, v_ref, sig_ref, o_ref, gated_ref, o_rows = refs[5:13]
+        x_s, xn_s, p_s, low_ref, code_ref, key_ref, g_all, xn_sem, p_sem, part_sem = refs[13:23]
+        sems, block_sems, w_sems, pack_sems, g_sems, moved, local = refs[23:30]
+        cot_sems, out_sems, ff_sems = refs[30:]
         line = Line(n_blk)
-        across = Exchange("head", n_head)
-        h_me, b_me = across.me, line.me
-        greet_all((across,), line)
-        mine = pl.ds(pl.multiple_of(h_me * rows_here, rows_here), rows_here)
+        across, along = Exchange("head", n_head), Exchange("blk", n_blk)
+        h, b = across.me, along.me
+        h_me, b_me = h, b
+        (th, tb), (sh, sb) = place_of_out_rows(n_head, n_blk)
+        stays = (th == h) & (tb == b)
+        moves = jnp.logical_not(stays)
+        greet_all((across, along), moves=(moves, {"head": sh, "blk": sb}))
+
+        def at_rows(head, blk):
+            first = (head * n_blk + blk) * rows_here
+            return pl.ds(pl.multiple_of(first, rows_here), rows_here)
+
+        def of_head(head):
+            size = n_blk * rows_here
+            return pl.ds(pl.multiple_of(head * size, size), size)
+
+        def out_rows_of(head):
+            return o_rows.at[pl.ds(pl.multiple_of(head * rows_here, rows_here), rows_here)]
+
+        def block_copies(k):
+            for w, there, here in weight_pieces(along.peer(k), q_cols, copies):
+                yield along.copy(
+                    k, w_src[w].at[:, there], w_ref.at[at_rows(h, b), here], block_sems.at[w]
+                )
+
+        def pack_copy(k):
+            return along.copy(k, pack_src, g_all.at[h, b], pack_sems)
+
+        def w_copy(k):
+            return across.copy(k, w_ref.at[of_head(h)], w_ref.at[of_head(h)], w_sems)
+
+        def g_copy(k):
+            return across.copy(k, g_all.at[h], g_all.at[h], g_sems)
 
         def out_copy(k):
-            return across.copy(k, moved_hbm, o_rows.at[mine], out_sems)
+            return across.copy(k, out_rows_of(h), out_rows_of(h), out_sems)
 
         def hop(e):
             weight, part, order = entries[e]
@@ -1127,17 +1066,97 @@
                 ff_src[weight].at[part], ff_out[weight].at[part], order[0], ff_sems, e
             )
 
-        own_out = pltpu.make_async_copy(moved_hbm, o_rows.at[mine], own_sem)
+        move_out = pltpu.make_async_remote_copy(
+            src_ref=out_src,
+            dst_ref=out_rows_of(th),
+            send_sem=moved.at[0],
+            recv_sem=moved.at[1],
+            device_id={"head": th, "blk": tb},
+            device_id_type=MESH,
+        )
+        keep_out = pltpu.make_async_copy(out_src, out_rows_of(h), moved.at[2])
+        locals_ = [
+            pltpu.make_async_copy(
+                w_src[w].at[:, there], w_ref.at[at_rows(h, b), here], local.at[w]
+            )
+            for w, there, here in weight_pieces(b, q_cols, copies)
+        ] + [pltpu.make_async_copy(pack_src, g_all.at[h, b], local.at[3])]
+        for k in range(1, n_blk):
+            for copy in block_copies(k):
+                copy.start()
+        tokens = Gather(line, src, Rows(x_s, 0, count, chips), sems)
         gather = Gather(line, cot_ref, cot_hbm, cot_sems)
+        for k in range(1, n_blk):
+            pack_copy(k).start()
+        for one in locals_:
+            one.start()
+
+        @pl.when(stays)
+        def _():
+            keep_out.start()
+
+        @pl.when(moves)
+        def _():
+            move_out.start()
+
+        for e in (2, 3):
+            hop(e).start()
+        half = HEAD_DIM // 2
+        index = lax.broadcasted_iota(jnp.int32, (half, ROWS), 0).astype(F32)
+        frequency = jnp.exp(index * (-2.0 * math.log(ROPE_BASE) / HEAD_DIM))
+        key_ref[...] = (seg[...] * pack + blk_ids[...]).astype(F32)
+
+        def tables(n, carry):
+            r = block_of(n)
+            angles = frequency * pos[:, r].astype(F32)
+            cosine, sine = jnp.cos(angles), jnp.sin(angles)
+            cos_ref[r, :] = jnp.concatenate([cosine, cosine], axis=0).T
+            sin_ref[r, :] = jnp.concatenate([-sine, sine], axis=0).T
+            low_ref[r, :] = jnp.broadcast_to((seg[:, r] * pack).astype(F32), (128, ROWS)).T
+            code_ref[r, :] = jnp.broadcast_to(key_ref[:, r], (128, ROWS)).T
+            return carry
+
+        lax.fori_loop(0, pack // ROWS, tables, 0)
+        for one in locals_:
+            one.wait()
+        for k in range(1, n_blk):
+            pack_copy(k).wait_recv()
+        for k in range(1, n_head):
+            g_copy(k).start()
+        for k in range(1, n_blk):
+            for copy in block_copies(k):
+                copy.wait_recv()
+        tokens.start()
+        for k in range(1, n_head):
+            w_copy(k).start()
+
+        @pl.when(stays)
+        def _():
+            keep_out.wait()
+
+        @pl.when(moves)
+        def _():
+            move_out.wait_recv()
+
         for k in range(1, n_head):
             out_copy(k).start()
-        own_out.start()
+        for s in range(1, chips):
+            tokens.step(s)
         gather.start()
-        for e in range(len(entries)):
+        for e in (0, 1):
             hop(e).start()
-
-        def load(n):
-            return pltpu.make_async_copy(x_hbm.at[block_of(n)], x_s.at[block_of(n)], in_sem.at[n])
+        for k in range(1, n_head):
+            g_copy(k).wait()
+        everyone = [g_all.at[d // n_blk, d % n_blk] for d in range(n_all)]
+        vec_ref[...] = jnp.zeros_like(vec_ref)
+        for t in range(width // 128):
+            tile = sum(one[...] for one in everyone[t * together : (t + 1) * together])
+            vec_ref[0:2, t * 128 : (t + 1) * 128] = tile[0:2]
+            gate_ref[:, t * 128 : (t + 1) * 128] = tile[8:].astype(BF16)
+        vec_ref[2:4, 0:128] = sum(one[2:4, :] for one in everyone)
+        tokens.finish()
+        for k in range(1, n_head):
+            w_copy(k).wait()
 
         def xn_store(n):
             return pltpu.make_async_copy(
@@ -1154,12 +1173,8 @@
                 x_s.at[block_of(n)], part_hbm.at[block_of(n)], part_sem.at[n]
             )
 
-        for n in range(blocks):
-            load(n).start()
-
         def project(n, carry):
             r = block_of(n)
-            load(n).wait()
             unit, _ = unit_of(x_s[r, :].astype(F32))
             xn = (unit * vec_ref[0:1, :]).astype(BF16)
             xn_s[r, :] = xn
@@ -1187,7 +1202,6 @@
 
         lax.fori_loop(0, blocks, project, 0)
         gather.step(1)
-        own_out.wait()
         for k in range(1, n_head):
             out_copy(k).wait_recv()
 
@@ -1221,6 +1235,15 @@
             out_copy(k).wait_send()
         for e in range(len(entries)):
             hop(e).wait()
+        for k in range(1, n_blk):
+            pack_copy(k).wait_send()
+            for copy in block_copies(k):
+                copy.wait_send()
+
+        @pl.when(moves)
+        def _():
+            move_out.wait_send()
+
         for n in range(blocks):
             xn_store(n).wait()
             part_store(n).wait()
@@ -1234,8 +1257,13 @@
             spec_of((pack, width), BF16),
             spec_of((pack, width), BF16),
             spec_of((q_here, pack, pack), BF16),
-            spec_of((chips, 2, count, width), BF16),
+            spec_of((chips, 2, *cot.shape), BF16),
             *(spec_of(w.shape, BF16) for w in ff),
+            spec_of((width, columns), BF16),
+            spec_of((8, width), F32),
+            spec_of((HEADS, width), BF16),
+            spec_of((pack, HEAD_DIM), F32),
+            spec_of((pack, HEAD_DIM), F32),
             spec_of((pack, columns), F32),
             spec_of((pack, q_cols), BF16),
             spec_of((pack, HEAD_DIM), BF16),
@@ -1245,25 +1273,34 @@
             spec_of((pack, q_cols), BF16),
             spec_of((q_cols, width), BF16),
         ),
-        in_specs=[ANYWHERE] * 5 + [IN_VMEM] * 9,
-        out_specs=[ANYWHERE] * 7 + [IN_VMEM] * 8,
+        in_specs=[IN_VMEM] * 2 + [ANYWHERE] * 8 + [IN_VMEM] * 3,
+        out_specs=[ANYWHERE] * 7 + [IN_VMEM] * 13,
         scratch_shapes=[
             pltpu.VMEM((pack, width), BF16),
             pltpu.VMEM((pack, width), BF16),
             pltpu.VMEM((q_here, pack, pack), BF16),
-            dma((blocks,)),
+            pltpu.VMEM((pack, 128), F32),
+            pltpu.VMEM((pack, 128), F32),
+            pltpu.VMEM((1, pack), F32),
+            pltpu.VMEM((n_head, n_blk, PACK_ROWS, 128), F32),
             dma((blocks,)),
             dma((q_here, blocks)),
             dma((blocks,)),
             gather_sems(chips),
+            dma((3, 2, n_blk)),
+            pair_sems(n_head),
+            pair_sems(n_blk),
+            pair_sems(n_head),
+            dma((3,)),
+            dma((4,)),
+            gather_sems(chips),
             pair_sems(n_head),
             pair_sems(len(entries)),
-            dma,
         ],
         compiler_params=local_params(collective_id),
         cost_estimate=comm_cost(pack * width),
         name="attention_forward",
-    )(x_all, out_moved, *ff, cot, w_attn, vec, gates, *tables)
+    )(rows, cot, *weights, small, w_out, *ff, *ids)
 
 
 def attention_backward(
@@ -1457,46 +1494,382 @@
     )(dy, xn, p, *have, *saved, w_attn, vec, gates, *tables, mlp_gain_part)
 
 
-class Rows:
-    def __init__(self, ref, q, size, chips):
-        self.ref, self.base, self.size = ref, q * size * chips * 2, size
-        self.at = self
-
-    def rows(self, j, core, start=0, count=None):
-        first = self.base + (j * 2 + core) * self.size + start
-        return pl.ds(pl.multiple_of(first, 16), count or self.size)
-
-    def __getitem__(self, index):
-        j, core, *inner = index
-        if inner:
-            return self.ref.at[self.rows(j, core, inner[0].start, inner[0].size)]
-        return self.ref.at[self.rows(j, core)]
-
-
-class OwnRows:
-    def __init__(self, rows, core):
-        self.view, self.core = rows, core
-        self.shape = (0, rows.size)
-
-    def __getitem__(self, index):
-        j, r, _ = index
-        return self.view.ref[self.view.rows(j, self.core, r.start, r.size), :]
-
-
-class LocalScatter(Scatter):
-    def __init__(self, line, part, bufs, sems):
-        super().__init__(line, part, (OwnRows(part, line.c), *bufs), sems)
-
-    def start(self):
-        chips = self.line.chips
-        order = []
-        for k in range((chips + 1) // 2):
-            order += [chips - 1 - k, k]
-        for j in order[:chips]:
-            self.to_sibling(j).start()
-
-    def ready(self, j):
-        self.to_sibling(j).wait_recv()
+def attention_end(
+    dy, xn, p, mlp_part, ff_sums, saved, w_attn, vec, gates, tables, token_rows, q_here, copies,
+    n_head, n_blk, collective_id
+):
+    pack, width = dy.shape
+    columns = w_attn.shape[1]
+    q_cols = q_here * HEAD_DIM
+    blocks = pack // ROWS
+    scale = 1.0 / math.sqrt(HEAD_DIM)
+    chips, count = n_blk // 2, pack // n_blk
+    rows_here = width // (n_head * n_blk)
+    lanes = n_blk * rows_here
+    entries = ff_entries(ff_sums[0].shape[1], n_head)
+
+    def kernel(dy_hbm, xn_hbm, p_hbm, mlp_hbm, *refs):
+        refs = list(refs)
+
+        def take(n):
+            taken = refs[:n]
+            del refs[:n]
+            return taken
+
+        ff_src = take(3)
+        lin_ref, q_ref, k_ref, v_ref, sig_ref, o_ref, gated_ref, o_rows = take(8)
+        w_ref, vec_ref, gate_ref, cos_ref, sin_ref = take(5)
+        x_ref, middle_ref, dmid_ref, mlp_gain_ref = take(4)
+        layer_out, input_grad, g_out, wq_out, wk_out, wv_out, o_out = take(7)
+        ff_out = take(3)
+        dy_s, xn_s, p_s, do_s, delta_s, dgate_s, dlin_s, dk_s, dv_s, dgq_s = take(10)
+        dw_s, pack_s, dout_s, w_in, w_sum, o_in, o_sum, g_in, g_sum, g_last = take(10)
+        mlp_scratch, dxn_scratch = take(5), take(4)
+        dy_sem, xn_sem, p_sem = take(3)
+        w_sems, block_sems, o_sems, g_sems, pack_sems, moved, ff_sems, local = refs
+        line = Line(n_blk)
+        across, along = Exchange("head", n_head), Exchange("blk", n_blk)
+        h, b = across.me, along.me
+        first_head = b * q_here
+        (sh, sb), (th, tb) = place_of_out_rows(n_head, n_blk)
+        stays = (th == h) & (tb == b)
+        moves = jnp.logical_not(stays)
+        greet_all((across, along), moves=(moves, {"head": sh, "blk": sb}))
+
+        def dy_load(n):
+            return pltpu.make_async_copy(
+                dy_hbm.at[block_of(n)], dy_s.at[block_of(n)], dy_sem.at[n]
+            )
+
+        def p_load(head, n):
+            return pltpu.make_async_copy(
+                p_hbm.at[head, block_of(n)], p_s.at[head, block_of(n)], p_sem.at[head, n]
+            )
+
+        def of_head(head):
+            return pl.ds(pl.multiple_of(head * lanes, lanes), lanes)
+
+        def of_blk(blk):
+            return pl.ds(pl.multiple_of(blk * rows_here, rows_here), rows_here)
+
+        def out_of(head):
+            return dout_s.at[pl.ds(pl.multiple_of(head * rows_here, rows_here), rows_here)]
+
+        def w_copy(k):
+            return across.copy(k, dw_s.at[of_head(across.peer(k))], w_in.at[k], w_sems)
+
+        def o_copy(k):
+            return across.copy(k, out_of(across.peer(k)), o_in.at[k], o_sems)
+
+        def g_part(head):
+            return pack_s.at[:, pl.ds(pl.multiple_of(head * lanes, 128), lanes)]
+
+        def g_copy(k):
+            return across.copy(k, g_part(across.peer(k)), g_in.at[k], g_sems)
+
+        def landings():
+            kv = pl.ds(pl.multiple_of(b // copies * HEAD_DIM, HEAD_DIM), HEAD_DIM)
+            return (
+                wq_out.at[:, pl.ds(pl.multiple_of(b * q_cols, HEAD_DIM), q_cols)],
+                wk_out.at[b % copies, :, kv],
+                wv_out.at[b % copies, :, kv],
+            )
+
+        spans = (
+            pl.ds(0, q_cols),
+            pl.ds(q_cols, HEAD_DIM),
+            pl.ds(q_cols + HEAD_DIM, HEAD_DIM),
+        )
+
+        def block_copies(k):
+            for w, there in enumerate(landings()):
+                src = w_sum.at[of_blk(along.peer(k)), spans[w]]
+                yield along.copy(k, src, there, block_sems.at[w])
+
+        def tile_of(blk):
+            return pl.ds(pl.multiple_of(blk * rows_here // 128 * 128, 128), 128)
+
+        def pack_copy(k):
+            return along.copy(k, g_sum.at[:, tile_of(along.peer(k))], g_last.at[b], pack_sems)
+
+        move_out = pltpu.make_async_remote_copy(
+            src_ref=o_sum,
+            dst_ref=o_out,
+            send_sem=moved.at[0],
+            recv_sem=moved.at[1],
+            device_id={"head": th, "blk": tb},
+            device_id_type=MESH,
+        )
+        keep_out = pltpu.make_async_copy(o_sum, o_out, moved.at[2])
+        hops = [
+            flip_copy(ff_src[w].at[1, part], ff_out[w].at[part], order[0], ff_sems, e)
+            for e, (w, part, order) in enumerate(entries)
+        ]
+        own_blocks = [
+            pltpu.make_async_copy(w_sum.at[of_blk(b), spans[w]], there, local.at[w])
+            for w, there in enumerate(landings())
+        ]
+        mlp = Scatter(line, mlp_hbm, mlp_scratch[:4], mlp_scratch[4])
+        dxn = LocalScatter(
+            line, Rows(dy_s, 0, count, chips), dxn_scratch[:3], dxn_scratch[3]
+        )
+        xn_load = pltpu.make_async_copy(xn_hbm, xn_s, xn_sem)
+        for n in range(blocks):
+            dy_load(n).start()
+        mlp.start()
+        for n in range(blocks):
+            for head in range(q_here):
+                p_load(head, n).start()
+        xn_load.start()
+        for hop in hops:
+            hop.start()
+
+        def through_gate(n, carry):
+            r = block_of(n)
+            dy_load(n).wait()
+            dgated = mm_nt(dy_s[r, :], o_rows[...])
+            lane = lax.broadcasted_iota(jnp.int32, (ROWS, GATE_PAD), 1)
+            dgates = jnp.zeros((ROWS, GATE_PAD), F32)
+            deltas = jnp.zeros((ROWS, GATE_PAD), F32)
+            for head in range(q_here):
+                at = slice(head * HEAD_DIM, (head + 1) * HEAD_DIM)
+                sig = sig_ref[r, head : head + 1]
+                out = o_ref[r, at].astype(F32)
+                do = (dgated[:, at] * sig).astype(BF16)
+                do_s[r, at] = do
+                dgate = jnp.sum(dgated[:, at] * out, axis=-1, keepdims=True) * sig * (1.0 - sig)
+                delta = jnp.sum(do.astype(F32) * out, axis=-1, keepdims=True)
+                dgates = jnp.where(lane == first_head + head, dgate, dgates)
+                deltas = jnp.where(lane == head, delta, deltas)
+            dgate_s[r, :] = dgates.astype(BF16)
+            delta_s[r, :] = deltas
+            return carry
+
+        lax.fori_loop(0, blocks, through_gate, 0)
+        mlp.step(0)
+
+        def out_grad(n, carry):
+            c = block_of(n)
+            dout_s[:, c] = mm_tn(gated_ref[...], dy_s[:, c]).astype(BF16)
+            return carry
+
+        lax.fori_loop(0, width // ROWS, out_grad, 0)
+        dk_s[...] = jnp.zeros_like(dk_s)
+        dv_s[...] = jnp.zeros_like(dv_s)
+        dgq_s[...] = jnp.zeros_like(dgq_s)
+        o_in[0] = dout_s[pl.ds(pl.multiple_of(h * rows_here, rows_here), rows_here), :]
+        for k in range(1, n_head):
+            o_copy(k).start()
+
+        def into_lin(grad, lin, gain, r):
+            grad = turned(grad.astype(BF16).astype(F32), cos_ref[r, :], -sin_ref[r, :])
+            unit, factor = unit_of(lin)
+            return unit_back(grad * gain, unit, factor).astype(BF16), grad * unit
+
+        def attend(n, carry):
+            r = block_of(n)
+            for head in range(q_here):
+                at = slice(head * HEAD_DIM, (head + 1) * HEAD_DIM)
+                p_load(head, n).wait()
+                do, prob, q = do_s[r, at], p_s[head, r, :], q_ref[r, at]
+                dp = mm_nt(do, v_ref[...])
+                ds = (prob.astype(F32) * (dp - delta_s[r, head : head + 1])).astype(BF16)
+                dq = mm(ds, k_ref[...]) * scale
+                dk_s[...] += mm(q.T, ds)
+                dv_s[...] += mm(do.T, prob)
+                dlin, part = into_lin(dq, lin_ref[r, at], vec_ref[2:3, :HEAD_DIM], r)
+                dlin_s[r, at] = dlin
+                dgq_s[...] += jnp.sum(part.reshape(ROWS // 8, 8, HEAD_DIM), axis=0)
+            return carry
+
+        lax.fori_loop(0, blocks // 2, attend, 0)
+        mlp.step(1)
+        lax.fori_loop(blocks // 2, blocks, attend, 0)
+        every = pl.ds(0, pack)
+        k_cols = slice(q_cols, q_cols + HEAD_DIM)
+        dlin, part = into_lin(
+            dk_s[...].T * scale, lin_ref[:, k_cols], vec_ref[3:4, :HEAD_DIM], every
+        )
+        dlin_s[:, k_cols] = dlin
+        dlin_s[:, q_cols + HEAD_DIM :] = dv_s[...].T.astype(BF16)
+
+        def into_x(n, carry):
+            r = block_of(n)
+            back = mm_nt(dlin_s[r, :], w_ref[...]) + mm(dgate_s[r, :HEADS], gate_ref[...])
+            dy_s[r, :] = back.astype(BF16)
+            return carry
+
+        lax.fori_loop(0, blocks, into_x, 0)
+        dxn.start()
+        for tau in range(2, chips - 1):
+            mlp.step(tau)
+        dxn.step(0)
+        dgk = jnp.sum(part, axis=0, keepdims=True)
+        dgq = jnp.sum(dgq_s[...], axis=0, keepdims=True)
+        pack_s[HEADS:, :] = jnp.zeros((PACK_ROWS - HEADS, width), F32)
+        pack_s[HEADS : HEADS + 1, :] = jnp.sum(mlp_gain_ref[...], axis=0, keepdims=True)
+        for t in range(width // HEAD_DIM):
+            at = slice(t * HEAD_DIM, (t + 1) * HEAD_DIM)
+            pack_s[HEADS + 1 : HEADS + 2, at] = dgq
+            pack_s[HEADS + 2 : HEADS + 3, at] = dgk
+        xn_load.wait()
+        dgate_t = dgate_s[...].astype(F32).T[:HEADS].astype(BF16)
+
+        def weights(n, carry):
+            c = block_of(n)
+            xn_cols = xn_s[:, c]
+            dw_s[c, :] = mm_tn(xn_cols, dlin_s[...]).astype(BF16)
+            pack_s[:HEADS, c] = mm(dgate_t, xn_cols)
+            return carry
+
+        lax.fori_loop(0, width // ROWS, weights, 0)
+        for k in range(1, n_head):
+            w_copy(k).start()
+            g_copy(k).start()
+        w_in[0] = dw_s[of_head(h), :]
+        g_in[0] = pack_s[:, pl.ds(pl.multiple_of(h * lanes, 128), lanes)]
+
+        def finish_layer(r, value):
+            layer_out[r, :] = (middle_ref[r, :] + value).astype(BF16)
+
+        mlp.total(finish_layer)
+        for tau in range(1, chips - 2):
+            dxn.step(tau)
+        for k in range(1, n_head):
+            g_copy(k).wait_recv()
+        g_sum[...] = sum(g_in[k] for k in range(n_head))
+        g_last[b] = g_sum[:, tile_of(b)]
+        for k in range(1, n_blk):
+            pack_copy(k).start()
+        for k in range(1, n_head):
+            o_copy(k).wait_recv()
+
+        def add_out(r):
+            o_sum[r, :] = sum(o_in[k, r, :].astype(F32) for k in range(n_head)).astype(BF16)
+
+        by_rows(rows_here, 16, add_out)
+
+        @pl.when(stays)
+        def _():
+            keep_out.start()
+
+        @pl.when(moves)
+        def _():
+            move_out.start()
+
+        for k in range(1, n_head):
+            w_copy(k).wait_recv()
+
+        def add(r):
+            w_sum[r, :] = sum(w_in[k, r, :].astype(F32) for k in range(n_head)).astype(BF16)
+
+        by_rows(lanes, 64, add)
+        for one in own_blocks:
+            one.start()
+        for k in range(1, n_blk):
+            for copy in block_copies(k):
+                copy.start()
+        dxn.step(chips - 2)
+
+        def consume(r, value):
+            unit, factor = unit_of(x_ref[r, :].astype(F32))
+            back = unit_back(value * vec_ref[0:1, :], unit, factor)
+            input_grad[r, :] = dmid_ref[r, :] + back
+
+        dxn.total(consume)
+        for k in range(1, n_blk):
+            pack_copy(k).wait_recv()
+        g_out[...] = sum(g_last[k] for k in range(n_blk))
+        mlp.finish()
+        dxn.finish()
+        for one in own_blocks:
+            one.wait()
+        for k in range(1, n_head):
+            g_copy(k).wait_send()
+            o_copy(k).wait_send()
+            w_copy(k).wait_send()
+        for k in range(1, n_blk):
+            pack_copy(k).wait_send()
+            for copy in block_copies(k):
+                copy.wait()
+        for hop in hops:
+            hop.wait()
+
+        @pl.when(stays)
+        def _():
+            keep_out.wait()
+
+        @pl.when(moves)
+        def _():
+            move_out.wait()
+
+    dma = pltpu.SemaphoreType.DMA
+    kv = spec_of((copies, rows_here, n_blk // copies * HEAD_DIM), BF16)
+    return pl.pallas_call(
+        kernel,
+        out_shape=(
+            spec_of((count, width), BF16),
+            spec_of((count, width), F32),
+            spec_of((PACK_ROWS, 128), F32),
+            spec_of((rows_here, n_blk * q_cols), BF16),
+            kv,
+            kv,
+            spec_of((rows_here, width), BF16),
+            *(spec_of(one.shape[1:], BF16) for one in ff_sums),
+        ),
+        in_specs=[ANYWHERE] * 7 + [IN_VMEM] * 17,
+        out_specs=[IN_VMEM] * 3 + [ANYWHERE] * 7,
+        scratch_shapes=[
+            pltpu.VMEM((pack, width), BF16),
+            pltpu.VMEM((pack, width), BF16),
+            pltpu.VMEM((q_here, pack, pack), BF16),
+            pltpu.VMEM((pack, q_cols), BF16),
+            pltpu.VMEM((pack, GATE_PAD), F32),
+            pltpu.VMEM((pack, GATE_PAD), BF16),
+            pltpu.VMEM((pack, columns), BF16),
+            pltpu.VMEM((HEAD_DIM, pack), F32),
+            pltpu.VMEM((HEAD_DIM, pack), F32),
+            pltpu.VMEM((8, HEAD_DIM), F32),
+            pltpu.VMEM((width, columns), BF16),
+            pltpu.VMEM((PACK_ROWS, width), F32),
+            pltpu.VMEM((q_cols, width), BF16),
+            pltpu.VMEM((n_head, lanes, columns), BF16),
+            pltpu.VMEM((lanes, columns), BF16),
+            pltpu.VMEM((n_head, rows_here, width), BF16),
+            pltpu.VMEM((rows_here, width), BF16),
+            pltpu.VMEM((n_head, PACK_ROWS, lanes), F32),
+            pltpu.VMEM((PACK_ROWS, lanes), F32),
+            pltpu.VMEM((n_blk, PACK_ROWS, 128), F32),
+            *scatter_bufs(chips, count, width),
+            *scatter_bufs(chips, count, width)[1:],
+            dma((blocks,)),
+            dma,
+            dma((q_here, blocks)),
+            pair_sems(n_head),
+            dma((3, 2, n_blk)),
+            pair_sems(n_head),
+            pair_sems(n_head),
+            pair_sems(n_blk),
+            dma((3,)),
+            pair_sems(len(entries)),
+            dma((3,)),
+        ],
+        compiler_params=local_params(collective_id),
+        cost_estimate=comm_cost(2 * pack * width),
+        name="attention_end",
+    )(
+        dy,
+        xn,
+        p,
+        mlp_part.reshape(chips, 2, count, width),
+        *ff_sums,
+        *saved,
+        w_attn,
+        vec,
+        gates,
+        *tables,
+        *token_rows,
+    )
 
 
 def feed_forward(attn_part, ff, halfway, cot, inputs, to_mlp, to_attention, n_head, n_blk, collective_id):
@@ -1522,7 +1895,7 @@
         made, hn_s, cot_s, dhn_s, u_s, da_s, db_s, stage = take(8)
         inboxes, weights = take(3), take(3)
         chunk_scratch = [take(8) for _ in range(CHUNKS)]
-        load_sems, hop_sems, cot_sems, stage_sems, sum_sems, grad_sems = refs
+        load_sems, hop_sems, cot_sems, stage_sems, sum_sems, grad_sems, late_sems = refs
         line = Line(n_blk)
         across = Exchange("head", n_head)
         greet_all((across,), line)
@@ -1542,13 +1915,13 @@
                 there = weights[w].at[place(key ^ second, span)]
                 hops.append(flip_copy(src, there, order[1], hop_sems, e, at))
 
-        def cot_loads(q):
+        def cot_loads():
             for j in range(chips):
                 for c in range(2):
                     yield pltpu.make_async_copy(
-                        cot_hbm.at[j, c, pl.ds(q * size, size)],
-                        Rows(cot_s, q, size, chips)[j, c],
-                        cot_sems.at[q, 2 * j + c],
+                        cot_hbm.at[j, c],
+                        Rows(cot_s, 0, size, chips)[j, c],
+                        cot_sems.at[2 * j + c],
                     )
 
         first, gather1, second, gather2 = [], [], [], []
@@ -1561,6 +1934,16 @@
                 LocalScatter(line, Rows(dhn_s, q, size, chips), (sib, inn, outgoing), sems2)
             )
             gather2.append(Gather(line, made.at[rows], View(dy_hbm, rows), g_sems2))
+
+        late = [
+            Gather(
+                line,
+                ins[1].at[pl.ds(q * size, size)],
+                Rows(cot_s, q, size, chips),
+                late_sems.at[q - 1],
+            )
+            for q in range(1, CHUNKS)
+        ]
 
         def turn(q, scatter, between, outs, gather):
             def consume(r, value):
@@ -1680,14 +2063,17 @@
             hop.start()
         for q in range(1, CHUNKS):
             first[q].start()
+        for one in late:
+            one.start()
         for load in loads:
             load.start()
-        for q in range(CHUNKS):
-            for load in cot_loads(q):
-                load.start()
+        for load in cot_loads():
+            load.start()
         steps = chips - 1
         for tau in range(steps):
             first[0].step(tau)
+            for one in late:
+                one.step(tau + 1)
         turn(0, first, to_mlp, (middle,), gather1)
         for tau in range(steps):
             first[1].step(tau)
@@ -1699,7 +2085,7 @@
         gather1[1].step(1)
         for load in loads:
             load.wait()
-        for load in cot_loads(0):
+        for load in cot_loads():
             load.wait()
         for hop in hops:
             hop.wait()
@@ -1714,8 +2100,8 @@
         back(0)
         second[0].start()
         gather1[1].finish()
-        for load in cot_loads(1):
-            load.wait()
+        for one in late:
+            one.finish()
         second[0].step(0)
         loop(blocks, lambda f: unit_block(1, f))
         second[0].step(1)
@@ -1779,10 +2165,11 @@
             *per_chunk,
             dma((len(entries), 2)),
             dma((2, len(entries), 2)),
-            dma((CHUNKS, n_blk)),
+            dma((n_blk,)),
             dma((n_blk,)),
             dma((2, len(entries), 2)),
             dma((len(entries), 2)),
+            dma((CHUNKS - 1, 7, chips, PIECES)),
         ],
         compiler_params=pltpu.CompilerParams(
             collective_id=collective_id, has_side_effects=True, vmem_limit_bytes=62 * 2**20
@@ -1791,7 +2178,7 @@
         name="feed_forward",
     )(
         attn_part.reshape(chips, 2, count, width),
-        cot.reshape(chips, 2, count, width),
+        cot,
         *ff,
         *halfway,
         *inputs,
@@ -1863,23 +2250,23 @@
     ids = [
         lax.dynamic_slice_in_dim(ids_, my_head, 1, 0) for ids_ in (positions, segment_ids, block_ids)
     ]
-    x_all, w_attn, out_moved, vec, gates, *tables = first_gather(
+    fused = n_head == 4 and pack <= 1024
+    ff = (w_gate, w_up, w_down)
+    attn_part, xn, prob, cot, *rest = attention_forward(
         hidden[0],
         (w_query, key_weight_matrix, value_weight_matrix),
         small,
         w_out,
         ids,
+        cotangent[0, : tokens // CHUNKS] if fused else cotangent[0],
+        ff,
         q_cols,
         kv_copies,
         n_head,
         n_blk,
         0,
     )
-    ff = (w_gate, w_up, w_down)
-    attn_part, xn, prob, cot, *rest = attention_forward(
-        x_all, w_attn, vec, gates, tables, out_moved, cotangent[0], ff, q_here, n_head, n_blk, 4
-    )
-    halfway, saved = rest[:3], rest[3:]
+    halfway, (w_attn, vec, gates), tables, saved = rest[:3], rest[3:6], rest[6:8], rest[8:]
 
     def to_mlp(r, total, ins, outs):
         x_ref, gain_ref = ins
@@ -1898,7 +2285,6 @@
         outs[0][r, :] = back
         return back
 
-    fused = n_head == 4 and pack <= 1024
     if fused:
 
         def into_mlp(r, total, ins, outs):
@@ -1974,38 +2360,60 @@
             2,
         )
 
-    layer_output = (
-        middle + lax.psum_scatter(mlp_part, "blk", scatter_dimension=0, tiled=True).astype(F32)
-    ).astype(BF16)[None]
-    dxn_part, attn_grad, small_parts, out_grad, *ff_last = attention_backward(
-        dy,
-        xn,
-        prob,
-        saved,
-        w_attn,
-        vec,
-        gates,
-        tables[:2],
-        mlp_gain_part,
-        q_here,
-        (ff_sums, n_head, 2) if fused else None,
-    )
-    back_x, query_grad, key_grad, value_grad, out_grad, small_sums, *ff_rest = last_scatter(
-        dxn_part,
-        attn_grad.reshape(n_head, n_blk, rows_here, -1),
-        out_grad,
-        small_parts,
-        () if fused else ff_sums,
-        hidden[0],
-        vec,
-        q_cols,
-        kv_copies,
-        n_head,
-        n_blk,
-        3,
-    )
-    ff_last = ff_last or ff_rest
-    input_grad = (dmid + back_x)[None]
+    if fused:
+        layer_output, input_grad, small_sums, query_grad, key_grad, value_grad, out_grad, *ff_last = (
+            attention_end(
+                dy,
+                xn,
+                prob,
+                mlp_part,
+                ff_sums,
+                saved,
+                w_attn,
+                vec,
+                gates,
+                tables,
+                (hidden[0], middle, dmid, mlp_gain_part),
+                q_here,
+                kv_copies,
+                n_head,
+                n_blk,
+                2,
+            )
+        )
+        layer_output, input_grad = layer_output[None], input_grad[None]
+    else:
+        layer_output = (
+            middle + lax.psum_scatter(mlp_part, "blk", scatter_dimension=0, tiled=True).astype(F32)
+        ).astype(BF16)[None]
+        dxn_part, attn_grad, small_parts, out_grad = attention_backward(
+            dy,
+            xn,
+            prob,
+            saved,
+            w_attn,
+            vec,
+            gates,
+            tables,
+            mlp_gain_part,
+            q_here,
+            None,
+        )
+        back_x, query_grad, key_grad, value_grad, out_grad, small_sums, *ff_last = last_scatter(
+            dxn_part,
+            attn_grad.reshape(n_head, n_blk, rows_here, -1),
+            out_grad,
+            small_parts,
+            ff_sums,
+            hidden[0],
+            vec,
+            q_cols,
+            kv_copies,
+            n_head,
+            n_blk,
+            3,
+        )
+        input_grad = (dmid + back_x)[None]
     ff_grads = [one[0].astype(F32) + two.astype(F32) for one, two in zip(ff_sums, ff_last)]
 
     query_grad = query_grad.astype(F32)

time: 421 us -> 383 us (0.910)
  Pallas kernels: 373 us -> 356 us
  between operations: 14.3 us -> 0.88 us
  other arithmetic: 16.9 us -> 11.5 us
    pallas_call x3 -> x1, Pallas kernels: 167 us -> 106 us  [attention_end(): pl.pallas_call(kernel, out_shape=(spec_of((count, width), BF16), spec_of(...]
    pallas_call x1, Pallas kernels: 49.3 us -> 88.1 us  [attention_forward(): pl.pallas_call(kernel, out_shape=(spec_of((pack, width), BF16), spec_of((...]
    pallas_call x1, Pallas kernels: 157 us -> 162 us  [feed_forward(): pl.pallas_call(kernel, out_shape=(jax.ShapeDtypeStruct((count, width), F3...]
  transfers between devices with their start and end apart: 1 -> 0, of which waited for: 0 -> 0; matrix products, arithmetic and copies ran while one was open for 4% -> 0% of each run, Pallas kernels for 24% -> 0%
where the time goes in v2:
time: 383 us; the launch traced here: 378 us
  Pallas kernels  356 us (93%)
  other arithmetic  11.5 us (3%)
  local copies, waits for them, and re-layouts  9.74 us (3%)
    pallas_call x1, Pallas kernels, feed_forward(): pl.pallas_call(kernel, out_shape=(jax.ShapeDtypeStruct((count, width), F3...  162 us
    pallas_call x1, Pallas kernels, attention_end(): pl.pallas_call(kernel, out_shape=(spec_of((count, width), BF16), spec_of(...  106 us
    pallas_call x1, Pallas kernels, attention_forward(): pl.pallas_call(kernel, out_shape=(spec_of((pack, width), BF16), spec_of((...  88.1 us

profile of v2, /device:TPU:16, one launch (start us, length us, event | category | flops | bytes accessed | tf_op | source)
XLA Modules:
  0.0 378.3 jit_solution(17676255442910948694)
XLA Ops:
  0.8 0.6 copy-done
  1.4 0.6 constant_dynamic-slice_fusion.3.refs_8_
  2.0 0.8 pad_maximum_fusion
  2.8 0.1 tile.9
  2.8 1.3 constant_dynamic-slice_fusion.1
  4.2 0.7 tile.10
  4.8 0.1 stack_tile.6
  5.0 0.7 tile.11
  5.6 0.1 stack_tile.7
  5.7 0.6 pad_add_fusion.refs_3_
  6.4 1.7 slice_bitcast_fusion.cot_ref
  8.0 88.1 %attention_forward.1 = (bf16[1024,2048]{1,0:T(8,128)(2,1)}, bf16[1024,2048]{1,0:T(8,128)(2,1)}, bf16[2,1024,1024]{2,1,0:T(8,128)(2,1)}, bf16[4,2,64,2048]{3,2,1,...) custom-call(bf16[128,2048]{1,0:T(8,128)(2,1)} %bitcast.37, ...), custom_call_target="tpu_custom_call" | custom-call | bytes 83886080 | tf_op jit(solution)/shard_map/attention_forward/pallas_call | solution.py:1254
  96.2 162.0 %feed_forward.1 = (f32[128,2048]{1,0:T(8,128)}, f32[128,2048]{1,0:T(8,128)}, f32[8,2048]{1,0:T(8,128)}, bf16[4,2,128,2048]{3,2,1,0:T(8,128)(2,1)}, bf16[4,2,128,...) custom-call(bf16[4,2,128,2048]{3,2,1,0:T(8,128)(2,1)} %bitcast.40, ...), custom_call_target="tpu_custom_call" | custom-call | bytes 167772160 | tf_op jit(solution)/shard_map/feed_forward/pallas_call | solution.py:2146
  258.2 106.1 %attention_end.1 = (bf16[128,2048]{1,0:T(8,128)(2,1)}, f32[128,2048]{1,0:T(8,128)}, f32[24,128]{1,0:T(8,128)}, bf16[64,2048]{1,0:T(8,128)(2,1)}, bf16[1,64,1024]...) custom-call(bf16[1024,2048]{1,0:T(8,128)(2,1)} %bitcast.41, ...), custom_call_target="tpu_custom_call" | custom-call | bytes 167772160 | tf_op jit(solution)/shard_map/attention_end/pallas_call | solution.py:1808
  364.3 2.7 convert_add_fusion
  367.0 1.4 convert_add_fusion.1
  368.3 0.6 copy-done.1
  368.9 0.2 copy-done.6
  369.2 1.4 convert_add_fusion.2
  370.6 0.1 constant_dynamic-slice_fusion
  370.7 0.5 slice_bitcast_fusion.3
  371.2 0.1 reshape.74
  371.3 0.1 select_reduce_fusion
  371.4 0.5 slice_bitcast_fusion.2
  371.9 0.6 multiply_reduce_fusion.3
  372.5 0.8 multiply_reduce_fusion.2
  373.4 0.8 multiply_reduce_fusion.1
  374.2 0.8 convert_element_type.70
  375.1 1.0 multiply_reduce_fusion
  376.0 0.5 convert_divide_fusion
  376.6 0.8 copy.33
  377.4 1.0 copy.34
  (40 shorter events, 0.2 us)
Async XLA Ops:
  0.6 0.7 copy-start
  258.2 106.1 %copy-start.3 = (bf16[2,192,2048]{2,1,0:T(8,128)(2,1)S(1)}, bf16[2,192,2048]{2,1,0:T(8,128)(2,1)}, u32[]{:S(2)}) copy-start(bf16[2,192,2048]{2,1,0:T(8,128)(2,1)} %get-tuple-element.64.refs_2_) | copy-start | bytes 4718596
  364.3 2.7 copy-start.2
  364.3 2.7 copy-start.7
  367.0 2.0 copy-start.1
  367.0 2.2 copy-start.6
  369.1 1.4 copy-start.16
  369.1 2.7 copy-start.15
  369.1 3.4 copy-start.8
  369.1 3.4 copy-start.14
  369.1 4.2 %copy-start.9 = (bf16[64,1024]{1,0:T(8,128)(2,1)S(1)}, bf16[64,1024]{1,0:T(8,128)(2,1)}, u32[]{:S(2)}) copy-start(bf16[64,1024]{1,0:T(8,128)(2,1)} %refs_2_.2) | copy-start | bytes 393220
  369.2 4.2 %copy-start.13 = (bf16[1,64,1024]{2,1,0:T(8,128)(2,1)S(1)}, bf16[1,64,1024]{2,1,0:T(8,128)(2,1)}, u32[]{:S(2)}) copy-start(bf16[1,64,1024]{2,1,0:T(8,128)(2,1)} %get-tuple-element.84) | copy-start | bytes 393220
  369.2 5.0 %copy-start.11 = (bf16[64,2048]{1,0:T(8,128)(2,1)S(1)}, bf16[64,2048]{1,0:T(8,128)(2,1)}, u32[]{:S(2)}) copy-start(bf16[64,2048]{1,0:T(8,128)(2,1)} %get-tuple-element.86) | copy-start | bytes 786436
  370.5 4.5 %copy-start.5 = (bf16[64,2048]{1,0:T(8,128)(2,1)S(1)}, bf16[64,2048]{1,0:T(8,128)(2,1)}, u32[]{:S(2)}) copy-start(bf16[64,2048]{1,0:T(8,128)(2,1)} %refs_0_.2) | copy-start | bytes 786436
  370.5 4.5 %copy-start.12 = (bf16[64,2048]{1,0:T(8,128)(2,1)S(1)}, bf16[64,2048]{1,0:T(8,128)(2,1)}, u32[]{:S(2)}) copy-start(bf16[64,2048]{1,0:T(8,128)(2,1)} %get-tuple-element.82) | copy-start | bytes 786436
  370.5 5.5 %copy-start.17 = (bf16[64]{0:T(256)(128)(2,1)S(1)}, bf16[64]{0:T(256)(128)(2,1)}, u32[]{:S(2)}) copy-start(bf16[64]{0:T(256)(128)(2,1)} %param.21) | copy-start | bytes 388
  370.6 6.0 %copy-start.10 = (bf16[128,2048]{1,0:T(8,128)(2,1)S(1)}, bf16[128,2048]{1,0:T(8,128)(2,1)}, u32[]{:S(2)}) copy-start(bf16[128,2048]{1,0:T(8,128)(2,1)} %get-tuple-element.80) | copy-start | bytes 1572868
  374.2 3.2 copy-start.4

commit v3 on v2

--- a/solution.py
+++ b/solution.py
@@ -1001,7 +1001,7 @@
 
 
 def attention_forward(
-    rows, weights, small, w_out, ids, cot, ff, q_cols, copies, n_head, n_blk, collective_id
+    rows, weights, small, w_out, ids, cot, cot_rows, ff, q_cols, copies, n_head, n_blk, collective_id
 ):
     count, width = rows.shape
     chips, pack = n_blk // 2, n_blk * count
@@ -1085,7 +1085,7 @@
             for copy in block_copies(k):
                 copy.start()
         tokens = Gather(line, src, Rows(x_s, 0, count, chips), sems)
-        gather = Gather(line, cot_ref, cot_hbm, cot_sems)
+        gather = Gather(line, cot_ref.at[pl.ds(0, cot_rows)], cot_hbm, cot_sems)
         for k in range(1, n_blk):
             pack_copy(k).start()
         for one in locals_:
@@ -1104,15 +1104,16 @@
         half = HEAD_DIM // 2
         index = lax.broadcasted_iota(jnp.int32, (half, ROWS), 0).astype(F32)
         frequency = jnp.exp(index * (-2.0 * math.log(ROPE_BASE) / HEAD_DIM))
-        key_ref[...] = (seg[...] * pack + blk_ids[...]).astype(F32)
+        pack_row = pl.ds(h, 1)
+        key_ref[...] = (seg[pack_row, :] * pack + blk_ids[pack_row, :]).astype(F32)
 
         def tables(n, carry):
             r = block_of(n)
-            angles = frequency * pos[:, r].astype(F32)
+            angles = frequency * pos[pack_row, r].astype(F32)
             cosine, sine = jnp.cos(angles), jnp.sin(angles)
             cos_ref[r, :] = jnp.concatenate([cosine, cosine], axis=0).T
             sin_ref[r, :] = jnp.concatenate([-sine, sine], axis=0).T
-            low_ref[r, :] = jnp.broadcast_to((seg[:, r] * pack).astype(F32), (128, ROWS)).T
+            low_ref[r, :] = jnp.broadcast_to((seg[pack_row, r] * pack).astype(F32), (128, ROWS)).T
             code_ref[r, :] = jnp.broadcast_to(key_ref[:, r], (128, ROWS)).T
             return carry
 
@@ -1257,7 +1258,7 @@
             spec_of((pack, width), BF16),
             spec_of((pack, width), BF16),
             spec_of((q_here, pack, pack), BF16),
-            spec_of((chips, 2, *cot.shape), BF16),
+            spec_of((chips, 2, cot_rows, width), BF16),
             *(spec_of(w.shape, BF16) for w in ff),
             spec_of((width, columns), BF16),
             spec_of((8, width), F32),
@@ -1524,7 +1525,7 @@
         ff_out = take(3)
         dy_s, xn_s, p_s, do_s, delta_s, dgate_s, dlin_s, dk_s, dv_s, dgq_s = take(10)
         dw_s, pack_s, dout_s, w_in, w_sum, o_in, o_sum, g_in, g_sum, g_last = take(10)
-        mlp_scratch, dxn_scratch = take(5), take(4)
+        mlp_scratch, dxn_scratch, (xg_s,) = take(5), take(4), take(1)
         dy_sem, xn_sem, p_sem = take(3)
         w_sems, block_sems, o_sems, g_sems, pack_sems, moved, ff_sems, local = refs
         line = Line(n_blk)
@@ -1621,7 +1622,7 @@
             for head in range(q_here):
                 p_load(head, n).start()
         xn_load.start()
-        for hop in hops:
+        for hop in hops[2:]:
             hop.start()
 
         def through_gate(n, carry):
@@ -1645,8 +1646,9 @@
             delta_s[r, :] = deltas
             return carry
 
-        lax.fori_loop(0, blocks, through_gate, 0)
+        lax.fori_loop(0, blocks // 2, through_gate, 0)
         mlp.step(0)
+        lax.fori_loop(blocks // 2, blocks, through_gate, 0)
 
         def out_grad(n, carry):
             c = block_of(n)
@@ -1657,6 +1659,7 @@
         dk_s[...] = jnp.zeros_like(dk_s)
         dv_s[...] = jnp.zeros_like(dv_s)
         dgq_s[...] = jnp.zeros_like(dgq_s)
+        xg_s[...] = jnp.zeros_like(xg_s)
         o_in[0] = dout_s[pl.ds(pl.multiple_of(h * rows_here, rows_here), rows_here), :]
         for k in range(1, n_head):
             o_copy(k).start()
@@ -1693,17 +1696,6 @@
         dlin_s[:, k_cols] = dlin
         dlin_s[:, q_cols + HEAD_DIM :] = dv_s[...].T.astype(BF16)
 
-        def into_x(n, carry):
-            r = block_of(n)
-            back = mm_nt(dlin_s[r, :], w_ref[...]) + mm(dgate_s[r, :HEADS], gate_ref[...])
-            dy_s[r, :] = back.astype(BF16)
-            return carry
-
-        lax.fori_loop(0, blocks, into_x, 0)
-        dxn.start()
-        for tau in range(2, chips - 1):
-            mlp.step(tau)
-        dxn.step(0)
         dgk = jnp.sum(part, axis=0, keepdims=True)
         dgq = jnp.sum(dgq_s[...], axis=0, keepdims=True)
         pack_s[HEADS:, :] = jnp.zeros((PACK_ROWS - HEADS, width), F32)
@@ -1725,10 +1717,27 @@
         lax.fori_loop(0, width // ROWS, weights, 0)
         for k in range(1, n_head):
             w_copy(k).start()
+        w_in[0] = dw_s[of_head(h), :]
+
+        def into_x(n, carry):
+            r = block_of(n)
+            back = mm_nt(dlin_s[r, :], w_ref[...]) + mm(dgate_s[r, :HEADS], gate_ref[...])
+            dy_s[r, :] = back.astype(BF16)
+            product = back * xn_s[r, :].astype(F32)
+            xg_s[...] += jnp.sum(product.reshape(ROWS // 8, 8, width), axis=0)
+            return carry
+
+        lax.fori_loop(0, blocks, into_x, 0)
+        dxn.start()
+        pack_s[HEADS + 3 : HEADS + 4, :] = jnp.sum(xg_s[...], axis=0, keepdims=True)
+        for k in range(1, n_head):
             g_copy(k).start()
-        w_in[0] = dw_s[of_head(h), :]
+        for hop in hops[:2]:
+            hop.start()
         g_in[0] = pack_s[:, pl.ds(pl.multiple_of(h * lanes, 128), lanes)]
-
+        for tau in range(2, chips - 1):
+            mlp.step(tau)
+        dxn.step(0)
         def finish_layer(r, value):
             layer_out[r, :] = (middle_ref[r, :] + value).astype(BF16)
 
@@ -1842,6 +1851,7 @@
             pltpu.VMEM((n_blk, PACK_ROWS, 128), F32),
             *scatter_bufs(chips, count, width),
             *scatter_bufs(chips, count, width)[1:],
+            pltpu.VMEM((8, width), F32),
             dma((blocks,)),
             dma,
             dma((q_here, blocks)),
@@ -2247,9 +2257,7 @@
     head_gains = jnp.stack([jnp.tile(q_gain, n_all), jnp.tile(k_gain, n_all)]).astype(F32)
     head_gains = jnp.where(lane // share == device, head_gains, 0)
     small = small + jnp.pad(head_gains, ((2, PACK_ROWS - 4), (0, 0)))
-    ids = [
-        lax.dynamic_slice_in_dim(ids_, my_head, 1, 0) for ids_ in (positions, segment_ids, block_ids)
-    ]
+    ids = (positions, segment_ids, block_ids)
     fused = n_head == 4 and pack <= 1024
     ff = (w_gate, w_up, w_down)
     attn_part, xn, prob, cot, *rest = attention_forward(
@@ -2258,7 +2266,8 @@
         small,
         w_out,
         ids,
-        cotangent[0, : tokens // CHUNKS] if fused else cotangent[0],
+        cotangent[0],
+        tokens // CHUNKS if fused else tokens,
         ff,
         q_cols,
         kv_copies,
@@ -2430,12 +2439,16 @@
     small_sums, head_sums = small_sums
     head_sums = lax.dynamic_slice_in_dim(head_sums, device * share, share, 1)
     head_gate_grad = small_sums[:HEADS].T
-    attn_gain_grad = (
-        jnp.sum(w_query.astype(F32) * query_grad, axis=1)
-        + jnp.sum(key_weight_matrix.astype(F32) * key_grad, axis=1)
-        + jnp.sum(value_weight_matrix.astype(F32) * value_grad, axis=1)
-        + jnp.sum(w_head_gate.astype(F32) * head_gate_grad, axis=1)
-    ) / attn_gain.astype(F32)
+    if fused:
+        scaled = small_sums[HEADS + 3]
+    else:
+        scaled = (
+            jnp.sum(w_query.astype(F32) * query_grad, axis=1)
+            + jnp.sum(key_weight_matrix.astype(F32) * key_grad, axis=1)
+            + jnp.sum(value_weight_matrix.astype(F32) * value_grad, axis=1)
+            + jnp.sum(w_head_gate.astype(F32) * head_gate_grad, axis=1)
+        )
+    attn_gain_grad = scaled / attn_gain.astype(F32)
     return (
         layer_output,
         input_grad,

time: 383 us -> 381 us (level)
  Pallas kernels: 356 us -> 361 us
  local copies, waits for them, and re-layouts: 9.74 us -> 5.32 us
where the time goes in v3:
time: 381 us; the launch traced here: 378 us
  Pallas kernels  361 us (95%)
  other arithmetic  10.8 us (3%)
  local copies, waits for them, and re-layouts  5.32 us (1%)
    pallas_call x1, Pallas kernels, feed_forward(): pl.pallas_call(kernel, out_shape=(jax.ShapeDtypeStruct((count, width), F3...  166 us
    pallas_call x1, Pallas kernels, attention_end(): pl.pallas_call(kernel, out_shape=(spec_of((count, width), BF16), spec_of(...  107 us
    pallas_call x1, Pallas kernels, attention_forward(): pl.pallas_call(kernel, out_shape=(spec_of((pack, width), BF16), spec_of((...  88.2 us

profile of v3, /device:TPU:16, one launch (start us, length us, event | category | flops | bytes accessed | tf_op | source)
XLA Modules:
  0.0 378.0 jit_solution(11647502533442545030)
XLA Ops:
  0.7 0.1 pad.9.clone
  0.8 0.8 pad_maximum_fusion
  1.6 0.1 tile.9
  1.7 0.7 tile.10
  2.3 0.1 stack_tile.6
  2.4 0.7 tile.11
  3.1 0.1 stack_tile.7
  3.2 0.6 pad_add_fusion.refs_3_
  3.8 88.2 %attention_forward.1 = (bf16[1024,2048]{1,0:T(8,128)(2,1)}, bf16[1024,2048]{1,0:T(8,128)(2,1)}, bf16[2,1024,1024]{2,1,0:T(8,128)(2,1)}, bf16[4,2,64,2048]{3,2,1,...) custom-call(bf16[128,2048]{1,0:T(8,128)(2,1)} %bitcast.36, ...), custom_call_target="tpu_custom_call" | custom-call | bytes 83886080 | tf_op jit(solution)/shard_map/attention_forward/pallas_call | solution.py:1255
  92.0 165.8 %feed_forward.1 = (f32[128,2048]{1,0:T(8,128)}, f32[128,2048]{1,0:T(8,128)}, f32[8,2048]{1,0:T(8,128)}, bf16[4,2,128,2048]{3,2,1,0:T(8,128)(2,1)}, bf16[4,2,128,...) custom-call(bf16[4,2,128,2048]{3,2,1,0:T(8,128)(2,1)} %bitcast.39, ...), custom_call_target="tpu_custom_call" | custom-call | bytes 167772160 | tf_op jit(solution)/shard_map/feed_forward/pallas_call | solution.py:2156
  257.8 0.0 copy-start.2
  257.8 106.9 %attention_end.1 = (bf16[128,2048]{1,0:T(8,128)(2,1)}, f32[128,2048]{1,0:T(8,128)}, f32[24,128]{1,0:T(8,128)}, bf16[64,2048]{1,0:T(8,128)(2,1)}, bf16[1,64,1024]...) custom-call(bf16[1024,2048]{1,0:T(8,128)(2,1)} %bitcast.40, ...), custom_call_target="tpu_custom_call" | custom-call | bytes 167772160 | tf_op jit(solution)/shard_map/attention_end/pallas_call | solution.py:1817
  364.7 0.0 copy-done.2
  364.7 0.0 copy-start
  364.8 0.0 copy-start.1
  364.8 2.7 convert_add_fusion.2
  367.4 0.0 copy-done
  367.4 0.0 copy-done.1
  367.5 3.7 convert_add_fusion
  371.1 0.1 constant_dynamic-slice_fusion
  371.2 0.5 slice_bitcast_fusion.3
  371.7 0.1 reshape.74
  371.8 0.1 select_reduce_fusion
  371.9 0.5 slice_bitcast_fusion.1
  372.4 0.5 fusion.2
  373.0 0.6 slice_bitcast_fusion
  373.6 0.0 copy-done.6
  373.6 0.8 convert_element_type.53
  374.4 0.8 convert_element_type.54
  375.2 0.8 bitcast_convert_fusion
  376.1 0.8 copy.33
  376.9 1.0 copy.34
  (22 shorter events, 0.1 us)
Async XLA Ops:
  257.8 106.9 %copy-start.2 = (bf16[2,192,2048]{2,1,0:T(8,128)(2,1)S(1)}, bf16[2,192,2048]{2,1,0:T(8,128)(2,1)}, u32[]{:S(2)}) copy-start(bf16[2,192,2048]{2,1,0:T(8,128)(2,1)} %get-tuple-element.62.refs_0_) | copy-start | bytes 4718596
  364.7 2.7 copy-start
  364.8 2.7 copy-start.1
  367.4 3.7 copy-start.9
  367.4 5.0 %copy-start.10 = (bf16[64]{0:T(256)(128)(2,1)S(1)}, bf16[64]{0:T(256)(128)(2,1)}, u32[]{:S(2)}) copy-start(bf16[64]{0:T(256)(128)(2,1)} %param.21) | copy-start | bytes 388
  367.4 6.1 %copy-start.6 = (bf16[64,2048]{1,0:T(8,128)(2,1)S(1)}, bf16[64,2048]{1,0:T(8,128)(2,1)}, u32[]{:S(2)}) copy-start(bf16[64,2048]{1,0:T(8,128)(2,1)} %get-tuple-element.83) | copy-start | bytes 786436
  367.4 7.0 %copy-start.5 = (bf16[64,2048]{1,0:T(8,128)(2,1)S(1)}, bf16[64,2048]{1,0:T(8,128)(2,1)}, u32[]{:S(2)}) copy-start(bf16[64,2048]{1,0:T(8,128)(2,1)} %get-tuple-element.86) | copy-start | bytes 786436
  371.1 4.1 %copy-start.7 = (bf16[1,64,1024]{2,1,0:T(8,128)(2,1)S(1)}, bf16[1,64,1024]{2,1,0:T(8,128)(2,1)}, u32[]{:S(2)}) copy-start(bf16[1,64,1024]{2,1,0:T(8,128)(2,1)} %get-tuple-element.84) | copy-start | bytes 393220
  371.1 4.1 %copy-start.8 = (bf16[1,64,1024]{2,1,0:T(8,128)(2,1)S(1)}, bf16[1,64,1024]{2,1,0:T(8,128)(2,1)}, u32[]{:S(2)}) copy-start(bf16[1,64,1024]{2,1,0:T(8,128)(2,1)} %get-tuple-element.85) | copy-start | bytes 393220
  371.1 5.0 %copy-start.4 = (bf16[128,2048]{1,0:T(8,128)(2,1)S(1)}, bf16[128,2048]{1,0:T(8,128)(2,1)}, u32[]{:S(2)}) copy-start(bf16[128,2048]{1,0:T(8,128)(2,1)} %get-tuple-element.80) | copy-start | bytes 1572868
  373.6 3.3 copy-start.3

commit v4 on v3

--- a/solution.py
+++ b/solution.py
@@ -1207,6 +1207,10 @@
             out_copy(k).wait_recv()
 
         def attend(n, carry):
+            @pl.when(n == blocks - 1)
+            def _():
+                gather.step(2)
+
             r = block_of(n)
             visible = (key_ref[...] >= low_ref[r, 0:1]) & (key_ref[...] <= code_ref[r, 0:1])
             for h in range(q_here):
@@ -1226,9 +1230,7 @@
             part_store(n).start()
             return carry
 
-        lax.fori_loop(0, blocks - 1, attend, 0)
-        gather.step(2)
-        lax.fori_loop(blocks - 1, blocks, attend, 0)
+        lax.fori_loop(0, blocks, attend, 0)
         for s in range(3, chips):
             gather.step(s)
         gather.finish()
@@ -1626,6 +1628,10 @@
             hop.start()
 
         def through_gate(n, carry):
+            @pl.when(n == blocks // 2)
+            def _():
+                mlp.step(0)
+
             r = block_of(n)
             dy_load(n).wait()
             dgated = mm_nt(dy_s[r, :], o_rows[...])
@@ -1646,9 +1652,7 @@
             delta_s[r, :] = deltas
             return carry
 
-        lax.fori_loop(0, blocks // 2, through_gate, 0)
-        mlp.step(0)
-        lax.fori_loop(blocks // 2, blocks, through_gate, 0)
+        lax.fori_loop(0, blocks, through_gate, 0)
 
         def out_grad(n, carry):
             c = block_of(n)
@@ -1670,6 +1674,10 @@
             return unit_back(grad * gain, unit, factor).astype(BF16), grad * unit
 
         def attend(n, carry):
+            @pl.when(n == blocks // 2)
+            def _():
+                mlp.step(1)
+
             r = block_of(n)
             for head in range(q_here):
                 at = slice(head * HEAD_DIM, (head + 1) * HEAD_DIM)
@@ -1685,9 +1693,7 @@
                 dgq_s[...] += jnp.sum(part.reshape(ROWS // 8, 8, HEAD_DIM), axis=0)
             return carry
 
-        lax.fori_loop(0, blocks // 2, attend, 0)
-        mlp.step(1)
-        lax.fori_loop(blocks // 2, blocks, attend, 0)
+        lax.fori_loop(0, blocks, attend, 0)
         every = pl.ds(0, pack)
         k_cols = slice(q_cols, q_cols + HEAD_DIM)
         dlin, part = into_lin(
@@ -2100,13 +2106,18 @@
         for hop in hops:
             hop.wait()
         blocks = units // ROWS
-        unit_block(0, 0)
-        for s in range(2, chips):
+
+        def first_units(f):
+            unit_block(0, f)
+            for s in range(2, chips):
+
+                @pl.when(f == s - 2)
+                def _(s=s):
+                    gather1[1].step(s)
+
+        loop(blocks, first_units)
+        for s in range(blocks + 2, chips):
             gather1[1].step(s)
-            if s == 2:
-                unit_block(0, 1)
-        for f in range(2, blocks):
-            unit_block(0, f)
         back(0)
         second[0].start()
         gather1[1].finish()

time: 381 us -> 368 us (0.966)
  Pallas kernels: 361 us -> 351 us
    pallas_call x1, Pallas kernels: 107 us -> 102 us  [attention_end(): pl.pallas_call(kernel, out_shape=(spec_of((count, width), BF16), spec_of(...]
    pallas_call x1, Pallas kernels: 166 us -> 161 us  [feed_forward(): pl.pallas_call(kernel, out_shape=(jax.ShapeDtypeStruct((count, width), F3...]
where the time goes in v4:
time: 368 us
  Pallas kernels  351 us (95%)
  other arithmetic  10.8 us (3%)
  local copies, waits for them, and re-layouts  5.32 us (1%)
    pallas_call x1, Pallas kernels, feed_forward(): pl.pallas_call(kernel, out_shape=(jax.ShapeDtypeStruct((count, width), F3...  161 us
    pallas_call x1, Pallas kernels, attention_end(): pl.pallas_call(kernel, out_shape=(spec_of((count, width), BF16), spec_of(...  102 us
    pallas_call x1, Pallas kernels, attention_forward(): pl.pallas_call(kernel, out_shape=(spec_of((pack, width), BF16), spec_of((...  88.2 us

profile of v4, /device:TPU:16, one launch (start us, length us, event | category | flops | bytes accessed | tf_op | source)
XLA Modules:
  0.0 368.2 jit_solution(1649030888532930356)
XLA Ops:
  0.7 0.1 pad.9.clone
  0.8 0.8 pad_maximum_fusion
  1.6 0.1 tile.9
  1.7 0.7 tile.10
  2.3 0.1 stack_tile.6
  2.4 0.7 tile.11
  3.1 0.1 stack_tile.7
  3.2 0.6 pad_add_fusion.refs_3_
  3.8 88.2 %attention_forward.1 = (bf16[1024,2048]{1,0:T(8,128)(2,1)}, bf16[1024,2048]{1,0:T(8,128)(2,1)}, bf16[2,1024,1024]{2,1,0:T(8,128)(2,1)}, bf16[4,2,64,2048]{3,2,1,...) custom-call(bf16[128,2048]{1,0:T(8,128)(2,1)} %bitcast.36, ...), custom_call_target="tpu_custom_call" | custom-call | bytes 83886080 | tf_op jit(solution)/shard_map/attention_forward/pallas_call | solution.py:1257
  92.0 161.5 %feed_forward.1 = (f32[128,2048]{1,0:T(8,128)}, f32[128,2048]{1,0:T(8,128)}, f32[8,2048]{1,0:T(8,128)}, bf16[4,2,128,2048]{3,2,1,0:T(8,128)(2,1)}, bf16[4,2,128,...) custom-call(bf16[4,2,128,2048]{3,2,1,0:T(8,128)(2,1)} %bitcast.39, ...), custom_call_target="tpu_custom_call" | custom-call | bytes 167772160 | tf_op jit(solution)/shard_map/feed_forward/pallas_call | solution.py:2167
  253.5 0.0 copy-start.2
  253.5 101.5 %attention_end.1 = (bf16[128,2048]{1,0:T(8,128)(2,1)}, f32[128,2048]{1,0:T(8,128)}, f32[24,128]{1,0:T(8,128)}, bf16[64,2048]{1,0:T(8,128)(2,1)}, bf16[1,64,1024]...) custom-call(bf16[1024,2048]{1,0:T(8,128)(2,1)} %bitcast.40, ...), custom_call_target="tpu_custom_call" | custom-call | bytes 167772160 | tf_op jit(solution)/shard_map/attention_end/pallas_call | solution.py:1823
  355.1 0.0 copy-done.2
  355.1 0.0 copy-start
  355.1 2.7 convert_add_fusion.2
  357.8 0.0 copy-start.6
  357.8 0.0 copy-start.5
  357.8 3.7 convert_add_fusion
  361.5 0.1 constant_dynamic-slice_fusion
  361.6 0.5 slice_bitcast_fusion.3
  362.1 0.1 reshape.74
  362.2 0.1 select_reduce_fusion
  362.3 0.5 slice_bitcast_fusion.1
  362.8 0.5 fusion.2
  363.3 0.6 slice_bitcast_fusion
  363.9 0.8 convert_element_type.53
  364.7 0.0 copy-done.5
  364.7 0.8 convert_element_type.54
  365.6 0.8 bitcast_convert_fusion
  366.4 0.0 copy-done.4
  366.4 0.8 copy.33
  367.2 1.0 copy.34
  (22 shorter events, 0.1 us)
Async XLA Ops:
  253.5 101.6 %copy-start.2 = (bf16[2,192,2048]{2,1,0:T(8,128)(2,1)S(1)}, bf16[2,192,2048]{2,1,0:T(8,128)(2,1)}, u32[]{:S(2)}) copy-start(bf16[2,192,2048]{2,1,0:T(8,128)(2,1)} %get-tuple-element.62.refs_0_) | copy-start | bytes 4718596
  355.1 2.7 copy-start
  355.1 2.7 copy-start.1
  357.8 3.7 %copy-start.9 = (f32[24,128]{1,0:T(8,128)S(1)}, f32[24,128]{1,0:T(8,128)}, u32[]{:S(2)}) copy-start(f32[24,128]{1,0:T(8,128)} %get-tuple-element.82) | copy-start | bytes 36868
  357.8 5.0 %copy-start.10 = (bf16[64]{0:T(256)(128)(2,1)S(1)}, bf16[64]{0:T(256)(128)(2,1)}, u32[]{:S(2)}) copy-start(bf16[64]{0:T(256)(128)(2,1)} %param.21) | copy-start | bytes 388
  357.8 6.1 %copy-start.6 = (bf16[64,2048]{1,0:T(8,128)(2,1)S(1)}, bf16[64,2048]{1,0:T(8,128)(2,1)}, u32[]{:S(2)}) copy-start(bf16[64,2048]{1,0:T(8,128)(2,1)} %get-tuple-element.83) | copy-start | bytes 786436
  357.8 7.0 %copy-start.5 = (bf16[64,2048]{1,0:T(8,128)(2,1)S(1)}, bf16[64,2048]{1,0:T(8,128)(2,1)}, u32[]{:S(2)}) copy-start(bf16[64,2048]{1,0:T(8,128)(2,1)} %get-tuple-element.86) | copy-start | bytes 786436
  361.5 4.1 %copy-start.7 = (bf16[1,64,1024]{2,1,0:T(8,128)(2,1)S(1)}, bf16[1,64,1024]{2,1,0:T(8,128)(2,1)}, u32[]{:S(2)}) copy-start(bf16[1,64,1024]{2,1,0:T(8,128)(2,1)} %get-tuple-element.84) | copy-start | bytes 393220
  361.5 4.1 %copy-start.8 = (bf16[1,64,1024]{2,1,0:T(8,128)(2,1)S(1)}, bf16[1,64,1024]{2,1,0:T(8,128)(2,1)}, u32[]{:S(2)}) copy-start(bf16[1,64,1024]{2,1,0:T(8,128)(2,1)} %get-tuple-element.85) | copy-start | bytes 393220
  361.5 5.0 %copy-start.4 = (bf16[128,2048]{1,0:T(8,128)(2,1)S(1)}, bf16[128,2048]{1,0:T(8,128)(2,1)}, u32[]{:S(2)}) copy-start(bf16[128,2048]{1,0:T(8,128)(2,1)} %get-tuple-element.80) | copy-start | bytes 1572868
  363.9 3.3 copy-start.3

commit v5 on v4

--- a/solution.py
+++ b/solution.py
@@ -1121,15 +1121,15 @@
         for one in locals_:
             one.wait()
         for k in range(1, n_blk):
-            pack_copy(k).wait_recv()
-        for k in range(1, n_head):
-            g_copy(k).start()
-        for k in range(1, n_blk):
             for copy in block_copies(k):
                 copy.wait_recv()
         tokens.start()
         for k in range(1, n_head):
             w_copy(k).start()
+        for k in range(1, n_blk):
+            pack_copy(k).wait_recv()
+        for k in range(1, n_head):
+            g_copy(k).start()
 
         @pl.when(stays)
         def _():

time: 368 us -> 369 us (level)
  no operation moved by 1% of the time
where the time goes in v5:
time: 369 us; the launch traced here: 368 us
  Pallas kernels  352 us (95%)
  other arithmetic  10.8 us (3%)
  local copies, waits for them, and re-layouts  5.32 us (1%)
    pallas_call x1, Pallas kernels, feed_forward(): pl.pallas_call(kernel, out_shape=(jax.ShapeDtypeStruct((count, width), F3...  162 us
    pallas_call x1, Pallas kernels, attention_end(): pl.pallas_call(kernel, out_shape=(spec_of((count, width), BF16), spec_of(...  101 us
    pallas_call x1, Pallas kernels, attention_forward(): pl.pallas_call(kernel, out_shape=(spec_of((pack, width), BF16), spec_of((...  88.8 us

profile of v5, /device:TPU:16, one launch (start us, length us, event | category | flops | bytes accessed | tf_op | source)
XLA Modules:
  0.0 368.5 jit_solution(16261226604344785564)
XLA Ops:
  0.7 0.1 pad.9.clone
  0.8 0.8 pad_maximum_fusion
  1.6 0.1 tile.9
  1.7 0.7 tile.10
  2.3 0.1 stack_tile.6
  2.4 0.7 tile.11
  3.1 0.1 stack_tile.7
  3.2 0.6 pad_add_fusion.refs_3_
  3.8 88.8 %attention_forward.1 = (bf16[1024,2048]{1,0:T(8,128)(2,1)}, bf16[1024,2048]{1,0:T(8,128)(2,1)}, bf16[2,1024,1024]{2,1,0:T(8,128)(2,1)}, bf16[4,2,64,2048]{3,2,1,...) custom-call(bf16[128,2048]{1,0:T(8,128)(2,1)} %bitcast.36, ...), custom_call_target="tpu_custom_call" | custom-call | bytes 83886080 | tf_op jit(solution)/shard_map/attention_forward/pallas_call | solution.py:1257
  92.6 161.5 %feed_forward.1 = (f32[128,2048]{1,0:T(8,128)}, f32[128,2048]{1,0:T(8,128)}, f32[8,2048]{1,0:T(8,128)}, bf16[4,2,128,2048]{3,2,1,0:T(8,128)(2,1)}, bf16[4,2,128,...) custom-call(bf16[4,2,128,2048]{3,2,1,0:T(8,128)(2,1)} %bitcast.39, ...), custom_call_target="tpu_custom_call" | custom-call | bytes 167772160 | tf_op jit(solution)/shard_map/feed_forward/pallas_call | solution.py:2167
  254.2 0.0 copy-start.2
  254.2 101.2 %attention_end.1 = (bf16[128,2048]{1,0:T(8,128)(2,1)}, f32[128,2048]{1,0:T(8,128)}, f32[24,128]{1,0:T(8,128)}, bf16[64,2048]{1,0:T(8,128)(2,1)}, bf16[1,64,1024]...) custom-call(bf16[1024,2048]{1,0:T(8,128)(2,1)} %bitcast.40, ...), custom_call_target="tpu_custom_call" | custom-call | bytes 167772160 | tf_op jit(solution)/shard_map/attention_end/pallas_call | solution.py:1823
  355.4 0.0 copy-done.2
  355.4 0.0 copy-start
  355.4 0.0 copy-start.1
  355.4 2.7 convert_add_fusion.2
  358.1 0.0 copy-done.1
  358.1 3.7 convert_add_fusion
  361.8 0.1 constant_dynamic-slice_fusion
  361.8 0.5 slice_bitcast_fusion.3
  362.4 0.1 reshape.74
  362.4 0.1 select_reduce_fusion
  362.6 0.5 slice_bitcast_fusion.1
  363.1 0.5 fusion.2
  363.6 0.6 slice_bitcast_fusion
  364.2 0.8 convert_element_type.53
  365.0 0.8 convert_element_type.54
  365.9 0.0 copy-done.8
  365.9 0.8 bitcast_convert_fusion
  366.7 0.8 copy.33
  367.5 0.0 copy-done.3
  367.5 1.0 copy.34
  (22 shorter events, 0.1 us)
Async XLA Ops:
  254.2 101.2 %copy-start.2 = (bf16[2,192,2048]{2,1,0:T(8,128)(2,1)S(1)}, bf16[2,192,2048]{2,1,0:T(8,128)(2,1)}, u32[]{:S(2)}) copy-start(bf16[2,192,2048]{2,1,0:T(8,128)(2,1)} %get-tuple-element.62.refs_0_) | copy-start | bytes 4718596
  355.4 2.7 copy-start
  355.4 2.7 copy-start.1
  358.1 3.7 %copy-start.9 = (f32[24,128]{1,0:T(8,128)S(1)}, f32[24,128]{1,0:T(8,128)}, u32[]{:S(2)}) copy-start(f32[24,128]{1,0:T(8,128)} %get-tuple-element.82) | copy-start | bytes 36868
  358.1 5.0 %copy-start.10 = (bf16[64]{0:T(256)(128)(2,1)S(1)}, bf16[64]{0:T(256)(128)(2,1)}, u32[]{:S(2)}) copy-start(bf16[64]{0:T(256)(128)(2,1)} %param.21) | copy-start | bytes 388
  358.1 6.1 %copy-start.6 = (bf16[64,2048]{1,0:T(8,128)(2,1)S(1)}, bf16[64,2048]{1,0:T(8,128)(2,1)}, u32[]{:S(2)}) copy-start(bf16[64,2048]{1,0:T(8,128)(2,1)} %get-tuple-element.83) | copy-start | bytes 786436
  358.1 7.0 %copy-start.5 = (bf16[64,2048]{1,0:T(8,128)(2,1)S(1)}, bf16[64,2048]{1,0:T(8,128)(2,1)}, u32[]{:S(2)}) copy-start(bf16[64,2048]{1,0:T(8,128)(2,1)} %get-tuple-element.86) | copy-start | bytes 786436
  361.7 4.1 %copy-start.7 = (bf16[1,64,1024]{2,1,0:T(8,128)(2,1)S(1)}, bf16[1,64,1024]{2,1,0:T(8,128)(2,1)}, u32[]{:S(2)}) copy-start(bf16[1,64,1024]{2,1,0:T(8,128)(2,1)} %get-tuple-element.84) | copy-start | bytes 393220
  361.7 4.1 %copy-start.8 = (bf16[1,64,1024]{2,1,0:T(8,128)(2,1)S(1)}, bf16[1,64,1024]{2,1,0:T(8,128)(2,1)}, u32[]{:S(2)}) copy-start(bf16[1,64,1024]{2,1,0:T(8,128)(2,1)} %get-tuple-element.85) | copy-start | bytes 393220
  361.7 5.0 %copy-start.4 = (bf16[128,2048]{1,0:T(8,128)(2,1)S(1)}, bf16[128,2048]{1,0:T(8,128)(2,1)}, u32[]{:S(2)}) copy-start(bf16[128,2048]{1,0:T(8,128)(2,1)} %get-tuple-element.80) | copy-start | bytes 1572868
  364.2 3.3 copy-start.3
